TPU v7x, 512 devices: a whole 4x8x8 slice. The times are simulated.
512 devices in a mesh: dp: 8 (over z), expert: 64 (over x, y, core).
Axes of the slice: x: 4, y: 8, z: 8, core: 2. Of those that a mesh axis runs over, the one named last changes fastest.
Arguments:
- hidden_in: bfloat16 [65536, 2048], P(('dp', 'expert')), may hold values from -16 to 16
- queries: bfloat16 [65536, 1024], P(('dp', 'expert')), may hold values from -6 to 6
- keys: bfloat16 [65536, 1024], P(('dp', 'expert')), may hold values from -6 to 6
- values: bfloat16 [65536, 1024], P(('dp', 'expert')), may hold values from -6 to 6
- segment_ids: int32 [65536], P(('dp', 'expert')), may hold values from 0 to 8191, as said below
- out_proj: bfloat16 [1024, 2048], P('dp', 'expert'), may hold values from -0.1875 to 0.1875
- norm_gain: float32 [2048], replicated, may hold values from 0.5 to 1.5
- w_gate: bfloat16 [64, 2048, 512], P('expert', 'dp'), may hold values from -0.125 to 0.125
- w_up: bfloat16 [64, 2048, 512], P('expert', 'dp'), may hold values from -0.125 to 0.125
- w_down: bfloat16 [64, 512, 2048], P('expert', None, 'dp'), may hold values from -0.25 to 0.25
- expert_ids: int32 [65536, 2], P(('dp', 'expert')), may hold values from 0 to 63, all different within a row; in each aligned block of 128 rows (0 to 127, 128 to 255, ...) at most 6 rows name the same one
- gate_fixed: int32 [65536, 2], P(('dp', 'expert')), may hold values from 1 to 4096
- grad_out: bfloat16 [65536, 2048], P(('dp', 'expert')), may hold values from -6 to 6
Outputs:
- layer_out: bfloat16 [65536, 2048], P(('dp', 'expert'))
- resid_grad: bfloat16 [65536, 2048], P(('dp', 'expert'))
- query_grad: bfloat16 [65536, 1024], P(('dp', 'expert'))
- key_grad: bfloat16 [65536, 1024], P(('dp', 'expert'))
- value_grad: bfloat16 [65536, 1024], P(('dp', 'expert'))
Inputs may be any that keep to these rules, and one draw needn't show every extreme that they name: `expert_ids`: each row names two different experts; in each aligned block of 128 rows (the rows of one device) no expert is named by more than 6 rows, a bound that some block reaches. `segment_ids`: ids never fall; a token's id is the first position of its series divided by 8; every series starts at a position that is a multiple of 8 and lies inside one aligned block of 128 positions; each block begins a new series, and a series begins at position 65528.
All inputs are finite; a program needn't handle non-finite values.
Results may differ from a plain program's by a relative error of at most 0.017.
Values may be sent and summed in bfloat16 or wider, within the bound.
No kernel may reach another device: no remote copies, remote signals or barrier semaphores. Data moves between devices by JAX's collectives and lax.ppermute only.
A program may use at most 64 MiB of HBM per device.

v0:
```python
import jax
import jax.numpy as jnp
from jax import lax
from jax.sharding import PartitionSpec as P

HEAD_DIM = 128


epsilon = 1e-06
masked = -1e30


def contract_last(left, right):
    return lax.dot_general(
        left, right, (((1,), (1,)), ((), ())), preferred_element_type=jnp.float32
    )


def contract_first(left, right):
    return lax.dot_general(
        left, right, (((0,), (0,)), ((), ())), preferred_element_type=jnp.float32
    )


def local_probs(query, keys, segment):
    rows = query.shape[0]
    q_three = query.reshape(rows, -1, HEAD_DIM)
    k_three = keys.reshape(rows, -1, HEAD_DIM)
    scores = jnp.einsum(
        "qhd,khd->hqk", q_three, k_three, preferred_element_type=jnp.float32
    ) * HEAD_DIM ** (-0.5)
    places = jnp.arange(rows, dtype=jnp.int32)
    allowed = (segment[:, None] == segment[None, :]) & (places[:, None] >= places[None, :])
    scores = jnp.where(allowed[None], scores, masked)
    top = jnp.max(scores, axis=-1, keepdims=True)
    weights = jnp.exp(scores - top)
    return weights / jnp.sum(weights, axis=-1, keepdims=True)


def expert_forward(rows_in, w_in_gate, w_in_up, w_out):
    pre_gate = jnp.dot(rows_in, w_in_gate, preferred_element_type=jnp.float32)
    pre_up = jnp.dot(rows_in, w_in_up, preferred_element_type=jnp.float32)
    act = (jax.nn.silu(pre_gate) * pre_up).astype(jnp.bfloat16)
    out = jnp.dot(act, w_out, preferred_element_type=jnp.float32).astype(jnp.bfloat16)
    return (out, pre_gate, pre_up)


def expert_backward(pre_gate, pre_up, grads_in, w_in_gate, w_in_up, w_out):
    act_grad = contract_last(grads_in, w_out)
    sig = jax.nn.sigmoid(pre_gate)
    gate_grad = (act_grad * pre_up * sig * (1.0 + pre_gate * (1.0 - sig))).astype(jnp.bfloat16)
    up_grad = (act_grad * jax.nn.silu(pre_gate)).astype(jnp.bfloat16)
    return (contract_last(gate_grad, w_in_gate) + contract_last(up_grad, w_in_up)).astype(
        jnp.bfloat16
    )


def local(
    hidden_in,
    queries,
    keys,
    values,
    segment_ids,
    out_proj,
    norm_gain,
    w_gate,
    w_up,
    w_down,
    expert_ids,
    gate_fixed,
    grad_out,
):
    tok, width = hidden_in.shape
    experts = lax.axis_size("expert")
    capacity = 3 * tok // experts
    proj_cols = lax.all_gather(out_proj, "expert", axis=1, tiled=True)
    proj_full = lax.all_gather(proj_cols, "dp", axis=0, tiled=True)
    gate_full, up_full, down_full = (
        lax.all_gather(w_gate, "dp", axis=1, tiled=True),
        lax.all_gather(w_up, "dp", axis=1, tiled=True),
        lax.all_gather(w_down, "dp", axis=2, tiled=True),
    )
    w_in_gate = gate_full[0]
    w_in_up = up_full[0]
    w_out = down_full[0]
    probs = local_probs(queries, keys, segment_ids)
    probs_bf = probs.astype(jnp.bfloat16)
    v_three = values.reshape(tok, -1, HEAD_DIM)
    context = (
        jnp.einsum("hqk,khd->qhd", probs_bf, v_three, preferred_element_type=jnp.float32)
        .astype(jnp.bfloat16)
        .reshape(tok, -1)
    )
    resid = (
        hidden_in.astype(jnp.float32)
        + jnp.dot(context, proj_full, preferred_element_type=jnp.float32)
    ).astype(jnp.bfloat16)
    resid_f = resid.astype(jnp.float32)
    inv_rms = lax.rsqrt(jnp.mean(resid_f * resid_f, axis=-1, keepdims=True) + epsilon)
    normed = (resid_f * inv_rms * norm_gain).astype(jnp.bfloat16)
    gates = gate_fixed.astype(jnp.float32) / 4096.0
    flat_ids = expert_ids.reshape(-1)
    onehot = (flat_ids[:, None] == jnp.arange(experts, dtype=jnp.int32)[None, :]).astype(
        jnp.bfloat16
    )
    order = jnp.arange(2 * tok, dtype=jnp.int32)
    earlier = (order[:, None] > order[None, :]).astype(jnp.bfloat16)
    before = jnp.dot(earlier, onehot, preferred_element_type=jnp.float32)
    slot = jnp.sum(before * onehot.astype(jnp.float32), axis=1).astype(jnp.int32)
    dest = (flat_ids * capacity + slot).reshape(tok, 2)
    slot_index = jnp.arange(experts * capacity, dtype=jnp.int32)[:, None]
    pick_first = (slot_index == dest[None, :, 0]).astype(jnp.bfloat16)
    pick_second = (slot_index == dest[None, :, 1]).astype(jnp.bfloat16)
    pick_both = pick_first + pick_second
    grad_f = grad_out.astype(jnp.float32)
    routed_first = (gates[:, 0:1] * grad_f).astype(jnp.bfloat16)
    routed_second = (gates[:, 1:2] * grad_f).astype(jnp.bfloat16)
    send_rows = (
        jnp.dot(pick_both, normed, preferred_element_type=jnp.float32)
        .astype(jnp.bfloat16)
        .reshape(experts, capacity, width)
    )
    send_grads = (
        (
            jnp.dot(pick_first, routed_first, preferred_element_type=jnp.float32)
            + jnp.dot(pick_second, routed_second, preferred_element_type=jnp.float32)
        )
        .astype(jnp.bfloat16)
        .reshape(experts, capacity, width)
    )
    recv_rows = lax.all_to_all(send_rows, "expert", split_axis=0, concat_axis=0, tiled=True)
    shape = recv_rows.shape
    out, pre_gate, pre_up = expert_forward(recv_rows.reshape(-1, width), w_in_gate, w_in_up, w_out)
    back_out = lax.all_to_all(out.reshape(shape), "expert", split_axis=0, concat_axis=0, tiled=True)
    recv_grads = lax.all_to_all(send_grads, "expert", split_axis=0, concat_axis=0, tiled=True)
    in_grad = expert_backward(
        pre_gate, pre_up, recv_grads.reshape(-1, width), w_in_gate, w_in_up, w_out
    )
    back_grad = lax.all_to_all(
        in_grad.reshape(shape), "expert", split_axis=0, concat_axis=0, tiled=True
    )
    out_flat = back_out.reshape(experts * capacity, width)
    grad_flat = back_grad.reshape(experts * capacity, width)
    out_first = contract_first(pick_first, out_flat)
    out_second = contract_first(pick_second, out_flat)
    layer_out = (resid_f + gates[:, 0:1] * out_first + gates[:, 1:2] * out_second).astype(
        jnp.bfloat16
    )
    normed_grad = contract_first(pick_both, grad_flat)
    scaled = normed_grad * norm_gain
    unit = resid_f * inv_rms
    resid_grad = (
        grad_f + inv_rms * (scaled - unit * jnp.mean(scaled * unit, axis=-1, keepdims=True))
    ).astype(jnp.bfloat16)
    context_grad = contract_last(resid_grad, proj_full).astype(jnp.bfloat16)
    c_three = context_grad.reshape(tok, -1, HEAD_DIM)
    q_three = queries.reshape(tok, -1, HEAD_DIM)
    k_three = keys.reshape(tok, -1, HEAD_DIM)
    value_grad = jnp.einsum(
        "hqk,qhd->khd", probs_bf, c_three, preferred_element_type=jnp.float32
    ).astype(jnp.bfloat16)
    prob_grad = jnp.einsum("qhd,khd->hqk", c_three, v_three, preferred_element_type=jnp.float32)
    inner = jnp.sum(prob_grad * probs, axis=-1, keepdims=True)
    score_grad = (probs * (prob_grad - inner) * HEAD_DIM ** (-0.5)).astype(jnp.bfloat16)
    query_grad = jnp.einsum(
        "hqk,khd->qhd", score_grad, k_three, preferred_element_type=jnp.float32
    ).astype(jnp.bfloat16)
    key_grad = jnp.einsum(
        "hqk,qhd->khd", score_grad, q_three, preferred_element_type=jnp.float32
    ).astype(jnp.bfloat16)
    return (
        layer_out,
        resid_grad,
        query_grad.reshape(tok, -1),
        key_grad.reshape(tok, -1),
        value_grad.reshape(tok, -1),
    )


def solution(mesh):
    in_specs = (
        P(("dp", "expert"), None),
        P(("dp", "expert"), None),
        P(("dp", "expert"), None),
        P(("dp", "expert"), None),
        P(("dp", "expert")),
        P("dp", "expert"),
        P(),
        P("expert", "dp", None),
        P("expert", "dp", None),
        P("expert", None, "dp"),
        P(("dp", "expert"), None),
        P(("dp", "expert"), None),
        P(("dp", "expert"), None),
    )
    out_specs = (
        P(("dp", "expert"), None),
        P(("dp", "expert"), None),
        P(("dp", "expert"), None),
        P(("dp", "expert"), None),
        P(("dp", "expert"), None),
    )
    return jax.shard_map(local, mesh=mesh, in_specs=in_specs, out_specs=out_specs, check_vma=False)
```

profile of v0, /device:TPU:1, one launch (start us, length us, event | category | flops | bytes accessed | tf_op | source)
XLA Modules:
  0.0 408.7 jit_solution(15399155705640917057)
XLA Ops:
  7.2 59.3 %all_gather.15 = bf16[128,2048]{0,1:T(8,128)(2,1)} all-gather(bf16[128,32]{0,1:T(8,128)(2,1)} %param.18), channel_id=1, replica_groups=mesh['dp'=8,'expert'=64] {'expert'}, dimensions={1}, use_global_device_ids=true | all-gather | bytes 532480 | tf_op jit(solution)/shard_map/all_gather | solution.py:76
  66.5 0.0 all-gather.11.cloned.1.call-start
  66.6 0.7 all-gather.11.cloned.1.call-update
  67.3 0.0 all-gather.7.cloned.1.call-start
  67.3 0.7 all-gather.7.cloned.1.call-update
  68.0 0.8 copy.73
  68.8 0.1 eq.66
  68.9 0.2 fusion.24
  69.2 0.1 convert_element_type.114
  69.3 0.1 copy.74
  69.4 0.7 multiply_add_fusion
  70.1 0.7 convert_multiply_fusion.2
  70.8 0.6 fusion.34
  71.4 0.7 add_convert_fusion.1
  72.1 1.6 reshape.131
  73.7 5.3 %all-to-all-start.2 = ((bf16[64,6,2048]{2,1,0:T(8,128)(2,1)}), bf16[64,6,2048]{2,1,0:T(8,128)(2,1)S(1)}, u32[]{:S(2)}, u32[]{:S(2)}) async-start(bf16[64,6,2048]{2,1,0:T(8,128)(2,1)} %reshape.131), calls=%async_computation.2 | async-start | bytes 4194304 | tf_op jit(solution)/shard_map/all_to_all | solution.py:135
  79.0 0.0 all-gather.9.cloned.1.call-start
  79.1 0.5 all-gather.9.cloned.1.call-update
  79.6 0.2 copy.90
  79.8 0.2 copy.91
  80.0 0.1 fusion.66
  80.1 0.3 fusion.22
  80.4 1.0 fusion.75
  81.3 1.0 convolution_convert_fusion.3
  82.4 45.0 %all-gather.5.cloned.1.call-done = bf16[1024,2048]{0,1:T(8,128)(2,1)} async-done(((bf16[128,2048]{0,1:T(8,128)(2,1)}), bf16[1024,2048]{0,1:T(8,128)(2,1)}) %all-gather.5.cloned.1.call-update) | async-done | bytes 4194320 | tf_op jit(solution)/shard_map/all_gather | solution.py:77
  127.4 4.0 multiply_reduce_fusion.1
  131.4 1.8 convolution_convert_fusion.1
  133.2 3.7 reshape.127
  136.9 14.3 %all-to-all-start = ((bf16[64,6,2048]{2,1,0:T(8,128)(2,1)}), bf16[64,6,2048]{2,1,0:T(8,128)(2,1)}, u32[]{:S(2)}, u32[]{:S(2)}) async-start(bf16[64,6,2048]{2,1,0:T(8,128)(2,1)} %reshape.127), calls=%async_computation | async-start | bytes 4194304 | tf_op jit(solution)/shard_map/all_to_all | solution.py:131
  151.2 1.5 reshape.132
  152.6 25.7 %all-gather.11.cloned.1.call-done = bf16[1,512,2048]{2,1,0:T(8,128)(2,1)} async-done(((bf16[1,512,256]{2,1,0:T(8,128)(2,1)}), bf16[1,512,2048]{2,1,0:T(8,128)(2,1)}) %all-gather.11.cloned.1.call-update) | async-done | bytes 2097168 | tf_op jit(solution)/shard_map/all_gather | solution.py:81
  178.3 4.0 fusion.7
  182.3 19.9 %all-to-all-done = bf16[64,6,2048]{2,1,0:T(8,128)(2,1)} async-done(((bf16[64,6,2048]{2,1,0:T(8,128)(2,1)}), bf16[64,6,2048]{2,1,0:T(8,128)(2,1)}, u32[]{:S(2)}, u32[]{:S(2)}) %all-to-all-start) | async-done | bytes 1572896 | tf_op jit(solution)/shard_map/all_to_all | solution.py:131
  202.3 2.6 reshape.128
  204.9 18.0 %all-gather.7.cloned.1.call-done = bf16[1,2048,512]{2,1,0:T(8,128)(2,1)} async-done(((bf16[1,256,512]{2,1,0:T(8,128)(2,1)}), bf16[1,2048,512]{2,1,0:T(8,128)(2,1)}) %all-gather.7.cloned.1.call-update) | async-done | bytes 2097168 | tf_op jit(solution)/shard_map/all_gather | solution.py:79
  222.9 3.5 fusion.15
  226.3 40.8 %all-gather.9.cloned.1.call-done = bf16[1,2048,512]{2,1,0:T(8,128)(2,1)} async-done(((bf16[1,256,512]{2,1,0:T(8,128)(2,1)}), bf16[1,2048,512]{2,1,0:T(8,128)(2,1)}) %all-gather.9.cloned.1.call-update) | async-done | bytes 2097168 | tf_op jit(solution)/shard_map/all_gather | solution.py:80
  267.1 2.7 fusion.11
  269.8 0.9 copy-done.17
  270.7 1.2 fusion.13
  271.9 0.4 copy-done.5
  272.3 1.0 add_convert_fusion
  273.3 1.6 reshape.133
  275.0 14.5 %all-to-all-start.3 = ((bf16[64,6,2048]{2,1,0:T(8,128)(2,1)}), bf16[64,6,2048]{2,1,0:T(8,128)(2,1)S(1)}, u32[]{:S(2)}, u32[]{:S(2)}) async-start(bf16[64,6,2048]{2,1,0:T(8,128)(2,1)} %reshape.133), calls=%async_computation.3 | async-start | bytes 4194304 | tf_op jit(solution)/shard_map/all_to_all | solution.py:139
  289.4 4.3 %convolution_convert_fusion = bf16[384,2048]{1,0:T(8,128)(2,1)} fusion(bf16[1,512,2048]{2,1,0:T(8,128)(2,1)} %all-gather.11.cloned.1.call-done, f32[384,512]{1,0:T(8,128)} %copy-done.17, f32[384,512]{1,0:T(8,128)} %fusion.15), kind=kOutput, calls=%fused_computation.4 | convolution fusion | flops 807272448 | bytes 5242880 | tf_op jit(solution)/shard_map/dot_general | solution.py:44
  293.7 3.7 reshape.129
  297.4 43.2 %all-to-all-done.3 = bf16[64,6,2048]{2,1,0:T(8,128)(2,1)S(1)} async-done(((bf16[64,6,2048]{2,1,0:T(8,128)(2,1)}), bf16[64,6,2048]{2,1,0:T(8,128)(2,1)S(1)}, u32[]{:S(2)}, u32[]{:S(2)}) %all-to-all-start.3) | async-done | bytes 1572896 | tf_op jit(solution)/shard_map/all_to_all | solution.py:139
  340.6 6.0 %all-to-all-start.1 = ((bf16[64,6,2048]{2,1,0:T(8,128)(2,1)}), bf16[64,6,2048]{2,1,0:T(8,128)(2,1)}, u32[]{:S(2)}, u32[]{:S(2)}) async-start(bf16[64,6,2048]{2,1,0:T(8,128)(2,1)} %reshape.129), calls=%async_computation.1 | async-start | bytes 4194304 | tf_op jit(solution)/shard_map/all_to_all | solution.py:134
  346.7 1.5 reshape.134
  348.2 2.1 multiply_reduce_fusion
  350.3 1.4 fusion.27
  351.7 0.7 convolution_convert_fusion.6
  352.5 0.2 copy.92
  352.7 1.6 convolution_convert_fusion.4
  354.2 0.9 copy.85
  355.1 0.2 fusion.42
  355.3 1.6 convolution_convert_fusion.5
  356.9 0.9 copy.84
  357.7 1.5 convolution_convert_fusion.2
  359.3 0.9 copy.83
  360.1 37.7 %all-to-all-done.1 = bf16[64,6,2048]{2,1,0:T(8,128)(2,1)} async-done(((bf16[64,6,2048]{2,1,0:T(8,128)(2,1)}), bf16[64,6,2048]{2,1,0:T(8,128)(2,1)}, u32[]{:S(2)}, u32[]{:S(2)}) %all-to-all-start.1) | async-done | bytes 1572896 | tf_op jit(solution)/shard_map/all_to_all | solution.py:134
  397.8 2.6 reshape.130
  400.4 0.5 fusion.3
  400.9 1.3 fusion.4
  (42 shorter events, 0.2 us)
Async XLA Ops:
  7.2 74.2 %copy-start = (bf16[128,1024]{1,0:T(8,128)(2,1)S(1)}, bf16[128,1024]{1,0:T(8,128)(2,1)}, u32[]{:S(2)}) copy-start(bf16[128,1024]{1,0:T(8,128)(2,1)} %param.16) | copy-start | bytes 786436
  7.2 63.6 %copy-start.2 = (bf16[128,2048]{1,0:T(8,128)(2,1)S(1)}, bf16[128,2048]{1,0:T(8,128)(2,1)}, u32[]{:S(2)}) copy-start(bf16[128,2048]{1,0:T(8,128)(2,1)} %param.25) | copy-start | bytes 1572868
  7.2 120.2 %all-gather.5.cloned.1.call-start = ((), (), s32[]{:S(2)}) async-start(), calls=%async_computation.4 | async-start | bytes 4718592 | tf_op jit(solution)/shard_map/all_gather | solution.py:77
  66.5 111.8 %all-gather.11.cloned.1.call-start = ((), (), s32[]{:S(2)}) async-start(), calls=%async_computation.7 | async-start | bytes 2359296 | tf_op jit(solution)/shard_map/all_gather | solution.py:81
  67.3 155.6 %all-gather.7.cloned.1.call-start = ((), (), s32[]{:S(2)}) async-start(), calls=%async_computation.5 | async-start | bytes 2359296 | tf_op jit(solution)/shard_map/all_gather | solution.py:79
  73.7 5.9 %copy-start.12 = (bf16[128,1024]{1,0:T(8,128)(2,1)S(1)}, bf16[128,1024]{1,0:T(8,128)(2,1)}, u32[]{:S(2)}) copy-start(bf16[128,1024]{1,0:T(8,128)(2,1)} %param.14) | copy-start | bytes 786436
  73.7 6.0 %copy-start.13 = (bf16[128,1024]{1,0:T(8,128)(2,1)S(1)}, bf16[128,1024]{1,0:T(8,128)(2,1)}, u32[]{:S(2)}) copy-start(bf16[128,1024]{1,0:T(8,128)(2,1)} %param.15) | copy-start | bytes 786436
  73.7 6.2 %copy-start.15 = (s32[128]{0:T(128)S(1)}, s32[128]{0:T(128)}, u32[]{:S(2)}) copy-start(s32[128]{0:T(128)} %param.17) | copy-start | bytes 1540
  73.7 63.1 %all-to-all-start.2 = ((bf16[64,6,2048]{2,1,0:T(8,128)(2,1)}), bf16[64,6,2048]{2,1,0:T(8,128)(2,1)S(1)}, u32[]{:S(2)}, u32[]{:S(2)}) async-start(bf16[64,6,2048]{2,1,0:T(8,128)(2,1)} %reshape.131), calls=%async_computation.2 | async-start | bytes 4194304 | tf_op jit(solution)/shard_map/all_to_all | solution.py:135
  79.0 188.1 %all-gather.9.cloned.1.call-start = ((), (), s32[]{:S(2)}) async-start(), calls=%async_computation.6 | async-start | bytes 2359296 | tf_op jit(solution)/shard_map/all_gather | solution.py:80
  79.8 2.6 copy-start.8
  80.0 2.4 copy-start.6
  80.4 47.0 %copy-start.3 = (f32[8,128,128]{1,2,0:T(8,128)}, f32[8,128,128]{1,2,0:T(8,128)S(1)}, u32[]{:S(2)}) copy-start(f32[8,128,128]{1,2,0:T(8,128)S(1)} %fusion.22) | copy-start | bytes 1572868
  127.4 4.0 copy-start.14
  136.9 65.4 %all-to-all-start = ((bf16[64,6,2048]{2,1,0:T(8,128)(2,1)}), bf16[64,6,2048]{2,1,0:T(8,128)(2,1)}, u32[]{:S(2)}, u32[]{:S(2)}) async-start(bf16[64,6,2048]{2,1,0:T(8,128)(2,1)} %reshape.127), calls=%async_computation | async-start | bytes 4194304 | tf_op jit(solution)/shard_map/all_to_all | solution.py:131
  267.1 3.6 copy-start.10
  267.1 3.6 copy-start.11
  267.1 3.6 copy-start.16
  269.8 0.9 copy-start.17
  270.7 1.6 copy-start.5
  275.0 65.7 %all-to-all-start.3 = ((bf16[64,6,2048]{2,1,0:T(8,128)(2,1)}), bf16[64,6,2048]{2,1,0:T(8,128)(2,1)S(1)}, u32[]{:S(2)}, u32[]{:S(2)}) async-start(bf16[64,6,2048]{2,1,0:T(8,128)(2,1)} %reshape.133), calls=%async_computation.3 | async-start | bytes 4194304 | tf_op jit(solution)/shard_map/all_to_all | solution.py:139
  340.6 57.1 %all-to-all-start.1 = ((bf16[64,6,2048]{2,1,0:T(8,128)(2,1)}), bf16[64,6,2048]{2,1,0:T(8,128)(2,1)}, u32[]{:S(2)}, u32[]{:S(2)}) async-start(bf16[64,6,2048]{2,1,0:T(8,128)(2,1)} %reshape.129), calls=%async_computation.1 | async-start | bytes 4194304 | tf_op jit(solution)/shard_map/all_to_all | solution.py:134
  348.2 3.5 copy-start.1
  351.7 0.8 copy-start.4
  352.6 2.7 copy-start.9
  355.1 2.6 copy-start.7
Sparse Core Ops, SparseCore 0:
  66.6 60.6 all-gather.4
  129.4 48.9 all-gather.10
  180.4 42.3 all-gather.6
  224.8 42.2 all-gather.8
where the time goes:
time: 410 us; the launch traced here: 409 us
  waiting for transfers between devices  232 us (57%)
  blocking collectives  59.3 us (14%)
  starting transfers between devices  40.2 us (10%)
  matrix products  34.8 us (8%)
  local copies, waits for them, and re-layouts  24.3 us (6%)
  between operations  14.1 us (3%)
    all_gather x1, blocking collectives, local(): proj_cols = lax.all_gather(out_proj, 'expert', axis=1, tiled=True)  59.3 us
    all_gather x1, waiting for transfers between devices, local(): proj_full = lax.all_gather(proj_cols, 'dp', axis=0, tiled=True)  45 us
    all_to_all x1, waiting for transfers between devices, local(): lax.all_to_all(in_grad.reshape(shape), 'expert', split_axis=0, concat_axi...  43.2 us
    all_gather x1, waiting for transfers between devices, local(): lax.all_gather(w_up, 'dp', axis=1, tiled=True)  40.8 us
    all_to_all x1, waiting for transfers between devices, local(): lax.all_to_all(out.reshape(shape), 'expert', split_axis=0, concat_axis=0,...  37.7 us
    all_gather x1, waiting for transfers between devices, local(): lax.all_gather(w_down, 'dp', axis=2, tiled=True)  25.7 us
    all_to_all x1, waiting for transfers between devices, local(): lax.all_to_all(send_rows, 'expert', split_axis=0, concat_axis=0, tiled=True)  19.9 us
    all_gather x1, waiting for transfers between devices, local(): lax.all_gather(w_gate, 'dp', axis=1, tiled=True)  18 us
  transfers between devices with their start and end apart: 8, of which 7 were waited for; matrix products, arithmetic and copies ran while one was open for 12% of the time, Pallas kernels for 0%

commit v1 on v0

v1 whole, which is shorter than its diff:
```python
import jax
import jax.numpy as jnp
from jax import lax
from jax.sharding import Mesh, PartitionSpec as P

HEAD_DIM = 128
EXPERT = ("x", "y", "core")
SPLIT = (4, 8, 2)


epsilon = 1e-06
masked = -1e30


def contract_last(left, right):
    return lax.dot_general(
        left, right, (((1,), (1,)), ((), ())), preferred_element_type=jnp.float32
    )


def contract_first(left, right):
    return lax.dot_general(
        left, right, (((0,), (0,)), ((), ())), preferred_element_type=jnp.float32
    )


def local_probs(query, keys, segment):
    rows = query.shape[0]
    q_three = query.reshape(rows, -1, HEAD_DIM)
    k_three = keys.reshape(rows, -1, HEAD_DIM)
    scores = jnp.einsum(
        "qhd,khd->hqk", q_three, k_three, preferred_element_type=jnp.float32
    ) * HEAD_DIM ** (-0.5)
    places = jnp.arange(rows, dtype=jnp.int32)
    allowed = (segment[:, None] == segment[None, :]) & (places[:, None] >= places[None, :])
    scores = jnp.where(allowed[None], scores, masked)
    top = jnp.max(scores, axis=-1, keepdims=True)
    weights = jnp.exp(scores - top)
    return weights / jnp.sum(weights, axis=-1, keepdims=True)


def spread(rows, axes):
    return lax.all_to_all(rows, axes, split_axis=0, concat_axis=0, tiled=True)


def gather_small(block, axes, count):
    return spread(jnp.broadcast_to(block[None], (count,) + block.shape), axes)


def gather_near(out_proj):
    heads, ys = lax.axis_size("dp"), lax.axis_size("y")
    near = gather_small(out_proj.T, ("dp", "y"), heads * ys)
    return near.reshape((heads, ys) + near.shape[1:])


def gather_proj(near):
    heads, ys, cols, depth = near.shape
    xs, place = lax.axis_size("x"), lax.axis_index("x")
    shifted = [near] + [
        lax.ppermute(near, "x", [(i, (i + k) % xs) for i in range(xs)]) for k in range(1, xs)
    ]
    first = lax.axis_index("core") == 0
    others = [lax.ppermute(part, "core", [(0, 1), (1, 0)]) for part in shifted]
    both = jnp.stack(
        [
            jnp.stack([jnp.where(first, mine, other), jnp.where(first, other, mine)])
            for mine, other in zip(shifted, others)
        ]
    )
    turned = jnp.stack([both[(place - p) % xs] for p in range(xs)])
    return turned.transpose(0, 3, 1, 4, 2, 5).reshape(xs * ys * 2 * cols, heads * depth)


def gather_experts(w_gate, w_up, w_down):
    rows = w_gate.shape[1]
    hidden = w_gate.shape[2]
    down = jnp.concatenate([w_down[0, :rows], w_down[0, rows:]], axis=1)
    mine = jnp.stack([w_gate[0], w_up[0], down])
    full = lax.all_gather(mine, "dp", axis=0, tiled=False)
    slices = full.shape[0]
    gate = full[:, 0].reshape(slices * rows, hidden)
    up = full[:, 1].reshape(slices * rows, hidden)
    back = full[:, 2].reshape(slices, rows, 2, rows).transpose(2, 1, 0, 3)
    return gate, up, back.reshape(hidden, slices * rows)


def local(
    hidden_in,
    queries,
    keys,
    values,
    segment_ids,
    out_proj,
    norm_gain,
    w_gate,
    w_up,
    w_down,
    expert_ids,
    gate_fixed,
    grad_out,
):
    tok, width = hidden_in.shape
    experts = lax.axis_size(EXPERT)
    capacity = 3 * tok // experts
    lanes = (experts, capacity * width // HEAD_DIM, HEAD_DIM)
    gates = gate_fixed.astype(jnp.float32) / 4096.0
    flat_ids = expert_ids.reshape(-1)
    onehot = (flat_ids[:, None] == jnp.arange(experts, dtype=jnp.int32)[None, :]).astype(
        jnp.bfloat16
    )
    order = jnp.arange(2 * tok, dtype=jnp.int32)
    earlier = (order[:, None] > order[None, :]).astype(jnp.bfloat16)
    before = jnp.dot(earlier, onehot, preferred_element_type=jnp.float32)
    slot = jnp.sum(before * onehot.astype(jnp.float32), axis=1).astype(jnp.int32)
    dest = (flat_ids * capacity + slot).reshape(tok, 2)
    slot_index = jnp.arange(experts * capacity, dtype=jnp.int32)[:, None]
    pick_first = (slot_index == dest[None, :, 0]).astype(jnp.bfloat16)
    pick_second = (slot_index == dest[None, :, 1]).astype(jnp.bfloat16)
    pick_both = pick_first + pick_second
    grad_f = grad_out.astype(jnp.float32)
    routed_first = (gates[:, 0:1] * grad_f).astype(jnp.bfloat16)
    routed_second = (gates[:, 1:2] * grad_f).astype(jnp.bfloat16)
    send_grads = (
        jnp.dot(pick_first, routed_first, preferred_element_type=jnp.float32)
        + jnp.dot(pick_second, routed_second, preferred_element_type=jnp.float32)
    ).astype(jnp.bfloat16)
    near, send_grads = lax.optimization_barrier((gather_near(out_proj), send_grads))
    recv_grads = spread(send_grads.reshape(lanes), EXPERT).reshape(-1, width)
    w_in_gate, w_in_up, w_out = gather_experts(w_gate, w_up, w_down)
    proj_rows = gather_proj(near)
    probs = local_probs(queries, keys, segment_ids)
    probs_bf = probs.astype(jnp.bfloat16)
    v_three = values.reshape(tok, -1, HEAD_DIM)
    context = (
        jnp.einsum("hqk,khd->qhd", probs_bf, v_three, preferred_element_type=jnp.float32)
        .astype(jnp.bfloat16)
        .reshape(tok, -1)
    )
    resid = (hidden_in.astype(jnp.float32) + contract_last(context, proj_rows)).astype(
        jnp.bfloat16
    )
    resid_f = resid.astype(jnp.float32)
    inv_rms = lax.rsqrt(jnp.mean(resid_f * resid_f, axis=-1, keepdims=True) + epsilon)
    normed = (resid_f * inv_rms * norm_gain).astype(jnp.bfloat16)
    send_rows = jnp.dot(pick_both, normed, preferred_element_type=jnp.float32).astype(
        jnp.bfloat16
    )
    recv_rows = spread(send_rows.reshape(lanes), EXPERT).reshape(-1, width)
    act_grad = contract_last(recv_grads, w_out)
    pre_gate = jnp.dot(recv_rows, w_in_gate, preferred_element_type=jnp.float32)
    pre_up = jnp.dot(recv_rows, w_in_up, preferred_element_type=jnp.float32)
    sig = jax.nn.sigmoid(pre_gate)
    gate_grad = (act_grad * pre_up * sig * (1.0 + pre_gate * (1.0 - sig))).astype(jnp.bfloat16)
    up_grad = (act_grad * jax.nn.silu(pre_gate)).astype(jnp.bfloat16)
    in_grad = (contract_last(gate_grad, w_in_gate) + contract_last(up_grad, w_in_up)).astype(
        jnp.bfloat16
    )
    back_grad = spread(in_grad.reshape(lanes), EXPERT).reshape(-1, width)
    act = (jax.nn.silu(pre_gate) * pre_up).astype(jnp.bfloat16)
    out = jnp.dot(act, w_out, preferred_element_type=jnp.float32).astype(jnp.bfloat16)
    back_out = spread(out.reshape(lanes), EXPERT).reshape(-1, width)
    normed_grad = contract_first(pick_both, back_grad)
    scaled = normed_grad * norm_gain
    unit = resid_f * inv_rms
    resid_grad = (
        grad_f + inv_rms * (scaled - unit * jnp.mean(scaled * unit, axis=-1, keepdims=True))
    ).astype(jnp.bfloat16)
    context_grad = jnp.dot(resid_grad, proj_rows, preferred_element_type=jnp.float32).astype(
        jnp.bfloat16
    )
    c_three = context_grad.reshape(tok, -1, HEAD_DIM)
    q_three = queries.reshape(tok, -1, HEAD_DIM)
    k_three = keys.reshape(tok, -1, HEAD_DIM)
    value_grad = jnp.einsum(
        "hqk,qhd->khd", probs_bf, c_three, preferred_element_type=jnp.float32
    ).astype(jnp.bfloat16)
    prob_grad = jnp.einsum("qhd,khd->hqk", c_three, v_three, preferred_element_type=jnp.float32)
    inner = jnp.sum(prob_grad * probs, axis=-1, keepdims=True)
    score_grad = (probs * (prob_grad - inner) * HEAD_DIM ** (-0.5)).astype(jnp.bfloat16)
    query_grad = jnp.einsum(
        "hqk,khd->qhd", score_grad, k_three, preferred_element_type=jnp.float32
    ).astype(jnp.bfloat16)
    key_grad = jnp.einsum(
        "hqk,qhd->khd", score_grad, q_three, preferred_element_type=jnp.float32
    ).astype(jnp.bfloat16)
    out_first = contract_first(pick_first, back_out)
    out_second = contract_first(pick_second, back_out)
    layer_out = (resid_f + gates[:, 0:1] * out_first + gates[:, 1:2] * out_second).astype(
        jnp.bfloat16
    )
    return (
        layer_out,
        resid_grad,
        query_grad.reshape(tok, -1),
        key_grad.reshape(tok, -1),
        value_grad.reshape(tok, -1),
    )


def solution(mesh):
    every = ("dp",) + EXPERT
    split = Mesh(mesh.devices.reshape(mesh.devices.shape[:1] + SPLIT), every)
    rows = P(every, None)
    in_specs = (
        rows,
        rows,
        rows,
        rows,
        P(every),
        P("dp", EXPERT),
        P(),
        P(EXPERT, "dp", None),
        P(EXPERT, "dp", None),
        P(EXPERT, None, "dp"),
        rows,
        rows,
        rows,
    )
    return jax.shard_map(
        local, mesh=split, in_specs=in_specs, out_specs=(rows,) * 5, check_vma=False
    )
```

time: 410 us -> 301 us (0.73)
  waiting for transfers between devices: 232 us -> 128 us
  blocking collectives: 59.3 us -> 0 us
  starting transfers between devices: 40.2 us -> 69.4 us
  local copies, waits for them, and re-layouts: 24.3 us -> 51.4 us
  matrix products: 34.8 us -> 26 us
  other arithmetic: 3.8 us -> 9.64 us
    all_gather x4 -> x1, waiting for transfers between devices: 129 us -> 0.01 us  [gather_experts(): full = lax.all_gather(mine, 'dp', axis=0, tiled=False)]
    all_gather x1 -> x0, blocking collectives: 59.3 us -> none  [local(): proj_cols = lax.all_gather(out_proj, 'expert', axis=1, tiled=True)]
    all_to_all x4 -> x5, waiting for transfers between devices: 101 us -> 128 us  [spread(): return lax.all_to_all(rows, axes, split_axis=0, concat_axis=0, tiled=True)]
    ppermute x0 -> x7, starting transfers between devices: none -> 26.1 us  [the longest x4 15 us: gather_proj(): others = [lax.ppermute(part, 'core', [(0, 1), (1, 0)]) for part in shifted]]
    slice x0 -> x2, local copies, waits for them, and re-layouts: none -> 8.52 us  [the longest x1 5.68 us: gather_experts(): gate = full[:, 0].reshape(slices * rows, hidden)]
    transpose x0 -> x2, local copies, waits for them, and re-layouts: none -> 7.93 us  [the longest x1 4.86 us: gather_proj(): turned.transpose(0, 3, 1, 4, 2, 5)]
    another operation x0 -> x9, other arithmetic: none -> 7.7 us  [the longest x4 4.66 us: gather_proj(): jnp.stack([jnp.where(first, mine, other), jnp.where(first, other, mine)])]
    dot_general x4, matrix products: 14.4 us -> 6.95 us  [the longest x1 4.3 us: local(): jnp.dot(act, w_out, preferred_element_type=jnp.float32).astype(jnp.bfloat16)]
  transfers between devices with their start and end apart: 8 -> 13, of which waited for: 7 -> 5; matrix products, arithmetic and copies ran while one was open for 12% -> 18% of each run, Pallas kernels for 0% -> 0%
where the time goes in v1:
time: 301 us; the launch traced here: 299 us
  waiting for transfers between devices  128 us (43%)
  starting transfers between devices  69.4 us (23%)
  local copies, waits for them, and re-layouts  51.4 us (17%)
  matrix products  26 us (9%)
  between operations  14.7 us (5%)
  other arithmetic  9.64 us (3%)
    all_to_all x5, waiting for transfers between devices, spread(): return lax.all_to_all(rows, axes, split_axis=0, concat_axis=0, tiled=True)  128 us
    all_to_all x5, starting transfers between devices, spread(): return lax.all_to_all(rows, axes, split_axis=0, concat_axis=0, tiled=True)  43.3 us
    ppermute x4, starting transfers between devices, gather_proj(): others = [lax.ppermute(part, 'core', [(0, 1), (1, 0)]) for part in shifted]  15 us
    ppermute x3, starting transfers between devices, gather_proj(): lax.ppermute(near, 'x', [(i, (i + k) % xs) for i in range(xs)])  11.1 us
    unnamed x59, local copies, waits for them, and re-layouts  8.06 us
    reshape x2, local copies, waits for them, and re-layouts, local(): recv_rows = spread(send_rows.reshape(lanes), EXPERT).reshape(-1, width)  7.41 us
    reshape x2, local copies, waits for them, and re-layouts, local(): back_out = spread(out.reshape(lanes), EXPERT).reshape(-1, width)  6.29 us
  transfers between devices with their start and end apart: 13, of which 5 were waited for; matrix products, arithmetic and copies ran while one was open for 18% of the time, Pallas kernels for 0%

profile of v1, /device:TPU:1, one launch (start us, length us, event | category | flops | bytes accessed | tf_op | source)
XLA Modules:
  0.0 299.4 jit_solution(4860528431942565213)
XLA Ops:
  7.2 1.0 slice_bitcast_fusion.1
  8.3 2.1 pad_maximum_fusion.1
  10.4 0.9 broadcast_in_dim.12
  11.3 17.1 %all-to-all-start = ((bf16[64,32,128]{2,1,0:T(8,128)(2,1)}), bf16[64,32,128]{2,1,0:T(8,128)(2,1)S(1)}, u32[]{:S(2)}, u32[]{:S(2)}) async-start(bf16[64,32,128]{2,1,0:T(8,128)(2,1)} %broadcast_in_dim.12), calls=%async_computation | async-start | bytes 1048576 | tf_op jit(solution)/shard_map/all_to_all | solution.py:43
  29.2 0.6 fusion.40
  29.9 0.7 add_convert_fusion.1
  30.6 15.3 %all-to-all-done = bf16[64,32,128]{2,1,0:T(8,128)(2,1)S(1)} async-done(((bf16[64,32,128]{2,1,0:T(8,128)(2,1)}), bf16[64,32,128]{2,1,0:T(8,128)(2,1)S(1)}, u32[]{:S(2)}, u32[]{:S(2)}) %all-to-all-start) | async-done | bytes 524320 | tf_op jit(solution)/shard_map/all_to_all | solution.py:43
  45.9 4.6 %collective-permute-start.3 = (bf16[8,8,32,128]{3,2,1,0:T(8,128)(2,1)S(1)}, bf16[8,8,32,128]{3,2,1,0:T(8,128)(2,1)}, u32[]{:S(2)}, u32[]{:S(2)}) collective-permute-start(bf16[8,8,32,128]{3,2,1,0:T(8,128)(2,1)S(1)} %bitcast.125), channel_id=1, source_target_pairs={{0,32},{16,48},{32,0},{48,16},{1,33},{17,49},{33,1},{49,17},{2,34}... | collective-permute-start | bytes 1572872 | tf_op jit(solution)/shard_map/ppermute | solution.py:60
  50.7 1.2 copy.142
  52.0 2.2 collective-permute-start.1
  54.3 4.3 %collective-permute-start.5 = (bf16[8,8,32,128]{3,2,1,0:T(8,128)(2,1)S(1)}, bf16[8,8,32,128]{3,2,1,0:T(8,128)(2,1)}, u32[]{:S(2)}, u32[]{:S(2)}) collective-permute-start(bf16[8,8,32,128]{3,2,1,0:T(8,128)(2,1)S(1)} %bitcast.127), channel_id=1, source_target_pairs={{0,48},{16,0},{32,16},{48,32},{1,49},{17,1},{33,17},{49,33},{2,50}... | collective-permute-start | bytes 1572872 | tf_op jit(solution)/shard_map/ppermute | solution.py:60
  58.6 6.0 %collective-permute-start = (bf16[8,8,32,128]{3,2,1,0:T(8,128)(2,1)S(1)}, bf16[8,8,32,128]{3,2,1,0:T(8,128)(2,1)}, u32[]{:S(2)}, u32[]{:S(2)}) collective-permute-start(bf16[8,8,32,128]{3,2,1,0:T(8,128)(2,1)S(1)} %bitcast.128), channel_id=1, source_target_pairs={{0,1},{1,0},{2,3},{3,2},{4,5},{5,4},{6,7},{7,6},{8,9},{9,8},{10,11... | collective-permute-start | bytes 1572872 | tf_op jit(solution)/shard_map/ppermute | solution.py:63
  64.9 4.4 %collective-permute-start.4 = (bf16[8,8,32,128]{3,2,1,0:T(8,128)(2,1)}, bf16[8,8,32,128]{3,2,1,0:T(8,128)(2,1)}, u32[]{:S(2)}, u32[]{:S(2)}) collective-permute-start(bf16[8,8,32,128]{3,2,1,0:T(8,128)(2,1)} %collective-permute-done.3), channel_id=1, source_target_pairs={{0,1},{1,0},{2,3},{3,2},{4,5},{5,4},{6,7},{7,6},{8,9},{9,8},{10,11... | collective-permute-start | bytes 1572872 | tf_op jit(solution)/shard_map/ppermute | solution.py:63
  69.3 0.9 fusion.83
  70.2 1.0 convolution_convert_fusion.3
  71.3 2.1 reshape.144
  73.4 7.5 %all-to-all-start.3 = ((bf16[64,96,128]{2,1,0:T(8,128)(2,1)}), bf16[64,96,128]{2,1,0:T(8,128)(2,1)S(1)}, u32[]{:S(2)}, u32[]{:S(2)}) async-start(bf16[64,96,128]{2,1,0:T(8,128)(2,1)} %reshape.144), calls=%async_computation.3 | async-start | bytes 3145728 | tf_op jit(solution)/shard_map/all_to_all | solution.py:43
  80.9 2.4 collective-permute-start.2
  83.3 2.1 collective-permute-start.6
  85.5 1.1 select_bitcast_fusion.7
  86.6 1.3 select_bitcast_fusion.3
  87.9 1.1 select_bitcast_fusion.1
  89.2 1.1 select_bitcast_fusion.5
  90.5 0.6 pad_maximum_fusion
  91.1 1.1 constant_dynamic-slice_fusion.3
  92.2 0.6 maximum_bitcast_fusion
  92.8 4.9 %copy.123 = bf16[4,8,2,32,8,128]{5,4,3,2,1,0:T(8,128)(2,1)S(1)} copy(bf16[4,8,2,32,8,128]{5,3,1,4,2,0:T(8,128)(2,1)S(1)} %maximum_bitcast_fusion) | data formatting | bytes 8388608 | tf_op jit(solution)/shard_map/transpose | solution.py:71
  97.7 1.6 multiply_reduce_fusion.1
  99.8 1.8 convolution_convert_fusion.1
  101.6 3.7 %reshape.139 = bf16[64,96,128]{2,1,0:T(8,128)(2,1)} reshape(bf16[384,2048]{1,0:T(8,128)(2,1)} %convolution_convert_fusion.1) | data formatting | bytes 3145728 | tf_op jit(solution)/shard_map/reshape | solution.py:148
  105.3 15.3 %all-to-all-done.3 = bf16[64,96,128]{2,1,0:T(8,128)(2,1)S(1)} async-done(((bf16[64,96,128]{2,1,0:T(8,128)(2,1)}), bf16[64,96,128]{2,1,0:T(8,128)(2,1)S(1)}, u32[]{:S(2)}, u32[]{:S(2)}) %all-to-all-start.3) | async-done | bytes 1572896 | tf_op jit(solution)/shard_map/all_to_all | solution.py:43
  120.7 6.3 %all-to-all-start.1 = ((bf16[64,96,128]{2,1,0:T(8,128)(2,1)}), bf16[64,96,128]{2,1,0:T(8,128)(2,1)}, u32[]{:S(2)}, u32[]{:S(2)}) async-start(bf16[64,96,128]{2,1,0:T(8,128)(2,1)} %reshape.139), calls=%async_computation.1 | async-start | bytes 3145728 | tf_op jit(solution)/shard_map/all_to_all | solution.py:43
  126.9 2.1 reshape.145
  129.0 37.6 %all-to-all-done.1 = bf16[64,96,128]{2,1,0:T(8,128)(2,1)} async-done(((bf16[64,96,128]{2,1,0:T(8,128)(2,1)}), bf16[64,96,128]{2,1,0:T(8,128)(2,1)}, u32[]{:S(2)}, u32[]{:S(2)}) %all-to-all-start.1) | async-done | bytes 1572896 | tf_op jit(solution)/shard_map/all_to_all | solution.py:43
  166.6 3.7 %reshape.140 = bf16[384,2048]{1,0:T(8,128)(2,1)} reshape(bf16[64,96,128]{2,1,0:T(8,128)(2,1)} %all-to-all-done.1) | data formatting | bytes 3145728 | tf_op jit(solution)/shard_map/reshape | solution.py:148
  170.3 5.7 %fusion.82 = (bf16[8,1,256,512]{3,2,1,0:T(8,128)(2,1)}, bf16[8,1,256,512]{3,2,1,0:T(8,128)(2,1)}, bf16[8,1,256,512]{3,2,1,0:T(8,128)(2,1)}) fusion(bf16[8,3,256,512]{3,2,1,0:T(8,128)(2,1)} %bitcast.122), kind=kLoop, calls=%fused_computation.126 | loop fusion | bytes 12582912 | tf_op jit(solution)/shard_map/slice | solution.py:81
  176.0 2.8 copy.124
  178.8 3.1 %copy.125 = bf16[2,256,8,256]{3,2,1,0:T(8,128)(2,1)} copy(bf16[2,256,8,256]{1,3,0,2:T(8,128)(2,1)S(1)} %bitcast.118) | data formatting | bytes 4194304 | tf_op jit(solution)/shard_map/transpose | solution.py:83
  181.9 2.4 copy.146
  184.6 1.0 fusion.84
  185.6 1.4 copy-done.1
  187.0 1.0 fusion.85
  188.4 1.1 fusion.86
  189.5 1.2 fusion.46
  190.7 1.0 add_convert_fusion
  191.8 2.1 reshape.146
  193.9 6.1 %all-to-all-start.4 = ((bf16[64,96,128]{2,1,0:T(8,128)(2,1)}), bf16[64,96,128]{2,1,0:T(8,128)(2,1)S(1)}, u32[]{:S(2)}, u32[]{:S(2)}) async-start(bf16[64,96,128]{2,1,0:T(8,128)(2,1)} %reshape.146), calls=%async_computation.4 | async-start | bytes 3145728 | tf_op jit(solution)/shard_map/all_to_all | solution.py:43
  200.0 4.3 %convolution_convert_fusion = bf16[384,2048]{1,0:T(8,128)(2,1)} fusion(bf16[512,2048]{1,0:T(8,128)(2,1)} %bitcast.131, f32[384,512]{1,0:T(8,128)} %copy-done.25, f32[384,512]{1,0:T(8,128)} %copy-done.15), kind=kOutput, calls=%fused_computation.12 | convolution fusion | flops 807272448 | bytes 5242880 | tf_op jit(solution)/shard_map/dot_general | solution.py:160
  204.3 3.7 %reshape.142 = bf16[64,96,128]{2,1,0:T(8,128)(2,1)} reshape(bf16[384,2048]{1,0:T(8,128)(2,1)} %convolution_convert_fusion) | data formatting | bytes 3145728 | tf_op jit(solution)/shard_map/reshape | solution.py:161
  208.0 31.7 %all-to-all-done.4 = bf16[64,96,128]{2,1,0:T(8,128)(2,1)S(1)} async-done(((bf16[64,96,128]{2,1,0:T(8,128)(2,1)}), bf16[64,96,128]{2,1,0:T(8,128)(2,1)S(1)}, u32[]{:S(2)}, u32[]{:S(2)}) %all-to-all-start.4) | async-done | bytes 1572896 | tf_op jit(solution)/shard_map/all_to_all | solution.py:43
  239.7 6.3 %all-to-all-start.2 = ((bf16[64,96,128]{2,1,0:T(8,128)(2,1)}), bf16[64,96,128]{2,1,0:T(8,128)(2,1)}, u32[]{:S(2)}, u32[]{:S(2)}) async-start(bf16[64,96,128]{2,1,0:T(8,128)(2,1)} %reshape.142), calls=%async_computation.2 | async-start | bytes 3145728 | tf_op jit(solution)/shard_map/all_to_all | solution.py:43
  246.0 2.1 reshape.147
  248.1 2.1 multiply_reduce_fusion
  250.9 0.7 fusion.27
  251.9 1.5 convolution_convert_fusion.4
  253.7 1.6 convolution_convert_fusion.2
  255.2 2.3 convolution_convert_fusion.5
  257.5 28.1 %all-to-all-done.2 = bf16[64,96,128]{2,1,0:T(8,128)(2,1)} async-done(((bf16[64,96,128]{2,1,0:T(8,128)(2,1)}), bf16[64,96,128]{2,1,0:T(8,128)(2,1)}, u32[]{:S(2)}, u32[]{:S(2)}) %all-to-all-start.2) | async-done | bytes 1572896 | tf_op jit(solution)/shard_map/all_to_all | solution.py:43
  285.7 2.5 reshape.143
  288.2 0.5 fusion.9
  288.8 1.3 fusion.13
  290.0 0.8 copy.136
  290.9 0.8 copy.135
  291.7 0.8 copy.134
  (84 shorter events, 4.0 us)
Async XLA Ops:
  7.2 63.1 %copy-start = (bf16[128,1024]{1,0:T(8,128)(2,1)S(1)}, bf16[128,1024]{1,0:T(8,128)(2,1)}, u32[]{:S(2)}) copy-start(bf16[128,1024]{1,0:T(8,128)(2,1)} %param.16) | copy-start | bytes 786436
  7.2 3.3 %copy-start.20 = (bf16[128,32]{0,1:T(8,128)(2,1)S(1)}, bf16[128,32]{0,1:T(8,128)(2,1)}, u32[]{:S(2)}) copy-start(bf16[128,32]{0,1:T(8,128)(2,1)} %param.18) | copy-start | bytes 24580
  7.2 163.1 %all-gather.3.cloned.1.call-start = ((), (), s32[]{:S(2)}) async-start(), calls=%async_computation.5 | async-start | bytes 7077888 | tf_op jit(solution)/shard_map/all_gather | solution.py:79
  8.3 20.2 %copy-start.21 = (s32[128,2]{0,1:T(2,128)S(1)}, s32[128,2]{0,1:T(2,128)}, u32[]{:S(2)}) copy-start(s32[128,2]{0,1:T(2,128)} %param.23) | copy-start | bytes 3076
  8.3 20.8 %copy-start.23 = (s32[128,2]{0,1:T(2,128)S(1)}, s32[128,2]{0,1:T(2,128)}, u32[]{:S(2)}) copy-start(s32[128,2]{0,1:T(2,128)} %param.24) | copy-start | bytes 3076
  8.3 20.9 %copy-start.2 = (bf16[128,2048]{1,0:T(8,128)(2,1)S(1)}, bf16[128,2048]{1,0:T(8,128)(2,1)}, u32[]{:S(2)}) copy-start(bf16[128,2048]{1,0:T(8,128)(2,1)} %param.25) | copy-start | bytes 1572868
  11.3 34.6 %all-to-all-start = ((bf16[64,32,128]{2,1,0:T(8,128)(2,1)}), bf16[64,32,128]{2,1,0:T(8,128)(2,1)S(1)}, u32[]{:S(2)}, u32[]{:S(2)}) async-start(bf16[64,32,128]{2,1,0:T(8,128)(2,1)} %broadcast_in_dim.12), calls=%async_computation | async-start | bytes 1048576 | tf_op jit(solution)/shard_map/all_to_all | solution.py:43
  29.9 20.7 %copy-start.17 = (bf16[128,1024]{1,0:T(8,128)(2,1)S(1)}, bf16[128,1024]{1,0:T(8,128)(2,1)}, u32[]{:S(2)}) copy-start(bf16[128,1024]{1,0:T(8,128)(2,1)} %param.14) | copy-start | bytes 786436
  29.9 22.1 %copy-start.22 = (s32[128]{0:T(128)S(1)}, s32[128]{0:T(128)}, u32[]{:S(2)}) copy-start(s32[128]{0:T(128)} %param.17) | copy-start | bytes 1540
  45.9 19.0 %collective-permute-start.3 = (bf16[8,8,32,128]{3,2,1,0:T(8,128)(2,1)S(1)}, bf16[8,8,32,128]{3,2,1,0:T(8,128)(2,1)}, u32[]{:S(2)}, u32[]{:S(2)}) collective-permute-start(bf16[8,8,32,128]{3,2,1,0:T(8,128)(2,1)S(1)} %bitcast.125), channel_id=1, source_target_pairs={{0,32},{16,48},{32,0},{48,16},{1,33},{17,49},{33,1},{49,17},{2,34}... | collective-permute-start | bytes 1572872 | tf_op jit(solution)/shard_map/ppermute | solution.py:60
  50.7 20.6 %copy-start.11 = (bf16[128,1024]{0,1:T(8,128)(2,1)}, bf16[128,1024]{0,1:T(8,128)(2,1)S(1)}, u32[]{:S(2)}) copy-start(bf16[128,1024]{0,1:T(8,128)(2,1)S(1)} %copy.141) | copy-start | bytes 786436
  51.9 19.3 %copy-start.13 = (bf16[128,1024]{0,1:T(8,128)(2,1)}, bf16[128,1024]{0,1:T(8,128)(2,1)S(1)}, u32[]{:S(2)}) copy-start(bf16[128,1024]{0,1:T(8,128)(2,1)S(1)} %copy.142) | copy-start | bytes 786436
  52.0 28.9 %collective-permute-start.1 = (bf16[8,8,32,128]{3,2,1,0:T(8,128)(2,1)S(1)}, bf16[8,8,32,128]{3,2,1,0:T(8,128)(2,1)}, u32[]{:S(2)}, u32[]{:S(2)}) collective-permute-start(bf16[8,8,32,128]{3,2,1,0:T(8,128)(2,1)S(1)} %bitcast.126), channel_id=1, source_target_pairs={{0,16},{16,32},{32,48},{48,0},{1,17},{17,33},{33,49},{49,1},{2,18}... | collective-permute-start | bytes 1572872 | tf_op jit(solution)/shard_map/ppermute | solution.py:60
  54.3 29.0 %collective-permute-start.5 = (bf16[8,8,32,128]{3,2,1,0:T(8,128)(2,1)S(1)}, bf16[8,8,32,128]{3,2,1,0:T(8,128)(2,1)}, u32[]{:S(2)}, u32[]{:S(2)}) collective-permute-start(bf16[8,8,32,128]{3,2,1,0:T(8,128)(2,1)S(1)} %bitcast.127), channel_id=1, source_target_pairs={{0,48},{16,0},{32,16},{48,32},{1,49},{17,1},{33,17},{49,33},{2,50}... | collective-permute-start | bytes 1572872 | tf_op jit(solution)/shard_map/ppermute | solution.py:60
  58.6 26.9 %collective-permute-start = (bf16[8,8,32,128]{3,2,1,0:T(8,128)(2,1)S(1)}, bf16[8,8,32,128]{3,2,1,0:T(8,128)(2,1)}, u32[]{:S(2)}, u32[]{:S(2)}) collective-permute-start(bf16[8,8,32,128]{3,2,1,0:T(8,128)(2,1)S(1)} %bitcast.128), channel_id=1, source_target_pairs={{0,1},{1,0},{2,3},{3,2},{4,5},{5,4},{6,7},{7,6},{8,9},{9,8},{10,11... | collective-permute-start | bytes 1572872 | tf_op jit(solution)/shard_map/ppermute | solution.py:63
  64.9 8.5 %copy-start.7 = (f32[8,128,128]{1,2,0:T(8,128)}, f32[8,128,128]{1,2,0:T(8,128)S(1)}, u32[]{:S(2)}) copy-start(f32[8,128,128]{1,2,0:T(8,128)S(1)} %fusion.25) | copy-start | bytes 1572868
  64.9 21.7 %collective-permute-start.4 = (bf16[8,8,32,128]{3,2,1,0:T(8,128)(2,1)}, bf16[8,8,32,128]{3,2,1,0:T(8,128)(2,1)}, u32[]{:S(2)}, u32[]{:S(2)}) collective-permute-start(bf16[8,8,32,128]{3,2,1,0:T(8,128)(2,1)} %collective-permute-done.3), channel_id=1, source_target_pairs={{0,1},{1,0},{2,3},{3,2},{4,5},{5,4},{6,7},{7,6},{8,9},{9,8},{10,11... | collective-permute-start | bytes 1572872 | tf_op jit(solution)/shard_map/ppermute | solution.py:63
  73.4 47.3 %all-to-all-start.3 = ((bf16[64,96,128]{2,1,0:T(8,128)(2,1)}), bf16[64,96,128]{2,1,0:T(8,128)(2,1)S(1)}, u32[]{:S(2)}, u32[]{:S(2)}) async-start(bf16[64,96,128]{2,1,0:T(8,128)(2,1)} %reshape.144), calls=%async_computation.3 | async-start | bytes 3145728 | tf_op jit(solution)/shard_map/all_to_all | solution.py:43
  80.9 8.3 %collective-permute-start.2 = (bf16[8,8,32,128]{3,2,1,0:T(8,128)(2,1)}, bf16[8,8,32,128]{3,2,1,0:T(8,128)(2,1)S(1)}, u32[]{:S(2)}, u32[]{:S(2)}) collective-permute-start(bf16[8,8,32,128]{3,2,1,0:T(8,128)(2,1)} %collective-permute-done.1), channel_id=1, source_target_pairs={{0,1},{1,0},{2,3},{3,2},{4,5},{5,4},{6,7},{7,6},{8,9},{9,8},{10,11... | collective-permute-start | bytes 1572872 | tf_op jit(solution)/shard_map/ppermute | solution.py:63
  83.3 4.6 %collective-permute-start.6 = (bf16[8,8,32,128]{3,2,1,0:T(8,128)(2,1)}, bf16[8,8,32,128]{3,2,1,0:T(8,128)(2,1)S(1)}, u32[]{:S(2)}, u32[]{:S(2)}) collective-permute-start(bf16[8,8,32,128]{3,2,1,0:T(8,128)(2,1)} %collective-permute-done.5), channel_id=1, source_target_pairs={{0,1},{1,0},{2,3},{3,2},{4,5},{5,4},{6,7},{7,6},{8,9},{9,8},{10,11... | collective-permute-start | bytes 1572872 | tf_op jit(solution)/shard_map/ppermute | solution.py:63
  92.8 4.9 %copy-start.24 = (bf16[128,2048]{1,0:T(8,128)(2,1)S(1)}, bf16[128,2048]{1,0:T(8,128)(2,1)}, u32[]{:S(2)}) copy-start(bf16[128,2048]{1,0:T(8,128)(2,1)} %param.13) | copy-start | bytes 1572868
  92.8 4.9 %copy-start.26 = (bf16[8,128,128]{1,2,0:T(8,128)(2,1)S(1)}, bf16[8,128,128]{1,2,0:T(8,128)(2,1)}, u32[]{:S(2)}) copy-start(bf16[8,128,128]{1,2,0:T(8,128)(2,1)} %convolution_convert_fusion.3) | copy-start | bytes 786436
  97.7 2.1 copy-start.4
  97.7 2.0 copy-start.19
  120.7 46.0 %all-to-all-start.1 = ((bf16[64,96,128]{2,1,0:T(8,128)(2,1)}), bf16[64,96,128]{2,1,0:T(8,128)(2,1)}, u32[]{:S(2)}, u32[]{:S(2)}) async-start(bf16[64,96,128]{2,1,0:T(8,128)(2,1)} %reshape.139), calls=%async_computation.1 | async-start | bytes 3145728 | tf_op jit(solution)/shard_map/all_to_all | solution.py:43
  181.9 2.5 copy-start.8
  181.9 2.7 copy-start.10
  184.4 3.6 %copy-start.6 = (bf16[64,8,8,256]{3,1,2,0:T(8,128)(2,1)}, bf16[64,8,8,256]{3,1,2,0:T(8,128)(2,1)S(1)}, u32[]{:S(2)}) copy-start(bf16[64,8,8,256]{3,1,2,0:T(8,128)(2,1)S(1)} %copy.146) | copy-start | bytes 6291460
  184.6 2.4 copy-start.1
  185.6 5.2 %copy-start.15 = (f32[384,512]{1,0:T(8,128)}, f32[384,512]{1,0:T(8,128)S(1)}, u32[]{:S(2)}) copy-start(f32[384,512]{1,0:T(8,128)S(1)} %fusion.84) | copy-start | bytes 2359300
  187.0 1.4 copy-start.9
  188.0 1.5 copy-start.25
  193.9 45.9 %all-to-all-start.4 = ((bf16[64,96,128]{2,1,0:T(8,128)(2,1)}), bf16[64,96,128]{2,1,0:T(8,128)(2,1)S(1)}, u32[]{:S(2)}, u32[]{:S(2)}) async-start(bf16[64,96,128]{2,1,0:T(8,128)(2,1)} %reshape.146), calls=%async_computation.4 | async-start | bytes 3145728 | tf_op jit(solution)/shard_map/all_to_all | solution.py:43
  239.7 46.0 %all-to-all-start.2 = ((bf16[64,96,128]{2,1,0:T(8,128)(2,1)}), bf16[64,96,128]{2,1,0:T(8,128)(2,1)}, u32[]{:S(2)}, u32[]{:S(2)}) async-start(bf16[64,96,128]{2,1,0:T(8,128)(2,1)} %reshape.142), calls=%async_computation.2 | async-start | bytes 3145728 | tf_op jit(solution)/shard_map/all_to_all | solution.py:43
  248.1 2.1 copy-start.3
  248.1 2.8 copy-start.5
  250.9 0.8 copy-start.16
  251.7 2.0 copy-start.14
  253.4 1.8 copy-start.12
  288.7 2.2 copy-start.18
Sparse Core Ops, SparseCore 0:
  10.6 93.2 all-gather.2

commit v2 on v1

v2 whole, which is shorter than its diff:
```python
import jax
import jax.numpy as jnp
from jax import lax
from jax.experimental import pallas as pl
from jax.experimental.pallas import tpu as pltpu
from jax.sharding import Mesh, PartitionSpec as P


HEAD_DIM = 128
EXPERT = ("x", "y", "core")
SPLIT = (4, 8, 2)
LANES = 128


epsilon = 1e-06
masked = -1e30
VMEM = pl.BlockSpec(memory_space=pltpu.VMEM)
SMEM = pl.BlockSpec(memory_space=pltpu.SMEM)


def contract_last(left, right):
    return lax.dot_general(
        left, right, (((1,), (1,)), ((), ())), preferred_element_type=jnp.float32
    )


def call(body, outs, scratch, specs):
    return pl.pallas_call(
        body,
        grid=(1,),
        out_shape=outs,
        in_specs=specs,
        out_specs=jax.tree.map(lambda _: VMEM, outs),
        scratch_shapes=scratch,
    )


def shape_of(rows, cols, dtype=jnp.bfloat16):
    return jax.ShapeDtypeStruct((rows, cols), dtype)


def to_tiled(rows_of, tiled, count, parts):
    for part in range(parts):
        tiled[pl.ds(part, count, stride=parts), :] = rows_of(part)


def to_rows(tiled, count, parts, put):
    for part in range(parts):
        put(part, tiled[pl.ds(part, count, stride=parts), :])


def lanes_of(part):
    return slice(part * LANES, (part + 1) * LANES)


def block(index, parts):
    return pl.ds(pl.multiple_of(index * parts, parts), parts)


def send_grads_kernel(dest, gate, grad, out, tiled):
    tok, width = grad.shape
    parts = width // LANES
    to_tiled(lambda p: grad[:, lanes_of(p)].astype(jnp.float32), tiled, tok, parts)
    out[...] = jnp.zeros_like(out)

    def step(t, carry):
        row = tiled[block(t, parts), :]
        out[block(dest[2 * t], parts), :] = (gate[2 * t] * row).astype(jnp.bfloat16)
        out[block(dest[2 * t + 1], parts), :] = (gate[2 * t + 1] * row).astype(jnp.bfloat16)
        return carry

    lax.fori_loop(0, tok, step, 0, unroll=8)


def send_grads(dest, gate, grad, slots):
    tok, width = grad.shape
    parts = width // LANES
    return call(
        send_grads_kernel,
        shape_of(slots * parts, LANES),
        [pltpu.VMEM((tok * parts, LANES), jnp.float32)],
        [SMEM, SMEM, VMEM],
    )(dest, gate, grad)


def resid_kernel(dest, place, *refs):
    pieces, (context, hidden, gain, proj, resid, out, tiled, normed) = refs[:8], refs[8:]
    tok, width = hidden.shape
    parts = width // LANES
    heads, ys, cols, depth = pieces[0].shape
    xs = len(pieces) // 2

    def fill(y, carry):
        for k in range(xs):
            x = lax.rem(place[0] + xs - k, xs)
            for which in range(2):
                core = place[1] if which == 0 else 1 - place[1]
                at = pl.multiple_of(((x * ys + y) * 2 + core) * cols, cols)
                for h in range(heads):
                    proj[pl.ds(at, cols), h * depth : (h + 1) * depth] = pieces[
                        2 * k + which
                    ][h, y]
        return carry

    lax.fori_loop(0, ys, fill, 0)
    chunk = 512
    total = jnp.zeros((tok, 1), jnp.float32)
    for n in range(0, width, chunk):
        some = slice(n, n + chunk)
        row = hidden[:, some].astype(jnp.float32) + contract_last(context[...], proj[some, :])
        row = row.astype(jnp.bfloat16)
        resid[:, some] = row
        row = row.astype(jnp.float32)
        total = total + jnp.sum(row * row, axis=-1, keepdims=True)
    inv_rms = lax.rsqrt(total / width + epsilon)
    to_tiled(
        lambda p: resid[:, lanes_of(p)].astype(jnp.float32) * inv_rms * gain[:, lanes_of(p)],
        tiled,
        tok,
        parts,
    )
    normed[...] = tiled[...].astype(jnp.bfloat16)
    out[...] = jnp.zeros_like(out)

    def step(t, carry):
        row = normed[block(t, parts), :]
        out[block(dest[2 * t], parts), :] = row
        out[block(dest[2 * t + 1], parts), :] = row
        return carry

    lax.fori_loop(0, tok, step, 0, unroll=8)


def make_resid(dest, place, pieces, context, hidden, gain, slots):
    tok, width = hidden.shape
    parts = width // LANES
    return call(
        resid_kernel,
        (
            shape_of(width, context.shape[1]),
            shape_of(tok, width),
            shape_of(slots * parts, LANES),
        ),
        [
            pltpu.VMEM((tok * parts, LANES), jnp.float32),
            pltpu.VMEM((tok * parts, LANES), jnp.bfloat16),
        ],
        [SMEM, SMEM] + [VMEM] * (len(pieces) + 3),
    )(dest, place, *pieces, context, hidden, gain[None])


def load_rows(source, tiled, rows):
    count, width = rows.shape
    parts = width // LANES
    tiled[...] = source[...].astype(jnp.float32)

    def put(part, values):
        rows[:, lanes_of(part)] = values.astype(jnp.bfloat16)

    to_rows(tiled, count, parts, put)


def act_grad_kernel(place, source, *refs):
    pieces, (out, weights, tiled, rows) = refs[:-4], refs[-4:]
    count, depth = weights.shape[0], weights.shape[2]
    half = depth // 2
    me = place[2]
    for n, piece in enumerate(pieces[:-2]):
        turn = (n + 1) // 2
        weights[lax.rem(me + (turn if n % 2 == 0 else count - turn), count)] = piece[...]
    opposite = lax.rem(me + count // 2, count)
    weights[opposite, :, :half] = pieces[-2][...]
    weights[opposite, :, half:] = pieces[-1][...]
    load_rows(source, tiled, rows)
    for part in range(2):
        some = slice(part * depth, (part + 1) * depth)
        total = None
        for d in range(count):
            term = contract_last(
                rows[:, d * depth : (d + 1) * depth], weights[d, 2, :, some]
            )
            total = term if total is None else total + term
        out[:, some] = total


def w_spec(weights, which):
    slices, _, depth, hidden = weights.shape
    return pl.BlockSpec(
        (slices, None, depth, hidden),
        lambda i: (0, which, 0, 0),
        pipeline_mode=pl.Buffered(1),
    )


def act_grad_of(place, source, pieces, width):
    slots = source.shape[0] * LANES // width
    kinds, depth, hidden = pieces[0].shape
    count = width // depth
    return call(
        act_grad_kernel,
        (
            shape_of(slots, hidden, jnp.float32),
            jax.ShapeDtypeStruct((count, kinds, depth, hidden), jnp.bfloat16),
        ),
        [pltpu.VMEM(source.shape, jnp.float32), pltpu.VMEM((slots, width), jnp.bfloat16)],
        [SMEM, VMEM] + [VMEM] * len(pieces),
    )(place, source, *pieces)


def expert_kernel(source, gate_w, up_w, act_grad, in_grad, act, tiled, rows):
    load_rows(source, tiled, rows)
    slices, depth, hidden = gate_w.shape
    count = rows.shape[0]
    values = rows[...]
    pre_gate = jnp.dot(
        values, gate_w[...].reshape(slices * depth, hidden), preferred_element_type=jnp.float32
    )
    pre_up = jnp.dot(
        values, up_w[...].reshape(slices * depth, hidden), preferred_element_type=jnp.float32
    )
    sig = jax.nn.sigmoid(pre_gate)
    silu = pre_gate * sig
    act[...] = (silu * pre_up).astype(jnp.bfloat16)
    back = act_grad[...]
    gate_grad = (back * pre_up * sig * (1.0 + pre_gate * (1.0 - sig))).astype(jnp.bfloat16)
    up_grad = (back * silu).astype(jnp.bfloat16)
    parts = slices * depth // LANES
    for d in range(slices):
        entry = contract_last(gate_grad, gate_w[d]) + contract_last(up_grad, up_w[d])
        for p in range(depth // LANES):
            tiled[pl.ds(d * (depth // LANES) + p, count, stride=parts), :] = entry[
                :, lanes_of(p)
            ]
    in_grad[...] = tiled[...].astype(jnp.bfloat16)


def expert_back(source, weights, act_grad):
    slots, hidden = act_grad.shape
    width = weights.shape[0] * weights.shape[2]
    return call(
        expert_kernel,
        (shape_of(*source.shape), shape_of(slots, hidden)),
        [pltpu.VMEM(source.shape, jnp.float32), pltpu.VMEM((slots, width), jnp.bfloat16)],
        [VMEM, w_spec(weights, 0), w_spec(weights, 1), VMEM],
    )(source, weights, weights, act_grad)


def out_kernel(act, down, out, tiled):
    slices, depth, _ = down.shape
    count = act.shape[0]
    parts = slices * depth // LANES
    for d in range(slices):
        total = jnp.dot(act[:, :depth], down[d, :, :depth], preferred_element_type=jnp.float32)
        total = total + jnp.dot(
            act[:, depth:], down[d, :, depth:], preferred_element_type=jnp.float32
        )
        for p in range(depth // LANES):
            tiled[pl.ds(d * (depth // LANES) + p, count, stride=parts), :] = total[
                :, lanes_of(p)
            ]
    out[...] = tiled[...].astype(jnp.bfloat16)


def expert_out(act, weights):
    slices, _, depth, _ = weights.shape
    rows = act.shape[0] * slices * depth // LANES
    return call(
        out_kernel,
        shape_of(rows, LANES),
        [pltpu.VMEM((rows, LANES), jnp.float32)],
        [VMEM, w_spec(weights, 2)],
    )(act, weights)


def resid_grad_kernel(dest, source, resid, gain, grad, proj, out, context_grad, tiled, rows):
    tok, width = resid.shape
    parts = width // LANES

    def step(t, carry):
        first = source[block(dest[2 * t], parts), :].astype(jnp.float32)
        second = source[block(dest[2 * t + 1], parts), :].astype(jnp.float32)
        tiled[block(t, parts), :] = first + second
        return carry

    lax.fori_loop(0, tok, step, 0, unroll=8)

    def put(part, values):
        rows[:, lanes_of(part)] = values * gain[:, lanes_of(part)]

    to_rows(tiled, tok, parts, put)
    resid_f = resid[...].astype(jnp.float32)
    inv_rms = lax.rsqrt(jnp.mean(resid_f * resid_f, axis=-1, keepdims=True) + epsilon)
    unit = resid_f * inv_rms
    scaled = rows[...]
    mean = jnp.mean(scaled * unit, axis=-1, keepdims=True)
    result = (grad[...].astype(jnp.float32) + inv_rms * (scaled - unit * mean)).astype(
        jnp.bfloat16
    )
    out[...] = result
    context_grad[...] = jnp.dot(
        result, proj[...], preferred_element_type=jnp.float32
    ).astype(jnp.bfloat16)


def resid_grad_of(dest, source, resid, gain, grad, proj):
    tok, width = resid.shape
    return call(
        resid_grad_kernel,
        (shape_of(tok, width), shape_of(tok, proj.shape[1])),
        [
            pltpu.VMEM((tok * width // LANES, LANES), jnp.float32),
            pltpu.VMEM((tok, width), jnp.float32),
        ],
        [SMEM] + [VMEM] * 5,
    )(dest, source, resid, gain[None], grad, proj)


def layer_out_kernel(dest, gate, source, resid, out, tiled):
    tok, width = resid.shape
    parts = width // LANES

    def step(t, carry):
        first = source[block(dest[2 * t], parts), :].astype(jnp.float32)
        second = source[block(dest[2 * t + 1], parts), :].astype(jnp.float32)
        tiled[block(t, parts), :] = gate[2 * t] * first + gate[2 * t + 1] * second
        return carry

    lax.fori_loop(0, tok, step, 0, unroll=8)

    def put(part, values):
        some = lanes_of(part)
        out[:, some] = (resid[:, some].astype(jnp.float32) + values).astype(jnp.bfloat16)

    to_rows(tiled, tok, parts, put)


def layer_out_of(dest, gate, source, resid):
    tok, width = resid.shape
    return call(
        layer_out_kernel,
        shape_of(tok, width),
        [pltpu.VMEM((tok * width // LANES, LANES), jnp.float32)],
        [SMEM, SMEM, VMEM, VMEM],
    )(dest, gate, source, resid)


def probs_of(query, keys, allowed):
    scores = contract_last(query, keys) * HEAD_DIM ** (-0.5)
    scores = jnp.where(allowed, scores, masked)
    top = jnp.max(scores, axis=-1, keepdims=True)
    weights = jnp.exp(scores - top)
    return weights / jnp.sum(weights, axis=-1, keepdims=True)


def allowed_of(seg_row, seg_col):
    rows = seg_row.shape[1]
    queries = lax.broadcasted_iota(jnp.int32, (rows, rows), 0)
    keys = lax.broadcasted_iota(jnp.int32, (rows, rows), 1)
    return (seg_row[...] == seg_col[...]) & (queries >= keys)


def context_kernel(seg_row, seg_col, queries, keys, values, out):
    allowed = allowed_of(seg_row, seg_col)
    for h in range(queries.shape[1] // HEAD_DIM):
        some = slice(h * HEAD_DIM, (h + 1) * HEAD_DIM)
        probs = probs_of(queries[:, some], keys[:, some], allowed).astype(jnp.bfloat16)
        out[:, some] = jnp.dot(
            probs, values[:, some], preferred_element_type=jnp.float32
        ).astype(jnp.bfloat16)


def context_of(segments, queries, keys, values):
    return call(
        context_kernel, shape_of(*queries.shape), [], [VMEM] * 5
    )(segments[None, :], segments[:, None], queries, keys, values)


def contract_first(left, right):
    return lax.dot_general(
        left, right, (((0,), (0,)), ((), ())), preferred_element_type=jnp.float32
    )


def attention_grad_kernel(
    seg_row, seg_col, queries, keys, values, context_grad, query_grad, key_grad, value_grad
):
    allowed = allowed_of(seg_row, seg_col)
    for h in range(queries.shape[1] // HEAD_DIM):
        some = slice(h * HEAD_DIM, (h + 1) * HEAD_DIM)
        query, key, back = queries[:, some], keys[:, some], context_grad[:, some]
        probs = probs_of(query, key, allowed)
        value_grad[:, some] = contract_first(probs.astype(jnp.bfloat16), back).astype(
            jnp.bfloat16
        )
        prob_grad = contract_last(back, values[:, some])
        inner = jnp.sum(prob_grad * probs, axis=-1, keepdims=True)
        score_grad = (probs * (prob_grad - inner) * HEAD_DIM ** (-0.5)).astype(jnp.bfloat16)
        query_grad[:, some] = jnp.dot(
            score_grad, key, preferred_element_type=jnp.float32
        ).astype(jnp.bfloat16)
        key_grad[:, some] = contract_first(score_grad, query).astype(jnp.bfloat16)


def attention_grad(segments, queries, keys, values, context_grad):
    return call(
        attention_grad_kernel, (shape_of(*queries.shape),) * 3, [], [VMEM] * 6
    )(segments[None, :], segments[:, None], queries, keys, values, context_grad)


def spread(rows, axes):
    return lax.all_to_all(rows, axes, split_axis=0, concat_axis=0, tiled=True)


def gather_near(out_proj):
    heads, ys = lax.axis_size("dp"), lax.axis_size("y")
    block = out_proj.T
    near = spread(jnp.broadcast_to(block[None], (heads * ys,) + block.shape), ("dp", "y"))
    return near.reshape((heads, ys) + block.shape)


def gather_pieces(near):
    xs = lax.axis_size("x")
    shifted = [near] + [
        lax.ppermute(near, "x", [(i, (i + k) % xs) for i in range(xs)])
        for k in range(1, xs)
    ]
    pieces = []
    for part in shifted:
        pieces += [part, lax.ppermute(part, "core", [(0, 1), (1, 0)])]
    return pieces


def pack_experts(w_gate, w_up, w_down):
    rows = w_gate.shape[1]
    down = jnp.concatenate([w_down[0, :rows], w_down[0, rows:]], axis=1)
    return jnp.stack([w_gate[0], w_up[0], down])


def ring_experts(mine):
    count, half = lax.axis_size("dp"), mine.shape[1] // 2
    ahead = [(i, (i + 1) % count) for i in range(count)]
    behind = [(i, (i - 1) % count) for i in range(count)]
    left = right = mine
    slices = [mine]
    for _ in range(count // 2 - 1):
        left = lax.ppermute(left, "dp", ahead)
        right = lax.ppermute(right, "dp", behind)
        slices += [left, right]
    slices.append(lax.ppermute(left[:, :half], "dp", ahead))
    slices.append(lax.ppermute(right[:, half:], "dp", behind))
    return slices


def slots_of(expert_ids, experts, capacity):
    flat_ids = expert_ids.reshape(-1)
    onehot = (flat_ids[:, None] == jnp.arange(experts, dtype=jnp.int32)[None, :]).astype(
        jnp.bfloat16
    )
    order = jnp.arange(flat_ids.shape[0], dtype=jnp.int32)
    earlier = (order[:, None] > order[None, :]).astype(jnp.bfloat16)
    before = jnp.dot(earlier, onehot, preferred_element_type=jnp.float32)
    slot = jnp.sum(before * onehot.astype(jnp.float32), axis=1).astype(jnp.int32)
    return flat_ids * capacity + slot


def local(
    hidden_in,
    queries,
    keys,
    values,
    segment_ids,
    out_proj,
    norm_gain,
    w_gate,
    w_up,
    w_down,
    expert_ids,
    gate_fixed,
    grad_out,
):
    tok, width = hidden_in.shape
    experts = lax.axis_size(EXPERT)
    capacity = 3 * tok // experts
    slots = experts * capacity
    lanes = (experts, capacity * width // LANES, LANES)
    place = jnp.stack([lax.axis_index(axis) for axis in ("x", "core", "dp")]).astype(jnp.int32)

    def exchange(tiles):
        return spread(tiles.reshape(lanes), EXPERT).reshape(-1, LANES)

    gates = gate_fixed.reshape(-1).astype(jnp.float32) / 4096.0
    dest = slots_of(expert_ids, experts, capacity)
    slices = ring_experts(pack_experts(w_gate, w_up, w_down))
    to_send = send_grads(dest, gates, grad_out, slots)
    near, to_send = lax.optimization_barrier((gather_near(out_proj), to_send))
    recv_grads = exchange(to_send)
    pieces = gather_pieces(near)
    context = context_of(segment_ids, queries, keys, values)
    proj, resid, rows = make_resid(dest, place, pieces, context, hidden_in, norm_gain, slots)
    recv_rows = exchange(rows)
    act_grad, weights = act_grad_of(place, recv_grads, slices, width)
    in_grad, act = expert_back(recv_rows, weights, act_grad)
    back_grad = exchange(in_grad)
    back_grad, out = lax.optimization_barrier((back_grad, expert_out(act, weights)))
    back_out = exchange(out)
    resid_grad, context_grad = resid_grad_of(dest, back_grad, resid, norm_gain, grad_out, proj)
    query_grad, key_grad, value_grad = attention_grad(
        segment_ids, queries, keys, values, context_grad
    )
    layer_out = layer_out_of(dest, gates, back_out, resid)
    return (
        layer_out,
        resid_grad,
        query_grad,
        key_grad,
        value_grad,
    )


def solution(mesh):
    every = ("dp",) + EXPERT
    split = Mesh(mesh.devices.reshape(mesh.devices.shape[:1] + SPLIT), every)
    rows = P(every, None)
    in_specs = (
        rows,
        rows,
        rows,
        rows,
        P(every),
        P("dp", EXPERT),
        P(),
        P(EXPERT, "dp", None),
        P(EXPERT, "dp", None),
        P(EXPERT, None, "dp"),
        rows,
        rows,
        rows,
    )
    return jax.shard_map(
        local, mesh=split, in_specs=in_specs, out_specs=(rows,) * 5, check_vma=False
    )
```

time: 301 us -> 322 us (1.070)
  Pallas kernels: 0 us -> 51.4 us
  starting transfers between devices: 69.4 us -> 118 us
  local copies, waits for them, and re-layouts: 51.4 us -> 9.07 us
  matrix products: 26 us -> 0.21 us
  between operations: 14.7 us -> 1.06 us
  waiting for transfers between devices: 128 us -> 139 us
  other arithmetic: 9.64 us -> 2.4 us
    ppermute x7 -> x15, waiting for transfers between devices: 0.02 us -> 62.9 us  [the longest x3 42.3 us: ring_experts(): right = lax.ppermute(right, 'dp', behind)]
    all_to_all x5, waiting for transfers between devices: 128 us -> 75.8 us  [spread(): return lax.all_to_all(rows, axes, split_axis=0, concat_axis=0, tiled=True)]
    pallas_call x0 -> x9, Pallas kernels: none -> 51.4 us  [the longest x1 9.02 us: expert_back(): call(expert_kernel, (shape_of(*source.shape), shape_of(slots, hidden)), [...]
    ppermute x7 -> x15, starting transfers between devices: 26.1 us -> 61 us  [the longest x4 27.1 us: gather_pieces(): pieces += [part, lax.ppermute(part, 'core', [(0, 1), (1, 0)])]]
    dot_general x21 -> x1, matrix products: 26 us -> 0.21 us  [slots_of(): before = jnp.dot(earlier, onehot, preferred_element_type=jnp.float32)]
    reshape x11 -> x1, local copies, waits for them, and re-layouts: 23.6 us -> 0.14 us  [slots_of(): flat_ids = expert_ids.reshape(-1)]
    all_to_all x5, starting transfers between devices: 43.3 us -> 57 us  [spread(): return lax.all_to_all(rows, axes, split_axis=0, concat_axis=0, tiled=True)]
    slice x2, local copies, waits for them, and re-layouts: 8.52 us -> 0.05 us  [the longest x1 0.03 us: ring_experts(): slices.append(lax.ppermute(left[:, :half], 'dp', ahead))]
  transfers between devices with their start and end apart: 13 -> 20, of which waited for: 5 -> 10; matrix products, arithmetic and copies ran while one was open for 18% -> 1% of each run, Pallas kernels for 0% -> 12%
where the time goes in v2:
time: 322 us; the launch traced here: 321 us
  waiting for transfers between devices  139 us (43%)
  starting transfers between devices  118 us (37%)
  Pallas kernels  51.4 us (16%)
  local copies, waits for them, and re-layouts  9.07 us (3%)
    all_to_all x5, waiting for transfers between devices, spread(): return lax.all_to_all(rows, axes, split_axis=0, concat_axis=0, tiled=True)  75.8 us
    all_to_all x5, starting transfers between devices, spread(): return lax.all_to_all(rows, axes, split_axis=0, concat_axis=0, tiled=True)  57 us
    ppermute x3, waiting for transfers between devices, ring_experts(): right = lax.ppermute(right, 'dp', behind)  42.3 us
    ppermute x4, starting transfers between devices, gather_pieces(): pieces += [part, lax.ppermute(part, 'core', [(0, 1), (1, 0)])]  27.1 us
    ppermute x3, waiting for transfers between devices, gather_pieces(): lax.ppermute(near, 'x', [(i, (i + k) % xs) for i in range(xs)])  12.1 us
    ppermute x3, starting transfers between devices, ring_experts(): right = lax.ppermute(right, 'dp', behind)  9.74 us
    ppermute x3, starting transfers between devices, gather_pieces(): lax.ppermute(near, 'x', [(i, (i + k) % xs) for i in range(xs)])  9.55 us
    pallas_call x1, Pallas kernels, expert_back(): call(expert_kernel, (shape_of(*source.shape), shape_of(slots, hidden)), [...  9.02 us
  transfers between devices with their start and end apart: 20, of which 10 were waited for; matrix products, arithmetic and copies ran while one was open for 1% of the time, Pallas kernels for 12%

profile of v2, /device:TPU:1, one launch (start us, length us, event | category | flops | bytes accessed | tf_op | source)
XLA Modules:
  0.0 320.8 jit_solution(7297395158680214889)
XLA Ops:
  0.7 1.6 broadcast_in_dim.8
  2.2 17.1 %all-to-all-start = ((bf16[64,32,128]{2,1,0:T(8,128)(2,1)}), bf16[64,32,128]{2,1,0:T(8,128)(2,1)S(1)}, u32[]{:S(2)}, u32[]{:S(2)}) async-start(bf16[64,32,128]{2,1,0:T(8,128)(2,1)} %broadcast_in_dim.8), calls=%async_computation | async-start | bytes 1048576 | tf_op jit(solution)/shard_map/all_to_all | solution.py:411
  19.4 0.1 copy.21
  19.5 0.7 div.10.gate
  20.2 0.1 copy.20
  20.3 0.1 reshape.46
  20.5 0.2 fusion
  20.7 0.6 convert_add_fusion.dest
  21.3 3.5 %shard_map.164 = bf16[6144,128]{1,0:T(8,128)(2,1)} custom-call(s32[256]{0:T(256)} %convert_add_fusion.dest, f32[256]{0:T(256)} %div.10.gate, bf16[128,2048]{1,0:T(8,128)(2,1)} %grad.3), custom_call_target="tpu_custom_call" | custom-call | tf_op jit(solution)/shard_map/pallas_call | solution.py:78
  24.8 12.0 %all-to-all-done = bf16[64,32,128]{2,1,0:T(8,128)(2,1)S(1)} async-done(((bf16[64,32,128]{2,1,0:T(8,128)(2,1)}), bf16[64,32,128]{2,1,0:T(8,128)(2,1)S(1)}, u32[]{:S(2)}, u32[]{:S(2)}) %all-to-all-start) | async-done | bytes 524320 | tf_op jit(solution)/shard_map/all_to_all | solution.py:411
  36.8 10.0 %all-to-all-start.2 = ((bf16[64,96,128]{2,1,0:T(8,128)(2,1)}), bf16[64,96,128]{2,1,0:T(8,128)(2,1)S(1)}, u32[]{:S(2)}, u32[]{:S(2)}) async-start(bf16[64,96,128]{2,1,0:T(8,128)(2,1)} %bitcast.22), calls=%async_computation.2 | async-start | bytes 3145728 | tf_op jit(solution)/shard_map/all_to_all | solution.py:411
  46.8 4.7 %collective-permute-start.5 = (bf16[8,8,32,128]{3,2,1,0:T(8,128)(2,1)S(1)}, bf16[8,8,32,128]{3,2,1,0:T(8,128)(2,1)S(1)}, u32[]{:S(2)}, u32[]{:S(2)}) collective-permute-start(bf16[8,8,32,128]{3,2,1,0:T(8,128)(2,1)S(1)} %bitcast.28), channel_id=1, source_target_pairs={{0,48},{16,0},{32,16},{48,32},{1,49},{17,1},{33,17},{49,33},{2,50}... | collective-permute-start | bytes 1572872 | tf_op jit(solution)/shard_map/ppermute | solution.py:424
  51.5 2.3 collective-permute-start.3
  53.8 2.6 collective-permute-start.1
  56.4 3.1 collective-permute-start
  59.5 11.0 %collective-permute-done.5.refs_6_ = bf16[8,8,32,128]{3,2,1,0:T(8,128)(2,1)S(1)} collective-permute-done((bf16[8,8,32,128]{3,2,1,0:T(8,128)(2,1)S(1)}, bf16[8,8,32,128]{3,2,1,0:T(8,128)(2,1)S(1)}, u32[]{:S(2)}, u32[]{:S(2)}) %collective-permute-start.5) | collective-permute-done | bytes 524320 | tf_op jit(solution)/shard_map/ppermute | solution.py:424
  70.5 19.6 %collective-permute-start.6 = (bf16[8,8,32,128]{3,2,1,0:T(8,128)(2,1)S(1)}, bf16[8,8,32,128]{3,2,1,0:T(8,128)(2,1)}, u32[]{:S(2)}, u32[]{:S(2)}) collective-permute-start(bf16[8,8,32,128]{3,2,1,0:T(8,128)(2,1)S(1)} %collective-permute-done.5.refs_6_), channel_id=1, source_target_pairs={{0,1},{1,0},{2,3},{3,2},{4,5},{5,4},{6,7},{7,6},{8,9},{9,8},{10,11... | collective-permute-start | bytes 1572872 | tf_op jit(solution)/shard_map/ppermute | solution.py:429
  90.2 0.0 collective-permute-done.3.refs_4_
  90.2 0.0 copy-start.13
  90.2 1.9 collective-permute-start.4
  92.1 1.1 collective-permute-done.1.refs_2_
  93.2 2.4 collective-permute-start.2
  95.6 0.7 copy.22.seg_col
  96.4 4.6 %shard_map.165.refs_8_ = bf16[128,1024]{1,0:T(8,128)(2,1)} custom-call(s32[1,128]{1,0:T(1,128)} %bitcast.38, s32[128,1]{1,0:T(8,128)} %copy.22.seg_col, bf16[128,1024]{1,0:T(8,128)(2,1)} %queries.3, bf16[128,1024]{1,0:T(8,128)(2,1)} %keys.3, bf16[128,1024]{1,0:T(8,128)(2,1)} %values.3), custom_call_target="tpu_custom_call" | custom-call | tf_op jit(solution)/shard_map/pallas_call | solution.py:373
  100.9 0.7 pad_add_fusion.place
  101.6 0.0 collective-permute-done.refs_1_
  101.6 0.0 collective-permute-done.6.refs_7_
  101.6 0.0 collective-permute-done.4.refs_5_
  101.6 0.0 collective-permute-done.2.refs_3_
  101.6 8.7 %shard_map.166 = (bf16[2048,1024]{1,0:T(8,128)(2,1)}, bf16[128,2048]{1,0:T(8,128)(2,1)}, bf16[6144,128]{1,0:T(8,128)(2,1)}) custom-call(s32[256]{0:T(256)} %convert_add_fusion.dest, s32[3]{0:T(128)} %pad_add_fusion.place, bf16[8,8,32,128]{3,2,1,0:T(8,128)(2,1)} %bitcast.32, bf16[8,8,32,128]{3,2,1,0:T(8,128)(2,1)} %collective-permute-done.refs_1_, ...), custom_call_target="tpu_custom_call" | custom-call | tf_op jit(solution)/shard_map/pallas_call | solution.py:137
  110.3 0.0 copy-start.15
  110.3 1.2 copy-done.3
  111.5 9.4 %all-to-all-start.1 = ((bf16[64,96,128]{2,1,0:T(8,128)(2,1)}), bf16[64,96,128]{2,1,0:T(8,128)(2,1)S(1)}, u32[]{:S(2)}, u32[]{:S(2)}) async-start(bf16[64,96,128]{2,1,0:T(8,128)(2,1)} %bitcast.33), calls=%async_computation.1 | async-start | bytes 3145728 | tf_op jit(solution)/shard_map/all_to_all | solution.py:411
  121.0 1.1 pad_maximum_fusion.refs_0_
  122.1 2.0 collective-permute-start.8
  124.2 3.2 %collective-permute-start.7 = (bf16[3,256,512]{2,1,0:T(8,128)(2,1)S(1)}, bf16[3,256,512]{2,1,0:T(8,128)(2,1)S(1)}, u32[]{:S(2)}, u32[]{:S(2)}) collective-permute-start(bf16[3,256,512]{2,1,0:T(8,128)(2,1)S(1)} %pad_maximum_fusion.refs_0_), channel_id=1, source_target_pairs={{0,64},{64,128},{128,192},{192,256},{256,320},{320,384},{384,448},... | collective-permute-start | bytes 2359304 | tf_op jit(solution)/shard_map/ppermute | solution.py:446
  127.4 15.2 %collective-permute-done.8.refs_2_ = bf16[3,256,512]{2,1,0:T(8,128)(2,1)S(1)} collective-permute-done((bf16[3,256,512]{2,1,0:T(8,128)(2,1)S(1)}, bf16[3,256,512]{2,1,0:T(8,128)(2,1)S(1)}, u32[]{:S(2)}, u32[]{:S(2)}) %collective-permute-start.8) | collective-permute-done | bytes 786464 | tf_op jit(solution)/shard_map/ppermute | solution.py:447
  142.6 3.2 %collective-permute-start.10 = (bf16[3,256,512]{2,1,0:T(8,128)(2,1)S(1)}, bf16[3,256,512]{2,1,0:T(8,128)(2,1)S(1)}, u32[]{:S(2)}, u32[]{:S(2)}) collective-permute-start(bf16[3,256,512]{2,1,0:T(8,128)(2,1)S(1)} %collective-permute-done.8.refs_2_), channel_id=1, source_target_pairs={{0,448},{64,0},{128,64},{192,128},{256,192},{320,256},{384,320},{4... | collective-permute-start | bytes 2359304 | tf_op jit(solution)/shard_map/ppermute | solution.py:447
  145.9 0.0 collective-permute-done.7.refs_1_
  145.9 2.0 collective-permute-start.9
  148.0 14.4 %collective-permute-done.10.refs_4_ = bf16[3,256,512]{2,1,0:T(8,128)(2,1)S(1)} collective-permute-done((bf16[3,256,512]{2,1,0:T(8,128)(2,1)S(1)}, bf16[3,256,512]{2,1,0:T(8,128)(2,1)S(1)}, u32[]{:S(2)}, u32[]{:S(2)}) %collective-permute-start.10) | collective-permute-done | bytes 786464 | tf_op jit(solution)/shard_map/ppermute | solution.py:447
  162.3 4.5 %collective-permute-start.12 = (bf16[3,256,512]{2,1,0:T(8,128)(2,1)S(1)}, bf16[3,256,512]{2,1,0:T(8,128)(2,1)S(1)}, u32[]{:S(2)}, u32[]{:S(2)}) collective-permute-start(bf16[3,256,512]{2,1,0:T(8,128)(2,1)S(1)} %collective-permute-done.10.refs_4_), channel_id=1, source_target_pairs={{0,448},{64,0},{128,64},{192,128},{256,192},{320,256},{384,320},{4... | collective-permute-start | bytes 2359304 | tf_op jit(solution)/shard_map/ppermute | solution.py:447
  166.8 0.0 collective-permute-done.9.refs_3_
  166.8 1.9 collective-permute-start.11
  168.7 12.7 %collective-permute-done.12.refs_6_ = bf16[3,256,512]{2,1,0:T(8,128)(2,1)S(1)} collective-permute-done((bf16[3,256,512]{2,1,0:T(8,128)(2,1)S(1)}, bf16[3,256,512]{2,1,0:T(8,128)(2,1)S(1)}, u32[]{:S(2)}, u32[]{:S(2)}) %collective-permute-start.12) | collective-permute-done | bytes 786464 | tf_op jit(solution)/shard_map/ppermute | solution.py:447
  181.5 5.3 %collective-permute-start.14 = (bf16[3,128,512]{2,1,0:T(8,128)(2,1)S(1)}, bf16[3,128,512]{2,1,0:T(8,128)(2,1)S(1)}, u32[]{:S(2)}, u32[]{:S(2)}) collective-permute-start(bf16[3,128,512]{2,1,0:T(8,128)(2,1)S(1)} %slice.17), channel_id=1, source_target_pairs={{0,448},{64,0},{128,64},{192,128},{256,192},{320,256},{384,320},{4... | collective-permute-start | bytes 1179656 | tf_op jit(solution)/shard_map/ppermute | solution.py:450
  186.9 0.9 copy-done.7
  187.8 2.1 collective-permute-start.13
  189.9 2.4 collective-permute-done.14.refs_8_
  192.3 6.1 %collective-permute-done.13.refs_7_ = bf16[3,128,512]{2,1,0:T(8,128)(2,1)} collective-permute-done((bf16[3,128,512]{2,1,0:T(8,128)(2,1)S(1)}, bf16[3,128,512]{2,1,0:T(8,128)(2,1)}, u32[]{:S(2)}, u32[]{:S(2)}) %collective-permute-start.13) | collective-permute-done | bytes 393248 | tf_op jit(solution)/shard_map/ppermute | solution.py:449
  198.4 6.5 %shard_map.167 = (f32[384,512]{1,0:T(8,128)}, bf16[8,3,256,512]{3,2,1,0:T(8,128)(2,1)}) custom-call(s32[3]{0:T(128)} %pad_add_fusion.place, bf16[6144,128]{1,0:T(8,128)(2,1)} %bitcast.26, bf16[3,256,512]{2,1,0:T(8,128)(2,1)} %copy-done.4, bf16[3,256,512]{2,1,0:T(8,128)(2,1)} %copy-done.9, bf16[3,256,512]{2,1,0:T(8,128)(2,1)} %copy-done.8, ...), custom_call_target="tpu_custom_call" | custom-call | tf_op jit(solution)/shard_map/pallas_call | solution.py:199
  204.9 0.0 all-to-all-done.1
  204.9 1.2 copy-done
  206.1 9.0 %shard_map.168 = (bf16[6144,128]{1,0:T(8,128)(2,1)}, bf16[384,512]{1,0:T(8,128)(2,1)}) custom-call(bf16[6144,128]{1,0:T(8,128)(2,1)} %bitcast.23, bf16[8,3,256,512]{3,2,1,0:T(8,128)(2,1)} %get-tuple-element.24.gate_w.up_w.down, bf16[8,3,256,512]{3,2,1,0:T(8,128)(2,1)} %get-tuple-element.24.gate_w.up_w.down, f32[384,512]{1,0:T(8,128)} %get-tuple-element.25.act_grad), custom_call_target="tpu_custom_call" | custom-call | tf_op jit(solution)/shard_map/pallas_call | solution.py:240
  215.1 14.3 %all-to-all-start.3 = ((bf16[64,96,128]{2,1,0:T(8,128)(2,1)}), bf16[64,96,128]{2,1,0:T(8,128)(2,1)S(1)}, u32[]{:S(2)}, u32[]{:S(2)}) async-start(bf16[64,96,128]{2,1,0:T(8,128)(2,1)} %bitcast.34), calls=%async_computation.3 | async-start | bytes 3145728 | tf_op jit(solution)/shard_map/all_to_all | solution.py:411
  229.4 4.4 %shard_map.169 = bf16[6144,128]{1,0:T(8,128)(2,1)} custom-call(bf16[384,512]{1,0:T(8,128)(2,1)} %get-tuple-element.27.act, bf16[8,3,256,512]{3,2,1,0:T(8,128)(2,1)} %get-tuple-element.24.gate_w.up_w.down), custom_call_target="tpu_custom_call" | custom-call | tf_op jit(solution)/shard_map/pallas_call | solution.py:267
  233.9 35.3 %all-to-all-done.3 = bf16[64,96,128]{2,1,0:T(8,128)(2,1)S(1)} async-done(((bf16[64,96,128]{2,1,0:T(8,128)(2,1)}), bf16[64,96,128]{2,1,0:T(8,128)(2,1)S(1)}, u32[]{:S(2)}, u32[]{:S(2)}) %all-to-all-start.3) | async-done | bytes 1572896 | tf_op jit(solution)/shard_map/all_to_all | solution.py:411
  269.2 1.2 copy-done.2
  270.4 6.1 %all-to-all-start.4 = ((bf16[64,96,128]{2,1,0:T(8,128)(2,1)}), bf16[64,96,128]{2,1,0:T(8,128)(2,1)S(1)}, u32[]{:S(2)}, u32[]{:S(2)}) async-start(bf16[64,96,128]{2,1,0:T(8,128)(2,1)} %bitcast.27), calls=%async_computation.4 | async-start | bytes 3145728 | tf_op jit(solution)/shard_map/all_to_all | solution.py:411
  276.5 5.6 %shard_map.171 = (bf16[128,2048]{1,0:T(8,128)(2,1)}, bf16[128,1024]{1,0:T(8,128)(2,1)}) custom-call(s32[256]{0:T(256)} %convert_add_fusion.dest, bf16[6144,128]{1,0:T(8,128)(2,1)} %bitcast.25, bf16[128,2048]{1,0:T(8,128)(2,1)} %get-tuple-element.29.resid, f32[1,2048]{1,0:T(1,128)} %bitcast.36, bf16[128,2048]{1,0:T(8,128)(2,1)} %grad.3, ...), custom_call_target="tpu_custom_call" | custom-call | tf_op jit(solution)/shard_map/pallas_call | solution.py:307
  282.0 5.8 %shard_map.172 = (bf16[128,1024]{1,0:T(8,128)(2,1)}, bf16[128,1024]{1,0:T(8,128)(2,1)}, bf16[128,1024]{1,0:T(8,128)(2,1)}) custom-call(s32[1,128]{1,0:T(1,128)} %bitcast.39, s32[128,1]{1,0:T(8,128)} %copy.22.seg_col, bf16[128,1024]{1,0:T(8,128)(2,1)} %queries.3, bf16[128,1024]{1,0:T(8,128)(2,1)} %keys.3, bf16[128,1024]{1,0:T(8,128)(2,1)} %values.3, ...), custom_call_target="tpu_custom_call" | custom-call | tf_op jit(solution)/shard_map/pallas_call | solution.py:405
  287.8 28.4 %all-to-all-done.4 = bf16[64,96,128]{2,1,0:T(8,128)(2,1)S(1)} async-done(((bf16[64,96,128]{2,1,0:T(8,128)(2,1)}), bf16[64,96,128]{2,1,0:T(8,128)(2,1)S(1)}, u32[]{:S(2)}, u32[]{:S(2)}) %all-to-all-start.4) | async-done | bytes 1572896 | tf_op jit(solution)/shard_map/all_to_all | solution.py:411
  316.2 1.2 copy-done.1
  317.4 3.4 %shard_map.170 = bf16[128,2048]{1,0:T(8,128)(2,1)} custom-call(s32[256]{0:T(256)} %convert_add_fusion.dest, f32[256]{0:T(256)} %div.10.gate, bf16[6144,128]{1,0:T(8,128)(2,1)} %bitcast.24, bf16[128,2048]{1,0:T(8,128)(2,1)} %get-tuple-element.29.resid), custom_call_target="tpu_custom_call" | custom-call | tf_op jit(solution)/shard_map/pallas_call | solution.py:339
  (38 shorter events, 0.2 us)
Async XLA Ops:
  0.6 18.7 %copy-start.18 = (s32[128,2]{0,1:T(2,128)S(1)}, s32[128,2]{0,1:T(2,128)}, u32[]{:S(2)}) copy-start(s32[128,2]{0,1:T(2,128)} %param.24) | copy-start | bytes 3076
  0.6 19.6 %copy-start.17 = (s32[128,2]{0,1:T(2,128)S(1)}, s32[128,2]{0,1:T(2,128)}, u32[]{:S(2)}) copy-start(s32[128,2]{0,1:T(2,128)} %param.23) | copy-start | bytes 3076
  2.2 34.6 %all-to-all-start = ((bf16[64,32,128]{2,1,0:T(8,128)(2,1)}), bf16[64,32,128]{2,1,0:T(8,128)(2,1)S(1)}, u32[]{:S(2)}, u32[]{:S(2)}) async-start(bf16[64,32,128]{2,1,0:T(8,128)(2,1)} %broadcast_in_dim.8), calls=%async_computation | async-start | bytes 1048576 | tf_op jit(solution)/shard_map/all_to_all | solution.py:411
  36.8 19.6 %copy-start.5 = (bf16[64,32,128]{2,1,0:T(8,128)(2,1)}, bf16[64,32,128]{2,1,0:T(8,128)(2,1)S(1)}, u32[]{:S(2)}) copy-start(bf16[64,32,128]{2,1,0:T(8,128)(2,1)S(1)} %all-to-all-done) | copy-start | bytes 1572868
  36.8 58.9 %copy-start.16 = (s32[128]{0:T(128)S(1)}, s32[128]{0:T(128)}, u32[]{:S(2)}) copy-start(s32[128]{0:T(128)} %param.17) | copy-start | bytes 1540
  36.8 73.5 %all-to-all-start.2 = ((bf16[64,96,128]{2,1,0:T(8,128)(2,1)}), bf16[64,96,128]{2,1,0:T(8,128)(2,1)S(1)}, u32[]{:S(2)}, u32[]{:S(2)}) async-start(bf16[64,96,128]{2,1,0:T(8,128)(2,1)} %bitcast.22), calls=%async_computation.2 | async-start | bytes 3145728 | tf_op jit(solution)/shard_map/all_to_all | solution.py:411
  46.8 23.7 %collective-permute-start.5 = (bf16[8,8,32,128]{3,2,1,0:T(8,128)(2,1)S(1)}, bf16[8,8,32,128]{3,2,1,0:T(8,128)(2,1)S(1)}, u32[]{:S(2)}, u32[]{:S(2)}) collective-permute-start(bf16[8,8,32,128]{3,2,1,0:T(8,128)(2,1)S(1)} %bitcast.28), channel_id=1, source_target_pairs={{0,48},{16,0},{32,16},{48,32},{1,49},{17,1},{33,17},{49,33},{2,50}... | collective-permute-start | bytes 1572872 | tf_op jit(solution)/shard_map/ppermute | solution.py:424
  51.5 38.7 %collective-permute-start.3 = (bf16[8,8,32,128]{3,2,1,0:T(8,128)(2,1)S(1)}, bf16[8,8,32,128]{3,2,1,0:T(8,128)(2,1)S(1)}, u32[]{:S(2)}, u32[]{:S(2)}) collective-permute-start(bf16[8,8,32,128]{3,2,1,0:T(8,128)(2,1)S(1)} %bitcast.29), channel_id=1, source_target_pairs={{0,32},{16,48},{32,0},{48,16},{1,33},{17,49},{33,1},{49,17},{2,34}... | collective-permute-start | bytes 1572872 | tf_op jit(solution)/shard_map/ppermute | solution.py:424
  53.8 39.4 %collective-permute-start.1 = (bf16[8,8,32,128]{3,2,1,0:T(8,128)(2,1)S(1)}, bf16[8,8,32,128]{3,2,1,0:T(8,128)(2,1)}, u32[]{:S(2)}, u32[]{:S(2)}) collective-permute-start(bf16[8,8,32,128]{3,2,1,0:T(8,128)(2,1)S(1)} %bitcast.30), channel_id=1, source_target_pairs={{0,16},{16,32},{32,48},{48,0},{1,17},{17,33},{33,49},{49,1},{2,18}... | collective-permute-start | bytes 1572872 | tf_op jit(solution)/shard_map/ppermute | solution.py:424
  56.4 45.2 %collective-permute-start = (bf16[8,8,32,128]{3,2,1,0:T(8,128)(2,1)S(1)}, bf16[8,8,32,128]{3,2,1,0:T(8,128)(2,1)}, u32[]{:S(2)}, u32[]{:S(2)}) collective-permute-start(bf16[8,8,32,128]{3,2,1,0:T(8,128)(2,1)S(1)} %bitcast.31), channel_id=1, source_target_pairs={{0,1},{1,0},{2,3},{3,2},{4,5},{5,4},{6,7},{7,6},{8,9},{9,8},{10,11... | collective-permute-start | bytes 1572872 | tf_op jit(solution)/shard_map/ppermute | solution.py:429
  70.5 31.1 %copy-start.12 = (bf16[8,8,32,128]{3,2,1,0:T(8,128)(2,1)}, bf16[8,8,32,128]{3,2,1,0:T(8,128)(2,1)S(1)}, u32[]{:S(2)}) copy-start(bf16[8,8,32,128]{3,2,1,0:T(8,128)(2,1)S(1)} %collective-permute-done.5.refs_6_) | copy-start | bytes 1572868
  70.5 31.0 %collective-permute-start.6 = (bf16[8,8,32,128]{3,2,1,0:T(8,128)(2,1)S(1)}, bf16[8,8,32,128]{3,2,1,0:T(8,128)(2,1)}, u32[]{:S(2)}, u32[]{:S(2)}) collective-permute-start(bf16[8,8,32,128]{3,2,1,0:T(8,128)(2,1)S(1)} %collective-permute-done.5.refs_6_), channel_id=1, source_target_pairs={{0,1},{1,0},{2,3},{3,2},{4,5},{5,4},{6,7},{7,6},{8,9},{9,8},{10,11... | collective-permute-start | bytes 1572872 | tf_op jit(solution)/shard_map/ppermute | solution.py:429
  90.2 11.4 %copy-start.13 = (bf16[8,8,32,128]{3,2,1,0:T(8,128)(2,1)}, bf16[8,8,32,128]{3,2,1,0:T(8,128)(2,1)S(1)}, u32[]{:S(2)}) copy-start(bf16[8,8,32,128]{3,2,1,0:T(8,128)(2,1)S(1)} %collective-permute-done.3.refs_4_) | copy-start | bytes 1572868
  90.2 11.4 %collective-permute-start.4 = (bf16[8,8,32,128]{3,2,1,0:T(8,128)(2,1)S(1)}, bf16[8,8,32,128]{3,2,1,0:T(8,128)(2,1)}, u32[]{:S(2)}, u32[]{:S(2)}) collective-permute-start(bf16[8,8,32,128]{3,2,1,0:T(8,128)(2,1)S(1)} %collective-permute-done.3.refs_4_), channel_id=1, source_target_pairs={{0,1},{1,0},{2,3},{3,2},{4,5},{5,4},{6,7},{7,6},{8,9},{9,8},{10,11... | collective-permute-start | bytes 1572872 | tf_op jit(solution)/shard_map/ppermute | solution.py:429
  93.2 8.4 %collective-permute-start.2 = (bf16[8,8,32,128]{3,2,1,0:T(8,128)(2,1)}, bf16[8,8,32,128]{3,2,1,0:T(8,128)(2,1)}, u32[]{:S(2)}, u32[]{:S(2)}) collective-permute-start(bf16[8,8,32,128]{3,2,1,0:T(8,128)(2,1)} %collective-permute-done.1.refs_2_), channel_id=1, source_target_pairs={{0,1},{1,0},{2,3},{3,2},{4,5},{5,4},{6,7},{7,6},{8,9},{9,8},{10,11... | collective-permute-start | bytes 1572872 | tf_op jit(solution)/shard_map/ppermute | solution.py:429
  110.3 1.2 copy-start.3
  110.3 10.6 %copy-start.15 = (bf16[1,512,256]{2,1,0:T(8,128)(2,1)S(1)}, bf16[1,512,256]{2,1,0:T(8,128)(2,1)}, u32[]{:S(2)}) copy-start(bf16[1,512,256]{2,1,0:T(8,128)(2,1)} %param.22) | copy-start | bytes 786436
  111.5 93.5 %all-to-all-start.1 = ((bf16[64,96,128]{2,1,0:T(8,128)(2,1)}), bf16[64,96,128]{2,1,0:T(8,128)(2,1)S(1)}, u32[]{:S(2)}, u32[]{:S(2)}) async-start(bf16[64,96,128]{2,1,0:T(8,128)(2,1)} %bitcast.33), calls=%async_computation.1 | async-start | bytes 3145728 | tf_op jit(solution)/shard_map/all_to_all | solution.py:411
  122.1 76.3 %copy-start.4 = (bf16[3,256,512]{2,1,0:T(8,128)(2,1)}, bf16[3,256,512]{2,1,0:T(8,128)(2,1)S(1)}, u32[]{:S(2)}) copy-start(bf16[3,256,512]{2,1,0:T(8,128)(2,1)S(1)} %pad_maximum_fusion.refs_0_) | copy-start | bytes 2359300
  122.1 20.5 %collective-permute-start.8 = (bf16[3,256,512]{2,1,0:T(8,128)(2,1)S(1)}, bf16[3,256,512]{2,1,0:T(8,128)(2,1)S(1)}, u32[]{:S(2)}, u32[]{:S(2)}) collective-permute-start(bf16[3,256,512]{2,1,0:T(8,128)(2,1)S(1)} %pad_maximum_fusion.refs_0_), channel_id=1, source_target_pairs={{0,448},{64,0},{128,64},{192,128},{256,192},{320,256},{384,320},{4... | collective-permute-start | bytes 2359304 | tf_op jit(solution)/shard_map/ppermute | solution.py:447
  124.2 21.7 %collective-permute-start.7 = (bf16[3,256,512]{2,1,0:T(8,128)(2,1)S(1)}, bf16[3,256,512]{2,1,0:T(8,128)(2,1)S(1)}, u32[]{:S(2)}, u32[]{:S(2)}) collective-permute-start(bf16[3,256,512]{2,1,0:T(8,128)(2,1)S(1)} %pad_maximum_fusion.refs_0_), channel_id=1, source_target_pairs={{0,64},{64,128},{128,192},{192,256},{256,320},{320,384},{384,448},... | collective-permute-start | bytes 2359304 | tf_op jit(solution)/shard_map/ppermute | solution.py:446
  142.6 5.3 %copy-start.8 = (bf16[3,256,512]{2,1,0:T(8,128)(2,1)}, bf16[3,256,512]{2,1,0:T(8,128)(2,1)S(1)}, u32[]{:S(2)}) copy-start(bf16[3,256,512]{2,1,0:T(8,128)(2,1)S(1)} %collective-permute-done.8.refs_2_) | copy-start | bytes 2359300
  142.6 19.7 %collective-permute-start.10 = (bf16[3,256,512]{2,1,0:T(8,128)(2,1)S(1)}, bf16[3,256,512]{2,1,0:T(8,128)(2,1)S(1)}, u32[]{:S(2)}, u32[]{:S(2)}) collective-permute-start(bf16[3,256,512]{2,1,0:T(8,128)(2,1)S(1)} %collective-permute-done.8.refs_2_), channel_id=1, source_target_pairs={{0,448},{64,0},{128,64},{192,128},{256,192},{320,256},{384,320},{4... | collective-permute-start | bytes 2359304 | tf_op jit(solution)/shard_map/ppermute | solution.py:447
  145.9 20.9 %copy-start.9 = (bf16[3,256,512]{2,1,0:T(8,128)(2,1)}, bf16[3,256,512]{2,1,0:T(8,128)(2,1)S(1)}, u32[]{:S(2)}) copy-start(bf16[3,256,512]{2,1,0:T(8,128)(2,1)S(1)} %collective-permute-done.7.refs_1_) | copy-start | bytes 2359300
  145.9 20.9 %collective-permute-start.9 = (bf16[3,256,512]{2,1,0:T(8,128)(2,1)S(1)}, bf16[3,256,512]{2,1,0:T(8,128)(2,1)S(1)}, u32[]{:S(2)}, u32[]{:S(2)}) collective-permute-start(bf16[3,256,512]{2,1,0:T(8,128)(2,1)S(1)} %collective-permute-done.7.refs_1_), channel_id=1, source_target_pairs={{0,64},{64,128},{128,192},{192,256},{256,320},{320,384},{384,448},... | collective-permute-start | bytes 2359304 | tf_op jit(solution)/shard_map/ppermute | solution.py:446
  162.3 6.4 %copy-start.10 = (bf16[3,256,512]{2,1,0:T(8,128)(2,1)}, bf16[3,256,512]{2,1,0:T(8,128)(2,1)S(1)}, u32[]{:S(2)}) copy-start(bf16[3,256,512]{2,1,0:T(8,128)(2,1)S(1)} %collective-permute-done.10.refs_4_) | copy-start | bytes 2359300
  162.3 19.2 %collective-permute-start.12 = (bf16[3,256,512]{2,1,0:T(8,128)(2,1)S(1)}, bf16[3,256,512]{2,1,0:T(8,128)(2,1)S(1)}, u32[]{:S(2)}, u32[]{:S(2)}) collective-permute-start(bf16[3,256,512]{2,1,0:T(8,128)(2,1)S(1)} %collective-permute-done.10.refs_4_), channel_id=1, source_target_pairs={{0,448},{64,0},{128,64},{192,128},{256,192},{320,256},{384,320},{4... | collective-permute-start | bytes 2359304 | tf_op jit(solution)/shard_map/ppermute | solution.py:447
  166.8 21.0 %copy-start.11 = (bf16[3,256,512]{2,1,0:T(8,128)(2,1)}, bf16[3,256,512]{2,1,0:T(8,128)(2,1)S(1)}, u32[]{:S(2)}) copy-start(bf16[3,256,512]{2,1,0:T(8,128)(2,1)S(1)} %collective-permute-done.9.refs_3_) | copy-start | bytes 2359300
  166.8 20.0 %collective-permute-start.11 = (bf16[3,256,512]{2,1,0:T(8,128)(2,1)S(1)}, bf16[3,256,512]{2,1,0:T(8,128)(2,1)S(1)}, u32[]{:S(2)}, u32[]{:S(2)}) collective-permute-start(bf16[3,256,512]{2,1,0:T(8,128)(2,1)S(1)} %collective-permute-done.9.refs_3_), channel_id=1, source_target_pairs={{0,64},{64,128},{128,192},{192,256},{256,320},{320,384},{384,448},... | collective-permute-start | bytes 2359304 | tf_op jit(solution)/shard_map/ppermute | solution.py:446
  181.5 16.9 %copy-start.6 = (bf16[3,256,512]{2,1,0:T(8,128)(2,1)}, bf16[3,256,512]{2,1,0:T(8,128)(2,1)S(1)}, u32[]{:S(2)}) copy-start(bf16[3,256,512]{2,1,0:T(8,128)(2,1)S(1)} %collective-permute-done.12.refs_6_) | copy-start | bytes 2359300
  181.5 10.8 %collective-permute-start.14 = (bf16[3,128,512]{2,1,0:T(8,128)(2,1)S(1)}, bf16[3,128,512]{2,1,0:T(8,128)(2,1)S(1)}, u32[]{:S(2)}, u32[]{:S(2)}) collective-permute-start(bf16[3,128,512]{2,1,0:T(8,128)(2,1)S(1)} %slice.17), channel_id=1, source_target_pairs={{0,448},{64,0},{128,64},{192,128},{256,192},{320,256},{384,320},{4... | collective-permute-start | bytes 1179656 | tf_op jit(solution)/shard_map/ppermute | solution.py:450
  186.9 0.9 copy-start.7
  187.8 10.6 %collective-permute-start.13 = (bf16[3,128,512]{2,1,0:T(8,128)(2,1)S(1)}, bf16[3,128,512]{2,1,0:T(8,128)(2,1)}, u32[]{:S(2)}, u32[]{:S(2)}) collective-permute-start(bf16[3,128,512]{2,1,0:T(8,128)(2,1)S(1)} %slice.16), channel_id=1, source_target_pairs={{0,64},{64,128},{128,192},{192,256},{256,320},{320,384},{384,448},... | collective-permute-start | bytes 1179656 | tf_op jit(solution)/shard_map/ppermute | solution.py:449
  192.3 6.1 %copy-start.14 = (bf16[3,128,512]{2,1,0:T(8,128)(2,1)}, bf16[3,128,512]{2,1,0:T(8,128)(2,1)S(1)}, u32[]{:S(2)}) copy-start(bf16[3,128,512]{2,1,0:T(8,128)(2,1)S(1)} %collective-permute-done.14.refs_8_) | copy-start | bytes 1179652
  204.9 1.2 copy-start
  215.1 54.1 %all-to-all-start.3 = ((bf16[64,96,128]{2,1,0:T(8,128)(2,1)}), bf16[64,96,128]{2,1,0:T(8,128)(2,1)S(1)}, u32[]{:S(2)}, u32[]{:S(2)}) async-start(bf16[64,96,128]{2,1,0:T(8,128)(2,1)} %bitcast.34), calls=%async_computation.3 | async-start | bytes 3145728 | tf_op jit(solution)/shard_map/all_to_all | solution.py:411
  269.2 1.2 copy-start.2
  270.4 45.9 %all-to-all-start.4 = ((bf16[64,96,128]{2,1,0:T(8,128)(2,1)}), bf16[64,96,128]{2,1,0:T(8,128)(2,1)S(1)}, u32[]{:S(2)}, u32[]{:S(2)}) async-start(bf16[64,96,128]{2,1,0:T(8,128)(2,1)} %bitcast.27), calls=%async_computation.4 | async-start | bytes 3145728 | tf_op jit(solution)/shard_map/all_to_all | solution.py:411
  316.2 1.2 copy-start.1

commit v3 on v2

--- a/solution.py
+++ b/solution.py
@@ -1,3 +1,5 @@
+import functools
+
 import jax
 import jax.numpy as jnp
 from jax import lax
@@ -10,6 +12,7 @@
 EXPERT = ("x", "y", "core")
 SPLIT = (4, 8, 2)
 LANES = 128
+VMEM_LIMIT = 24 << 20
 
 
 epsilon = 1e-06
@@ -27,11 +30,11 @@
 def call(body, outs, scratch, specs):
     return pl.pallas_call(
         body,
-        grid=(1,),
         out_shape=outs,
         in_specs=specs,
         out_specs=jax.tree.map(lambda _: VMEM, outs),
         scratch_shapes=scratch,
+        compiler_params=pltpu.CompilerParams(vmem_limit_bytes=VMEM_LIMIT),
     )
 
 
@@ -83,33 +86,52 @@
     )(dest, gate, grad)
 
 
-def resid_kernel(dest, place, *refs):
-    pieces, (context, hidden, gain, proj, resid, out, tiled, normed) = refs[:8], refs[8:]
+def slab_kernel(near, *refs):
+    pairs, outs, slab = refs[:4], refs[4:8], refs[8]
+    heads, ys, cols, depth = near.shape
+    for y in range(ys):
+        for h in range(heads):
+            slab[y * cols : (y + 1) * cols, h * depth : (h + 1) * depth] = near[h, y]
+    for pair, out in zip(pairs, outs):
+        for n in range(2):
+            out[n] = contract_last(pair[n], slab[...]).astype(jnp.bfloat16)
+
+
+def slab_products(near, contexts):
+    heads, ys, cols, depth = near.shape
+    tok = contexts[0].shape[1]
+    out = jax.ShapeDtypeStruct((2, tok, ys * cols), jnp.bfloat16)
+    return call(
+        slab_kernel,
+        (out,) * len(contexts),
+        [pltpu.VMEM((ys * cols, heads * depth), jnp.bfloat16)],
+        [VMEM] * (1 + len(contexts)),
+    )(near, *contexts)
+
+
+def spread_matrix(core, rows, cols):
+    source = lax.broadcasted_iota(jnp.int32, (rows, 2 * rows), 0)
+    target = lax.broadcasted_iota(jnp.int32, (rows, 2 * rows), 1)
+    at = source + (source // cols) * cols + core * cols
+    return jnp.where(target == at, 1.0, 0.0).astype(jnp.bfloat16)
+
+
+def resid_kernel(cols, dest, place, *refs):
+    mine, (other, hidden, gain, resid, out, tiled, normed) = refs[:4], refs[4:]
     tok, width = hidden.shape
     parts = width // LANES
-    heads, ys, cols, depth = pieces[0].shape
-    xs = len(pieces) // 2
-
-    def fill(y, carry):
-        for k in range(xs):
-            x = lax.rem(place[0] + xs - k, xs)
-            for which in range(2):
-                core = place[1] if which == 0 else 1 - place[1]
-                at = pl.multiple_of(((x * ys + y) * 2 + core) * cols, cols)
-                for h in range(heads):
-                    proj[pl.ds(at, cols), h * depth : (h + 1) * depth] = pieces[
-                        2 * k + which
-                    ][h, y]
-        return carry
-
-    lax.fori_loop(0, ys, fill, 0)
-    chunk = 512
+    xs = len(mine)
+    span = width // xs
+    put_mine = spread_matrix(place[1], span // 2, cols)
+    put_other = spread_matrix(1 - place[1], span // 2, cols)
     total = jnp.zeros((tok, 1), jnp.float32)
-    for n in range(0, width, chunk):
-        some = slice(n, n + chunk)
-        row = hidden[:, some].astype(jnp.float32) + contract_last(context[...], proj[some, :])
-        row = row.astype(jnp.bfloat16)
-        resid[:, some] = row
+    for k in range(xs):
+        at = pl.multiple_of(lax.rem(place[0] + k, xs) * span, span)
+        row = jnp.dot(mine[k][0], put_mine, preferred_element_type=jnp.float32) + jnp.dot(
+            other[k], put_other, preferred_element_type=jnp.float32
+        )
+        row = (hidden[:, pl.ds(at, span)].astype(jnp.float32) + row).astype(jnp.bfloat16)
+        resid[:, pl.ds(at, span)] = row
         row = row.astype(jnp.float32)
         total = total + jnp.sum(row * row, axis=-1, keepdims=True)
     inv_rms = lax.rsqrt(total / width + epsilon)
@@ -131,22 +153,18 @@
     lax.fori_loop(0, tok, step, 0, unroll=8)
 
 
-def make_resid(dest, place, pieces, context, hidden, gain, slots):
+def make_resid(dest, place, mine, other, hidden, gain, slots, cols):
     tok, width = hidden.shape
     parts = width // LANES
     return call(
-        resid_kernel,
-        (
-            shape_of(width, context.shape[1]),
-            shape_of(tok, width),
-            shape_of(slots * parts, LANES),
-        ),
+        functools.partial(resid_kernel, cols),
+        (shape_of(tok, width), shape_of(slots * parts, LANES)),
         [
             pltpu.VMEM((tok * parts, LANES), jnp.float32),
             pltpu.VMEM((tok * parts, LANES), jnp.bfloat16),
         ],
-        [SMEM, SMEM] + [VMEM] * (len(pieces) + 3),
-    )(dest, place, *pieces, context, hidden, gain[None])
+        [SMEM, SMEM] + [VMEM] * (len(mine) + 3),
+    )(dest, place, *mine, other, hidden, gain[None])
 
 
 def load_rows(source, tiled, rows):
@@ -161,46 +179,43 @@
 
 
 def act_grad_kernel(place, source, *refs):
-    pieces, (out, weights, tiled, rows) = refs[:-4], refs[-4:]
-    count, depth = weights.shape[0], weights.shape[2]
+    pieces, (out, gate_w, up_w, down_w, tiled, rows) = refs[:-6], refs[-6:]
+    count, depth = down_w.shape[0], down_w.shape[1]
     half = depth // 2
     me = place[2]
+
+    def keep(piece, at, first, size):
+        row = pl.multiple_of(at * depth + first, half)
+        gate_w[pl.ds(row, size), :] = piece[0]
+        up_w[pl.ds(row, size), :] = piece[1]
+        down_w[at, first : first + size] = piece[2]
+
     for n, piece in enumerate(pieces[:-2]):
         turn = (n + 1) // 2
-        weights[lax.rem(me + (turn if n % 2 == 0 else count - turn), count)] = piece[...]
+        keep(piece, lax.rem(me + (turn if n % 2 == 0 else count - turn), count), 0, depth)
     opposite = lax.rem(me + count // 2, count)
-    weights[opposite, :, :half] = pieces[-2][...]
-    weights[opposite, :, half:] = pieces[-1][...]
+    keep(pieces[-2], opposite, 0, half)
+    keep(pieces[-1], opposite, half, half)
     load_rows(source, tiled, rows)
     for part in range(2):
         some = slice(part * depth, (part + 1) * depth)
         total = None
         for d in range(count):
-            term = contract_last(
-                rows[:, d * depth : (d + 1) * depth], weights[d, 2, :, some]
-            )
+            term = contract_last(rows[:, d * depth : (d + 1) * depth], down_w[d, :, some])
             total = term if total is None else total + term
         out[:, some] = total
 
 
-def w_spec(weights, which):
-    slices, _, depth, hidden = weights.shape
-    return pl.BlockSpec(
-        (slices, None, depth, hidden),
-        lambda i: (0, which, 0, 0),
-        pipeline_mode=pl.Buffered(1),
-    )
-
-
 def act_grad_of(place, source, pieces, width):
     slots = source.shape[0] * LANES // width
-    kinds, depth, hidden = pieces[0].shape
-    count = width // depth
+    _, depth, hidden = pieces[0].shape
     return call(
         act_grad_kernel,
         (
             shape_of(slots, hidden, jnp.float32),
-            jax.ShapeDtypeStruct((count, kinds, depth, hidden), jnp.bfloat16),
+            shape_of(width, hidden),
+            shape_of(width, hidden),
+            jax.ShapeDtypeStruct((width // depth, depth, hidden), jnp.bfloat16),
         ),
         [pltpu.VMEM(source.shape, jnp.float32), pltpu.VMEM((slots, width), jnp.bfloat16)],
         [SMEM, VMEM] + [VMEM] * len(pieces),
@@ -209,40 +224,36 @@
 
 def expert_kernel(source, gate_w, up_w, act_grad, in_grad, act, tiled, rows):
     load_rows(source, tiled, rows)
-    slices, depth, hidden = gate_w.shape
-    count = rows.shape[0]
+    count, width = rows.shape
     values = rows[...]
-    pre_gate = jnp.dot(
-        values, gate_w[...].reshape(slices * depth, hidden), preferred_element_type=jnp.float32
-    )
-    pre_up = jnp.dot(
-        values, up_w[...].reshape(slices * depth, hidden), preferred_element_type=jnp.float32
-    )
+    pre_gate = jnp.dot(values, gate_w[...], preferred_element_type=jnp.float32)
+    pre_up = jnp.dot(values, up_w[...], preferred_element_type=jnp.float32)
     sig = jax.nn.sigmoid(pre_gate)
     silu = pre_gate * sig
     act[...] = (silu * pre_up).astype(jnp.bfloat16)
     back = act_grad[...]
     gate_grad = (back * pre_up * sig * (1.0 + pre_gate * (1.0 - sig))).astype(jnp.bfloat16)
     up_grad = (back * silu).astype(jnp.bfloat16)
-    parts = slices * depth // LANES
-    for d in range(slices):
-        entry = contract_last(gate_grad, gate_w[d]) + contract_last(up_grad, up_w[d])
+    parts = width // LANES
+    depth = 256
+    for d in range(0, width, depth):
+        entry = contract_last(gate_grad, gate_w[d : d + depth]) + contract_last(
+            up_grad, up_w[d : d + depth]
+        )
         for p in range(depth // LANES):
-            tiled[pl.ds(d * (depth // LANES) + p, count, stride=parts), :] = entry[
-                :, lanes_of(p)
-            ]
+            tiled[pl.ds(d // LANES + p, count, stride=parts), :] = entry[:, lanes_of(p)]
     in_grad[...] = tiled[...].astype(jnp.bfloat16)
 
 
-def expert_back(source, weights, act_grad):
+def expert_back(source, gate_w, up_w, act_grad):
     slots, hidden = act_grad.shape
-    width = weights.shape[0] * weights.shape[2]
+    width = gate_w.shape[0]
     return call(
         expert_kernel,
         (shape_of(*source.shape), shape_of(slots, hidden)),
         [pltpu.VMEM(source.shape, jnp.float32), pltpu.VMEM((slots, width), jnp.bfloat16)],
-        [VMEM, w_spec(weights, 0), w_spec(weights, 1), VMEM],
-    )(source, weights, weights, act_grad)
+        [VMEM] * 4,
+    )(source, gate_w, up_w, act_grad)
 
 
 def out_kernel(act, down, out, tiled):
@@ -261,20 +272,20 @@
     out[...] = tiled[...].astype(jnp.bfloat16)
 
 
-def expert_out(act, weights):
-    slices, _, depth, _ = weights.shape
+def expert_out(act, down):
+    slices, depth, _ = down.shape
     rows = act.shape[0] * slices * depth // LANES
     return call(
-        out_kernel,
-        shape_of(rows, LANES),
-        [pltpu.VMEM((rows, LANES), jnp.float32)],
-        [VMEM, w_spec(weights, 2)],
-    )(act, weights)
-
-
-def resid_grad_kernel(dest, source, resid, gain, grad, proj, out, context_grad, tiled, rows):
+        out_kernel, shape_of(rows, LANES), [pltpu.VMEM((rows, LANES), jnp.float32)], [VMEM, VMEM]
+    )(act, down)
+
+
+def resid_grad_kernel(dest, place, source, resid, gain, grad, *refs):
+    pieces, (out, context_grad, tiled, rows, proj) = refs[:8], refs[8:]
     tok, width = resid.shape
     parts = width // LANES
+    heads, ys, cols, depth = pieces[0].shape
+    xs = len(pieces) // 2
 
     def step(t, carry):
         first = source[block(dest[2 * t], parts), :].astype(jnp.float32)
@@ -288,6 +299,20 @@
         rows[:, lanes_of(part)] = values * gain[:, lanes_of(part)]
 
     to_rows(tiled, tok, parts, put)
+
+    def fill(y, carry):
+        for k in range(xs):
+            x = lax.rem(place[0] + xs - k, xs)
+            for which in range(2):
+                core = place[1] if which == 0 else 1 - place[1]
+                at = pl.multiple_of(((x * ys + y) * 2 + core) * cols, cols)
+                for h in range(heads):
+                    proj[pl.ds(at, cols), h * depth : (h + 1) * depth] = pieces[
+                        2 * k + which
+                    ][h, y]
+        return carry
+
+    lax.fori_loop(0, ys, fill, 0)
     resid_f = resid[...].astype(jnp.float32)
     inv_rms = lax.rsqrt(jnp.mean(resid_f * resid_f, axis=-1, keepdims=True) + epsilon)
     unit = resid_f * inv_rms
@@ -302,17 +327,19 @@
     ).astype(jnp.bfloat16)
 
 
-def resid_grad_of(dest, source, resid, gain, grad, proj):
+def resid_grad_of(dest, place, source, resid, gain, grad, pieces):
     tok, width = resid.shape
+    heads, _, _, depth = pieces[0].shape
     return call(
         resid_grad_kernel,
-        (shape_of(tok, width), shape_of(tok, proj.shape[1])),
+        (shape_of(tok, width), shape_of(tok, heads * depth)),
         [
             pltpu.VMEM((tok * width // LANES, LANES), jnp.float32),
             pltpu.VMEM((tok, width), jnp.float32),
+            pltpu.VMEM((width, heads * depth), jnp.bfloat16),
         ],
-        [SMEM] + [VMEM] * 5,
-    )(dest, source, resid, gain[None], grad, proj)
+        [SMEM, SMEM] + [VMEM] * (4 + len(pieces)),
+    )(dest, place, source, resid, gain[None], grad, *pieces)
 
 
 def layer_out_kernel(dest, gate, source, resid, out, tiled):
@@ -428,6 +455,27 @@
     for part in shifted:
         pieces += [part, lax.ppermute(part, "core", [(0, 1), (1, 0)])]
     return pieces
+
+
+def swap_cores(block):
+    return lax.ppermute(block, "core", [(0, 1), (1, 0)])
+
+
+def move_x(block, turn):
+    xs = lax.axis_size("x")
+    return lax.ppermute(block, "x", [(i, (i + turn) % xs) for i in range(xs)])
+
+
+def gather_contexts(context):
+    pair = jnp.stack([context, swap_cores(context)])
+    return [pair] + [move_x(pair, k) for k in range(1, lax.axis_size("x"))]
+
+
+def return_products(products):
+    xs = lax.axis_size("x")
+    mine = [products[0]] + [move_x(products[k], xs - k) for k in range(1, xs)]
+    other = swap_cores(jnp.stack([block[1] for block in mine]))
+    return mine, other
 
 
 def pack_experts(w_gate, w_up, w_down):
@@ -492,18 +540,24 @@
     dest = slots_of(expert_ids, experts, capacity)
     slices = ring_experts(pack_experts(w_gate, w_up, w_down))
     to_send = send_grads(dest, gates, grad_out, slots)
+    context = context_of(segment_ids, queries, keys, values)
+    contexts = gather_contexts(context)
     near, to_send = lax.optimization_barrier((gather_near(out_proj), to_send))
     recv_grads = exchange(to_send)
+    mine, other = return_products(slab_products(near, contexts))
+    resid, rows = make_resid(
+        dest, place, mine, other, hidden_in, norm_gain, slots, out_proj.shape[1]
+    )
     pieces = gather_pieces(near)
-    context = context_of(segment_ids, queries, keys, values)
-    proj, resid, rows = make_resid(dest, place, pieces, context, hidden_in, norm_gain, slots)
     recv_rows = exchange(rows)
-    act_grad, weights = act_grad_of(place, recv_grads, slices, width)
-    in_grad, act = expert_back(recv_rows, weights, act_grad)
+    act_grad, gate_full, up_full, down_full = act_grad_of(place, recv_grads, slices, width)
+    in_grad, act = expert_back(recv_rows, gate_full, up_full, act_grad)
     back_grad = exchange(in_grad)
-    back_grad, out = lax.optimization_barrier((back_grad, expert_out(act, weights)))
+    back_grad, out = lax.optimization_barrier((back_grad, expert_out(act, down_full)))
     back_out = exchange(out)
-    resid_grad, context_grad = resid_grad_of(dest, back_grad, resid, norm_gain, grad_out, proj)
+    resid_grad, context_grad = resid_grad_of(
+        dest, place, back_grad, resid, norm_gain, grad_out, pieces
+    )
     query_grad, key_grad, value_grad = attention_grad(
         segment_ids, queries, keys, values, context_grad
     )

time: 322 us -> 353 us (1.096)
  starting transfers between devices: 118 us -> 140 us
  Pallas kernels: 51.4 us -> 31 us
  waiting for transfers between devices: 139 us -> 154 us
  local copies, waits for them, and re-layouts: 9.07 us -> 23.9 us
    ppermute x0 -> x8, waiting for transfers between devices: none -> 41 us  [the longest x6 38.8 us: move_x(): return lax.ppermute(block, 'x', [(i, (i + turn) % xs) for i in range(xs)])]
    all_to_all x5, waiting for transfers between devices: 75.8 us -> 49.1 us  [spread(): return lax.all_to_all(rows, axes, split_axis=0, concat_axis=0, tiled=True)]
    ppermute x0 -> x8, starting transfers between devices: none -> 22.6 us  [the longest x6 16.8 us: move_x(): return lax.ppermute(block, 'x', [(i, (i + turn) % xs) for i in range(xs)])]
    unnamed x39 -> x63, local copies, waits for them, and re-layouts: 5.73 us -> 20.7 us
    pallas_call x3 -> x4, Pallas kernels: 20.8 us -> 10.4 us  [the longest x1 3.67 us: resid_grad_of(): call(resid_grad_kernel, (shape_of(tok, width), shape_of(tok, heads * dept...]
    pallas_call x1, Pallas kernels: 9.02 us -> 5.27 us  [expert_back(): call(expert_kernel, (shape_of(*source.shape), shape_of(slots, hidden)), [...]
  transfers between devices with their start and end apart: 20 -> 28, of which waited for: 10 -> 17; matrix products, arithmetic and copies ran while one was open for 1% -> 1% of each run, Pallas kernels for 12% -> 7%
where the time goes in v3:
time: 353 us; the launch traced here: 351 us
  waiting for transfers between devices  154 us (44%)
  starting transfers between devices  140 us (40%)
  Pallas kernels  31 us (9%)
  local copies, waits for them, and re-layouts  23.9 us (7%)
    all_to_all x5, starting transfers between devices, spread(): return lax.all_to_all(rows, axes, split_axis=0, concat_axis=0, tiled=True)  55.3 us
    all_to_all x5, waiting for transfers between devices, spread(): return lax.all_to_all(rows, axes, split_axis=0, concat_axis=0, tiled=True)  49.1 us
    ppermute x3, waiting for transfers between devices, ring_experts(): right = lax.ppermute(right, 'dp', behind)  42.4 us
    ppermute x6, waiting for transfers between devices, move_x(): return lax.ppermute(block, 'x', [(i, (i + turn) % xs) for i in range(xs)])  38.8 us
    ppermute x4, starting transfers between devices, gather_pieces(): pieces += [part, lax.ppermute(part, 'core', [(0, 1), (1, 0)])]  27.8 us
    unnamed x63, local copies, waits for them, and re-layouts  20.7 us
    ppermute x6, starting transfers between devices, move_x(): return lax.ppermute(block, 'x', [(i, (i + turn) % xs) for i in range(xs)])  16.8 us
    ppermute x3, waiting for transfers between devices, gather_pieces(): lax.ppermute(near, 'x', [(i, (i + k) % xs) for i in range(xs)])  11.7 us
  transfers between devices with their start and end apart: 28, of which 17 were waited for; matrix products, arithmetic and copies ran while one was open for 1% of the time, Pallas kernels for 7%

profile of v3, /device:TPU:1, one launch (start us, length us, event | category | flops | bytes accessed | tf_op | source)
XLA Modules:
  0.0 350.9 jit_solution(17479099232455991081)
XLA Ops:
  0.7 1.6 broadcast_in_dim.8
  2.3 17.1 %all-to-all-start = ((bf16[64,32,128]{2,1,0:T(8,128)(2,1)}), bf16[64,32,128]{2,1,0:T(8,128)(2,1)S(1)}, u32[]{:S(2)}, u32[]{:S(2)}) async-start(bf16[64,32,128]{2,1,0:T(8,128)(2,1)} %broadcast_in_dim.8), calls=%async_computation | async-start | bytes 1048576 | tf_op jit(solution)/shard_map/all_to_all | solution.py:438
  20.2 3.0 shard_map.164
  23.2 13.6 %all-to-all-done = bf16[64,32,128]{2,1,0:T(8,128)(2,1)S(1)} async-done(((bf16[64,32,128]{2,1,0:T(8,128)(2,1)}), bf16[64,32,128]{2,1,0:T(8,128)(2,1)S(1)}, u32[]{:S(2)}, u32[]{:S(2)}) %all-to-all-start) | async-done | bytes 524320 | tf_op jit(solution)/shard_map/all_to_all | solution.py:438
  36.9 10.0 %all-to-all-start.2 = ((bf16[64,96,128]{2,1,0:T(8,128)(2,1)}), bf16[64,96,128]{2,1,0:T(8,128)(2,1)S(1)}, u32[]{:S(2)}, u32[]{:S(2)}) async-start(bf16[64,96,128]{2,1,0:T(8,128)(2,1)} %bitcast.12), calls=%async_computation.2 | async-start | bytes 3145728 | tf_op jit(solution)/shard_map/all_to_all | solution.py:438
  47.0 2.7 shard_map.165
  49.7 2.4 collective-permute-start
  52.1 1.1 collective-permute-done
  53.3 4.7 %collective-permute-start.3 = (bf16[2,128,1024]{2,1,0:T(8,128)(2,1)S(1)}, bf16[2,128,1024]{2,1,0:T(8,128)(2,1)S(1)}, u32[]{:S(2)}, u32[]{:S(2)}) collective-permute-start(bf16[2,128,1024]{2,1,0:T(8,128)(2,1)S(1)} %pad_maximum_fusion.1.refs_0_), channel_id=1, source_target_pairs={{0,48},{16,0},{32,16},{48,32},{1,49},{17,1},{33,17},{49,33},{2,50}... | collective-permute-start | bytes 1572872 | tf_op jit(solution)/shard_map/ppermute | solution.py:466
  58.1 2.3 collective-permute-start.2
  60.4 2.6 collective-permute-start.1
  63.0 16.6 %collective-permute-done.3.refs_3_ = bf16[2,128,1024]{2,1,0:T(8,128)(2,1)S(1)} collective-permute-done((bf16[2,128,1024]{2,1,0:T(8,128)(2,1)S(1)}, bf16[2,128,1024]{2,1,0:T(8,128)(2,1)S(1)}, u32[]{:S(2)}, u32[]{:S(2)}) %collective-permute-start.3) | collective-permute-done | bytes 524320 | tf_op jit(solution)/shard_map/ppermute | solution.py:466
  79.6 4.7 %collective-permute-done.2.refs_2_ = bf16[2,128,1024]{2,1,0:T(8,128)(2,1)S(1)} collective-permute-done((bf16[2,128,1024]{2,1,0:T(8,128)(2,1)S(1)}, bf16[2,128,1024]{2,1,0:T(8,128)(2,1)S(1)}, u32[]{:S(2)}, u32[]{:S(2)}) %collective-permute-start.2) | collective-permute-done | bytes 524320 | tf_op jit(solution)/shard_map/ppermute | solution.py:466
  84.3 12.7 %collective-permute-done.1.refs_1_ = bf16[2,128,1024]{2,1,0:T(8,128)(2,1)S(1)} collective-permute-done((bf16[2,128,1024]{2,1,0:T(8,128)(2,1)S(1)}, bf16[2,128,1024]{2,1,0:T(8,128)(2,1)S(1)}, u32[]{:S(2)}, u32[]{:S(2)}) %collective-permute-start.1) | collective-permute-done | bytes 524320 | tf_op jit(solution)/shard_map/ppermute | solution.py:466
  96.9 1.5 shard_map.166
  98.5 1.9 collective-permute-start.4
  100.4 2.2 collective-permute-start.5
  102.6 3.1 collective-permute-start.6
  106.4 1.2 collective-permute-done.5.refs_2_
  107.6 3.6 %collective-permute-done.6.refs_3_ = bf16[2,128,256]{2,1,0:T(8,128)(2,1)S(1)} collective-permute-done((bf16[2,128,256]{2,1,0:T(8,128)(2,1)S(1)}, bf16[2,128,256]{2,1,0:T(8,128)(2,1)S(1)}, u32[]{:S(2)}, u32[]{:S(2)}) %collective-permute-start.6) | collective-permute-done | bytes 131104 | tf_op jit(solution)/shard_map/ppermute | solution.py:466
  111.2 3.4 collective-permute-start.7
  116.7 2.4 shard_map.167
  119.9 1.2 copy-done.13
  121.2 7.6 %all-to-all-start.1 = ((bf16[64,96,128]{2,1,0:T(8,128)(2,1)}), bf16[64,96,128]{2,1,0:T(8,128)(2,1)S(1)}, u32[]{:S(2)}, u32[]{:S(2)}) async-start(bf16[64,96,128]{2,1,0:T(8,128)(2,1)} %bitcast.34), calls=%async_computation.1 | async-start | bytes 3145728 | tf_op jit(solution)/shard_map/all_to_all | solution.py:438
  129.8 1.1 pad_maximum_fusion.refs_0_
  130.9 2.0 collective-permute-start.9
  133.0 3.2 collective-permute-start.8
  136.2 15.2 %collective-permute-done.9.refs_2_ = bf16[3,256,512]{2,1,0:T(8,128)(2,1)S(1)} collective-permute-done((bf16[3,256,512]{2,1,0:T(8,128)(2,1)S(1)}, bf16[3,256,512]{2,1,0:T(8,128)(2,1)S(1)}, u32[]{:S(2)}, u32[]{:S(2)}) %collective-permute-start.9) | collective-permute-done | bytes 786464 | tf_op jit(solution)/shard_map/ppermute | solution.py:495
  151.5 3.2 collective-permute-start.11
  154.7 2.0 collective-permute-start.10
  156.8 14.4 %collective-permute-done.11.refs_4_ = bf16[3,256,512]{2,1,0:T(8,128)(2,1)S(1)} collective-permute-done((bf16[3,256,512]{2,1,0:T(8,128)(2,1)S(1)}, bf16[3,256,512]{2,1,0:T(8,128)(2,1)S(1)}, u32[]{:S(2)}, u32[]{:S(2)}) %collective-permute-start.11) | collective-permute-done | bytes 786464 | tf_op jit(solution)/shard_map/ppermute | solution.py:495
  171.1 4.5 %collective-permute-start.13 = (bf16[3,256,512]{2,1,0:T(8,128)(2,1)S(1)}, bf16[3,256,512]{2,1,0:T(8,128)(2,1)S(1)}, u32[]{:S(2)}, u32[]{:S(2)}) collective-permute-start(bf16[3,256,512]{2,1,0:T(8,128)(2,1)S(1)} %collective-permute-done.11.refs_4_), channel_id=1, source_target_pairs={{0,448},{64,0},{128,64},{192,128},{256,192},{320,256},{384,320},{4... | collective-permute-start | bytes 2359304 | tf_op jit(solution)/shard_map/ppermute | solution.py:495
  175.6 1.9 collective-permute-start.12
  177.5 12.8 %collective-permute-done.13.refs_6_ = bf16[3,256,512]{2,1,0:T(8,128)(2,1)S(1)} collective-permute-done((bf16[3,256,512]{2,1,0:T(8,128)(2,1)S(1)}, bf16[3,256,512]{2,1,0:T(8,128)(2,1)S(1)}, u32[]{:S(2)}, u32[]{:S(2)}) %collective-permute-start.13) | collective-permute-done | bytes 786464 | tf_op jit(solution)/shard_map/ppermute | solution.py:495
  190.3 5.3 %collective-permute-start.15 = (bf16[3,128,512]{2,1,0:T(8,128)(2,1)S(1)}, bf16[3,128,512]{2,1,0:T(8,128)(2,1)S(1)}, u32[]{:S(2)}, u32[]{:S(2)}) collective-permute-start(bf16[3,128,512]{2,1,0:T(8,128)(2,1)S(1)} %slice.36), channel_id=1, source_target_pairs={{0,448},{64,0},{128,64},{192,128},{256,192},{320,256},{384,320},{4... | collective-permute-start | bytes 1179656 | tf_op jit(solution)/shard_map/ppermute | solution.py:498
  195.7 2.1 collective-permute-start.14
  197.8 3.3 collective-permute-done.15.refs_8_
  201.1 5.1 %collective-permute-done.14.refs_7_ = bf16[3,128,512]{2,1,0:T(8,128)(2,1)S(1)} collective-permute-done((bf16[3,128,512]{2,1,0:T(8,128)(2,1)S(1)}, bf16[3,128,512]{2,1,0:T(8,128)(2,1)S(1)}, u32[]{:S(2)}, u32[]{:S(2)}) %collective-permute-start.14) | collective-permute-done | bytes 393248 | tf_op jit(solution)/shard_map/ppermute | solution.py:497
  206.2 2.8 shard_map.168
  209.0 1.3 copy-done.2
  210.3 1.4 copy-done.4
  211.7 1.3 copy-done.8
  214.0 1.6 copy-done.3
  215.5 1.6 copy-done.5
  217.1 1.1 copy-done.21
  218.3 5.3 %shard_map.169 = (bf16[6144,128]{1,0:T(8,128)(2,1)S(1)}, bf16[384,512]{1,0:T(8,128)(2,1)S(1)}) custom-call(bf16[6144,128]{1,0:T(8,128)(2,1)S(1)} %bitcast.25, bf16[2048,512]{1,0:T(8,128)(2,1)S(1)} %copy-done.3, bf16[2048,512]{1,0:T(8,128)(2,1)S(1)} %copy-done.5, f32[384,512]{1,0:T(8,128)S(1)} %copy-done.21), custom_call_target="tpu_custom_call" | custom-call | tf_op jit(solution)/shard_map/pallas_call | solution.py:251
  223.6 1.1 copy-done.14
  225.5 14.4 %all-to-all-start.3 = ((bf16[64,96,128]{2,1,0:T(8,128)(2,1)}), bf16[64,96,128]{2,1,0:T(8,128)(2,1)S(1)}, u32[]{:S(2)}, u32[]{:S(2)}) async-start(bf16[64,96,128]{2,1,0:T(8,128)(2,1)} %bitcast.35), calls=%async_computation.3 | async-start | bytes 3145728 | tf_op jit(solution)/shard_map/all_to_all | solution.py:438
  239.9 1.6 copy-done.9
  241.5 2.7 shard_map.170
  244.2 35.4 %all-to-all-done.3 = bf16[64,96,128]{2,1,0:T(8,128)(2,1)S(1)} async-done(((bf16[64,96,128]{2,1,0:T(8,128)(2,1)}), bf16[64,96,128]{2,1,0:T(8,128)(2,1)S(1)}, u32[]{:S(2)}, u32[]{:S(2)}) %all-to-all-start.3) | async-done | bytes 1572896 | tf_op jit(solution)/shard_map/all_to_all | solution.py:438
  279.7 6.1 %all-to-all-start.4 = ((bf16[64,96,128]{2,1,0:T(8,128)(2,1)}), bf16[64,96,128]{2,1,0:T(8,128)(2,1)S(1)}, u32[]{:S(2)}, u32[]{:S(2)}) async-start(bf16[64,96,128]{2,1,0:T(8,128)(2,1)} %bitcast.19), calls=%async_computation.4 | async-start | bytes 3145728 | tf_op jit(solution)/shard_map/all_to_all | solution.py:438
  285.8 4.7 %collective-permute-start.21 = (bf16[8,8,32,128]{3,2,1,0:T(8,128)(2,1)}, bf16[8,8,32,128]{3,2,1,0:T(8,128)(2,1)S(1)}, u32[]{:S(2)}, u32[]{:S(2)}) collective-permute-start(bf16[8,8,32,128]{3,2,1,0:T(8,128)(2,1)} %bitcast.29), channel_id=1, source_target_pairs={{0,48},{16,0},{32,16},{48,32},{1,49},{17,1},{33,17},{49,33},{2,50}... | collective-permute-start | bytes 1572872 | tf_op jit(solution)/shard_map/ppermute | solution.py:451
  290.5 2.3 collective-permute-start.19
  292.7 2.6 collective-permute-start.17
  295.3 3.1 collective-permute-start.16
  298.5 10.8 %collective-permute-done.21.refs_6_ = bf16[8,8,32,128]{3,2,1,0:T(8,128)(2,1)S(1)} collective-permute-done((bf16[8,8,32,128]{3,2,1,0:T(8,128)(2,1)}, bf16[8,8,32,128]{3,2,1,0:T(8,128)(2,1)S(1)}, u32[]{:S(2)}, u32[]{:S(2)}) %collective-permute-start.21) | collective-permute-done | bytes 524320 | tf_op jit(solution)/shard_map/ppermute | solution.py:451
  309.3 20.1 %collective-permute-start.22 = (bf16[8,8,32,128]{3,2,1,0:T(8,128)(2,1)S(1)}, bf16[8,8,32,128]{3,2,1,0:T(8,128)(2,1)S(1)}, u32[]{:S(2)}, u32[]{:S(2)}) collective-permute-start(bf16[8,8,32,128]{3,2,1,0:T(8,128)(2,1)S(1)} %collective-permute-done.21.refs_6_), channel_id=1, source_target_pairs={{0,1},{1,0},{2,3},{3,2},{4,5},{5,4},{6,7},{7,6},{8,9},{9,8},{10,11... | collective-permute-start | bytes 1572872 | tf_op jit(solution)/shard_map/ppermute | solution.py:456
  329.5 1.9 collective-permute-start.20
  332.2 2.6 collective-permute-start.18
  334.9 1.3 collective-permute-done.18.refs_3_
  339.3 3.7 %shard_map.172 = (bf16[128,2048]{1,0:T(8,128)(2,1)}, bf16[128,1024]{1,0:T(8,128)(2,1)S(1)}) custom-call(s32[256]{0:T(256)S(1)} %convert_add_fusion.dest, s32[3]{0:T(128)S(1)} %pad_add_fusion.place, bf16[6144,128]{1,0:T(8,128)(2,1)S(1)} %bitcast.26, bf16[128,2048]{1,0:T(8,128)(2,1)S(1)} %copy-done.11, f32[1,2048]{1,0:T(1,128)S(1)} %bitcast.38, ...), custom_call_target="tpu_custom_call" | custom-call | tf_op jit(solution)/shard_map/pallas_call | solution.py:333
  342.9 4.5 %shard_map.173 = (bf16[128,1024]{1,0:T(8,128)(2,1)}, bf16[128,1024]{1,0:T(8,128)(2,1)}, bf16[128,1024]{1,0:T(8,128)(2,1)}) custom-call(s32[1,128]{1,0:T(1,128)S(1)} %bitcast.41, s32[128,1]{1,0:T(8,128)S(1)} %copy.22.seg_col, bf16[128,1024]{1,0:T(8,128)(2,1)S(1)} %copy-done.15, bf16[128,1024]{1,0:T(8,128)(2,1)S(1)} %copy-done.17, ...), custom_call_target="tpu_custom_call" | custom-call | tf_op jit(solution)/shard_map/pallas_call | solution.py:432
  348.5 2.4 shard_map.171
  (85 shorter events, 12.3 us)
Async XLA Ops:
  0.6 18.8 %copy-start.30 = (s32[128,2]{0,1:T(2,128)S(1)}, s32[128,2]{0,1:T(2,128)}, u32[]{:S(2)}) copy-start(s32[128,2]{0,1:T(2,128)} %param.24) | copy-start | bytes 3076
  0.6 19.1 %copy-start.29 = (s32[128,2]{0,1:T(2,128)S(1)}, s32[128,2]{0,1:T(2,128)}, u32[]{:S(2)}) copy-start(s32[128,2]{0,1:T(2,128)} %param.23) | copy-start | bytes 3076
  0.7 19.5 %copy-start.6 = (bf16[128,2048]{1,0:T(8,128)(2,1)S(1)}, bf16[128,2048]{1,0:T(8,128)(2,1)}, u32[]{:S(2)}) copy-start(bf16[128,2048]{1,0:T(8,128)(2,1)} %grad.3) | copy-start | bytes 1572868
  2.3 34.6 %all-to-all-start = ((bf16[64,32,128]{2,1,0:T(8,128)(2,1)}), bf16[64,32,128]{2,1,0:T(8,128)(2,1)S(1)}, u32[]{:S(2)}, u32[]{:S(2)}) async-start(bf16[64,32,128]{2,1,0:T(8,128)(2,1)} %broadcast_in_dim.8), calls=%async_computation | async-start | bytes 1048576 | tf_op jit(solution)/shard_map/all_to_all | solution.py:438
  36.8 60.1 %copy-start = (bf16[64,32,128]{2,1,0:T(8,128)(2,1)}, bf16[64,32,128]{2,1,0:T(8,128)(2,1)S(1)}, u32[]{:S(2)}) copy-start(bf16[64,32,128]{2,1,0:T(8,128)(2,1)S(1)} %all-to-all-done) | copy-start | bytes 1572868
  36.8 10.1 %copy-start.28 = (s32[128]{0:T(128)S(1)}, s32[128]{0:T(128)}, u32[]{:S(2)}) copy-start(s32[128]{0:T(128)} %param.17) | copy-start | bytes 1540
  36.8 10.2 %copy-start.15 = (bf16[128,1024]{1,0:T(8,128)(2,1)S(1)}, bf16[128,1024]{1,0:T(8,128)(2,1)}, u32[]{:S(2)}) copy-start(bf16[128,1024]{1,0:T(8,128)(2,1)} %queries.3) | copy-start | bytes 786436
  36.8 10.2 %copy-start.16 = (bf16[128,1024]{1,0:T(8,128)(2,1)S(1)}, bf16[128,1024]{1,0:T(8,128)(2,1)}, u32[]{:S(2)}) copy-start(bf16[128,1024]{1,0:T(8,128)(2,1)} %keys.3) | copy-start | bytes 786436
  36.8 10.2 %copy-start.18 = (bf16[128,1024]{1,0:T(8,128)(2,1)S(1)}, bf16[128,1024]{1,0:T(8,128)(2,1)}, u32[]{:S(2)}) copy-start(bf16[128,1024]{1,0:T(8,128)(2,1)} %values.3) | copy-start | bytes 786436
  36.9 84.3 %all-to-all-start.2 = ((bf16[64,96,128]{2,1,0:T(8,128)(2,1)}), bf16[64,96,128]{2,1,0:T(8,128)(2,1)S(1)}, u32[]{:S(2)}, u32[]{:S(2)}) async-start(bf16[64,96,128]{2,1,0:T(8,128)(2,1)} %bitcast.12), calls=%async_computation.2 | async-start | bytes 3145728 | tf_op jit(solution)/shard_map/all_to_all | solution.py:438
  49.7 3.5 %collective-permute-start = (bf16[128,1024]{1,0:T(8,128)(2,1)S(1)}, bf16[128,1024]{1,0:T(8,128)(2,1)S(1)}, u32[]{:S(2)}, u32[]{:S(2)}) collective-permute-start(bf16[128,1024]{1,0:T(8,128)(2,1)S(1)} %shard_map.165), channel_id=1, source_target_pairs={{0,1},{1,0},{2,3},{3,2},{4,5},{5,4},{6,7},{7,6},{8,9},{9,8},{10,11... | collective-permute-start | bytes 786440 | tf_op jit(solution)/shard_map/ppermute | solution.py:461
  53.3 62.5 %copy-start.22 = (bf16[128,2048]{1,0:T(8,128)(2,1)S(1)}, bf16[128,2048]{1,0:T(8,128)(2,1)}, u32[]{:S(2)}) copy-start(bf16[128,2048]{1,0:T(8,128)(2,1)} %refs_5_.1) | copy-start | bytes 1572868
  53.3 62.5 %copy-start.27 = (f32[2048]{0:T(1024)S(1)}, f32[2048]{0:T(1024)}, u32[]{:S(2)}) copy-start(f32[2048]{0:T(1024)} %param.19) | copy-start | bytes 24580
  53.3 26.2 %collective-permute-start.3 = (bf16[2,128,1024]{2,1,0:T(8,128)(2,1)S(1)}, bf16[2,128,1024]{2,1,0:T(8,128)(2,1)S(1)}, u32[]{:S(2)}, u32[]{:S(2)}) collective-permute-start(bf16[2,128,1024]{2,1,0:T(8,128)(2,1)S(1)} %pad_maximum_fusion.1.refs_0_), channel_id=1, source_target_pairs={{0,48},{16,0},{32,16},{48,32},{1,49},{17,1},{33,17},{49,33},{2,50}... | collective-permute-start | bytes 1572872 | tf_op jit(solution)/shard_map/ppermute | solution.py:466
  58.1 26.2 %collective-permute-start.2 = (bf16[2,128,1024]{2,1,0:T(8,128)(2,1)S(1)}, bf16[2,128,1024]{2,1,0:T(8,128)(2,1)S(1)}, u32[]{:S(2)}, u32[]{:S(2)}) collective-permute-start(bf16[2,128,1024]{2,1,0:T(8,128)(2,1)S(1)} %pad_maximum_fusion.1.refs_0_), channel_id=1, source_target_pairs={{0,32},{16,48},{32,0},{48,16},{1,33},{17,49},{33,1},{49,17},{2,34}... | collective-permute-start | bytes 1572872 | tf_op jit(solution)/shard_map/ppermute | solution.py:466
  60.4 36.6 %collective-permute-start.1 = (bf16[2,128,1024]{2,1,0:T(8,128)(2,1)S(1)}, bf16[2,128,1024]{2,1,0:T(8,128)(2,1)S(1)}, u32[]{:S(2)}, u32[]{:S(2)}) collective-permute-start(bf16[2,128,1024]{2,1,0:T(8,128)(2,1)S(1)} %pad_maximum_fusion.1.refs_0_), channel_id=1, source_target_pairs={{0,16},{16,32},{32,48},{48,0},{1,17},{17,33},{33,49},{49,1},{2,18}... | collective-permute-start | bytes 1572872 | tf_op jit(solution)/shard_map/ppermute | solution.py:466
  98.5 7.9 %collective-permute-start.4 = (bf16[2,128,256]{2,1,0:T(8,128)(2,1)S(1)}, bf16[2,128,256]{2,1,0:T(8,128)(2,1)S(1)}, u32[]{:S(2)}, u32[]{:S(2)}) collective-permute-start(bf16[2,128,256]{2,1,0:T(8,128)(2,1)S(1)} %get-tuple-element.28), channel_id=1, source_target_pairs={{0,48},{16,0},{32,16},{48,32},{1,49},{17,1},{33,17},{49,33},{2,50}... | collective-permute-start | bytes 393224 | tf_op jit(solution)/shard_map/ppermute | solution.py:466
  100.4 7.2 %collective-permute-start.5 = (bf16[2,128,256]{2,1,0:T(8,128)(2,1)S(1)}, bf16[2,128,256]{2,1,0:T(8,128)(2,1)S(1)}, u32[]{:S(2)}, u32[]{:S(2)}) collective-permute-start(bf16[2,128,256]{2,1,0:T(8,128)(2,1)S(1)} %get-tuple-element.29), channel_id=1, source_target_pairs={{0,32},{16,48},{32,0},{48,16},{1,33},{17,49},{33,1},{49,17},{2,34}... | collective-permute-start | bytes 393224 | tf_op jit(solution)/shard_map/ppermute | solution.py:466
  102.6 8.6 %collective-permute-start.6 = (bf16[2,128,256]{2,1,0:T(8,128)(2,1)S(1)}, bf16[2,128,256]{2,1,0:T(8,128)(2,1)S(1)}, u32[]{:S(2)}, u32[]{:S(2)}) collective-permute-start(bf16[2,128,256]{2,1,0:T(8,128)(2,1)S(1)} %get-tuple-element.30), channel_id=1, source_target_pairs={{0,16},{16,32},{32,48},{48,0},{1,17},{17,33},{33,49},{49,1},{2,18}... | collective-permute-start | bytes 393224 | tf_op jit(solution)/shard_map/ppermute | solution.py:466
  105.7 0.7 copy-start.25
  111.2 4.5 %collective-permute-start.7 = (bf16[4,128,256]{2,1,0:T(8,128)(2,1)S(1)}, bf16[4,128,256]{2,1,0:T(8,128)(2,1)S(1)}, u32[]{:S(2)}, u32[]{:S(2)}) collective-permute-start(bf16[4,128,256]{2,1,0:T(8,128)(2,1)S(1)} %pad_maximum_fusion.2), channel_id=1, source_target_pairs={{0,1},{1,0},{2,3},{3,2},{4,5},{5,4},{6,7},{7,6},{8,9},{9,8},{10,11... | collective-permute-start | bytes 786440 | tf_op jit(solution)/shard_map/ppermute | solution.py:461
  115.8 0.9 copy-start.26
  119.1 0.8 copy-start.10
  119.9 1.2 copy-start.13
  121.2 92.8 %all-to-all-start.1 = ((bf16[64,96,128]{2,1,0:T(8,128)(2,1)}), bf16[64,96,128]{2,1,0:T(8,128)(2,1)S(1)}, u32[]{:S(2)}, u32[]{:S(2)}) async-start(bf16[64,96,128]{2,1,0:T(8,128)(2,1)} %bitcast.34), calls=%async_computation.1 | async-start | bytes 3145728 | tf_op jit(solution)/shard_map/all_to_all | solution.py:438
  130.9 20.5 %collective-permute-start.9 = (bf16[3,256,512]{2,1,0:T(8,128)(2,1)S(1)}, bf16[3,256,512]{2,1,0:T(8,128)(2,1)S(1)}, u32[]{:S(2)}, u32[]{:S(2)}) collective-permute-start(bf16[3,256,512]{2,1,0:T(8,128)(2,1)S(1)} %pad_maximum_fusion.refs_0_), channel_id=1, source_target_pairs={{0,448},{64,0},{128,64},{192,128},{256,192},{320,256},{384,320},{4... | collective-permute-start | bytes 2359304 | tf_op jit(solution)/shard_map/ppermute | solution.py:495
  133.0 21.7 %collective-permute-start.8 = (bf16[3,256,512]{2,1,0:T(8,128)(2,1)S(1)}, bf16[3,256,512]{2,1,0:T(8,128)(2,1)S(1)}, u32[]{:S(2)}, u32[]{:S(2)}) collective-permute-start(bf16[3,256,512]{2,1,0:T(8,128)(2,1)S(1)} %pad_maximum_fusion.refs_0_), channel_id=1, source_target_pairs={{0,64},{64,128},{128,192},{192,256},{256,320},{320,384},{384,448},... | collective-permute-start | bytes 2359304 | tf_op jit(solution)/shard_map/ppermute | solution.py:494
  151.5 19.7 %collective-permute-start.11 = (bf16[3,256,512]{2,1,0:T(8,128)(2,1)S(1)}, bf16[3,256,512]{2,1,0:T(8,128)(2,1)S(1)}, u32[]{:S(2)}, u32[]{:S(2)}) collective-permute-start(bf16[3,256,512]{2,1,0:T(8,128)(2,1)S(1)} %collective-permute-done.9.refs_2_), channel_id=1, source_target_pairs={{0,448},{64,0},{128,64},{192,128},{256,192},{320,256},{384,320},{4... | collective-permute-start | bytes 2359304 | tf_op jit(solution)/shard_map/ppermute | solution.py:495
  154.7 20.9 %collective-permute-start.10 = (bf16[3,256,512]{2,1,0:T(8,128)(2,1)S(1)}, bf16[3,256,512]{2,1,0:T(8,128)(2,1)S(1)}, u32[]{:S(2)}, u32[]{:S(2)}) collective-permute-start(bf16[3,256,512]{2,1,0:T(8,128)(2,1)S(1)} %collective-permute-done.8.refs_1_), channel_id=1, source_target_pairs={{0,64},{64,128},{128,192},{192,256},{256,320},{320,384},{384,448},... | collective-permute-start | bytes 2359304 | tf_op jit(solution)/shard_map/ppermute | solution.py:494
  171.1 19.2 %collective-permute-start.13 = (bf16[3,256,512]{2,1,0:T(8,128)(2,1)S(1)}, bf16[3,256,512]{2,1,0:T(8,128)(2,1)S(1)}, u32[]{:S(2)}, u32[]{:S(2)}) collective-permute-start(bf16[3,256,512]{2,1,0:T(8,128)(2,1)S(1)} %collective-permute-done.11.refs_4_), channel_id=1, source_target_pairs={{0,448},{64,0},{128,64},{192,128},{256,192},{320,256},{384,320},{4... | collective-permute-start | bytes 2359304 | tf_op jit(solution)/shard_map/ppermute | solution.py:495
  175.6 20.1 %collective-permute-start.12 = (bf16[3,256,512]{2,1,0:T(8,128)(2,1)S(1)}, bf16[3,256,512]{2,1,0:T(8,128)(2,1)S(1)}, u32[]{:S(2)}, u32[]{:S(2)}) collective-permute-start(bf16[3,256,512]{2,1,0:T(8,128)(2,1)S(1)} %collective-permute-done.10.refs_3_), channel_id=1, source_target_pairs={{0,64},{64,128},{128,192},{192,256},{256,320},{320,384},{384,448},... | collective-permute-start | bytes 2359304 | tf_op jit(solution)/shard_map/ppermute | solution.py:494
  190.3 10.8 %collective-permute-start.15 = (bf16[3,128,512]{2,1,0:T(8,128)(2,1)S(1)}, bf16[3,128,512]{2,1,0:T(8,128)(2,1)S(1)}, u32[]{:S(2)}, u32[]{:S(2)}) collective-permute-start(bf16[3,128,512]{2,1,0:T(8,128)(2,1)S(1)} %slice.36), channel_id=1, source_target_pairs={{0,448},{64,0},{128,64},{192,128},{256,192},{320,256},{384,320},{4... | collective-permute-start | bytes 1179656 | tf_op jit(solution)/shard_map/ppermute | solution.py:498
  195.7 10.5 %collective-permute-start.14 = (bf16[3,128,512]{2,1,0:T(8,128)(2,1)S(1)}, bf16[3,128,512]{2,1,0:T(8,128)(2,1)S(1)}, u32[]{:S(2)}, u32[]{:S(2)}) collective-permute-start(bf16[3,128,512]{2,1,0:T(8,128)(2,1)S(1)} %slice.35), channel_id=1, source_target_pairs={{0,64},{64,128},{128,192},{192,256},{256,320},{320,384},{384,448},... | collective-permute-start | bytes 1179656 | tf_op jit(solution)/shard_map/ppermute | solution.py:497
  209.0 1.4 copy-start.2
  210.3 1.4 copy-start.4
  211.7 1.3 copy-start.8
  213.0 0.9 copy-start.20
  213.9 1.6 copy-start.3
  215.5 1.6 copy-start.5
  217.1 1.1 copy-start.21
  223.6 1.1 copy-start.14
  224.7 0.8 copy-start.23
  225.5 14.4 %copy-start.24 = (bf16[384,512]{1,0:T(8,128)(2,1)S(1)}, bf16[384,512]{1,0:T(8,128)(2,1)}, u32[]{:S(2)}) copy-start(bf16[384,512]{1,0:T(8,128)(2,1)} %copy-done.23) | copy-start | bytes 1179652
  225.5 54.2 %all-to-all-start.3 = ((bf16[64,96,128]{2,1,0:T(8,128)(2,1)}), bf16[64,96,128]{2,1,0:T(8,128)(2,1)S(1)}, u32[]{:S(2)}, u32[]{:S(2)}) async-start(bf16[64,96,128]{2,1,0:T(8,128)(2,1)} %bitcast.35), calls=%async_computation.3 | async-start | bytes 3145728 | tf_op jit(solution)/shard_map/all_to_all | solution.py:438
  239.9 1.6 copy-start.9
  279.7 67.8 %all-to-all-start.4 = ((bf16[64,96,128]{2,1,0:T(8,128)(2,1)}), bf16[64,96,128]{2,1,0:T(8,128)(2,1)S(1)}, u32[]{:S(2)}, u32[]{:S(2)}) async-start(bf16[64,96,128]{2,1,0:T(8,128)(2,1)} %bitcast.19), calls=%async_computation.4 | async-start | bytes 3145728 | tf_op jit(solution)/shard_map/all_to_all | solution.py:438
  285.8 23.5 %collective-permute-start.21 = (bf16[8,8,32,128]{3,2,1,0:T(8,128)(2,1)}, bf16[8,8,32,128]{3,2,1,0:T(8,128)(2,1)S(1)}, u32[]{:S(2)}, u32[]{:S(2)}) collective-permute-start(bf16[8,8,32,128]{3,2,1,0:T(8,128)(2,1)} %bitcast.29), channel_id=1, source_target_pairs={{0,48},{16,0},{32,16},{48,32},{1,49},{17,1},{33,17},{49,33},{2,50}... | collective-permute-start | bytes 1572872 | tf_op jit(solution)/shard_map/ppermute | solution.py:451
  290.5 39.0 %collective-permute-start.19 = (bf16[8,8,32,128]{3,2,1,0:T(8,128)(2,1)}, bf16[8,8,32,128]{3,2,1,0:T(8,128)(2,1)S(1)}, u32[]{:S(2)}, u32[]{:S(2)}) collective-permute-start(bf16[8,8,32,128]{3,2,1,0:T(8,128)(2,1)} %bitcast.30), channel_id=1, source_target_pairs={{0,32},{16,48},{32,0},{48,16},{1,33},{17,49},{33,1},{49,17},{2,34}... | collective-permute-start | bytes 1572872 | tf_op jit(solution)/shard_map/ppermute | solution.py:451
  292.7 39.5 %collective-permute-start.17 = (bf16[8,8,32,128]{3,2,1,0:T(8,128)(2,1)}, bf16[8,8,32,128]{3,2,1,0:T(8,128)(2,1)S(1)}, u32[]{:S(2)}, u32[]{:S(2)}) collective-permute-start(bf16[8,8,32,128]{3,2,1,0:T(8,128)(2,1)} %bitcast.31), channel_id=1, source_target_pairs={{0,16},{16,32},{32,48},{48,0},{1,17},{17,33},{33,49},{49,1},{2,18}... | collective-permute-start | bytes 1572872 | tf_op jit(solution)/shard_map/ppermute | solution.py:451
  295.3 39.5 %collective-permute-start.16 = (bf16[8,8,32,128]{3,2,1,0:T(8,128)(2,1)}, bf16[8,8,32,128]{3,2,1,0:T(8,128)(2,1)S(1)}, u32[]{:S(2)}, u32[]{:S(2)}) collective-permute-start(bf16[8,8,32,128]{3,2,1,0:T(8,128)(2,1)} %bitcast.32), channel_id=1, source_target_pairs={{0,1},{1,0},{2,3},{3,2},{4,5},{5,4},{6,7},{7,6},{8,9},{9,8},{10,11... | collective-permute-start | bytes 1572872 | tf_op jit(solution)/shard_map/ppermute | solution.py:456
  309.3 25.6 %collective-permute-start.22 = (bf16[8,8,32,128]{3,2,1,0:T(8,128)(2,1)S(1)}, bf16[8,8,32,128]{3,2,1,0:T(8,128)(2,1)S(1)}, u32[]{:S(2)}, u32[]{:S(2)}) collective-permute-start(bf16[8,8,32,128]{3,2,1,0:T(8,128)(2,1)S(1)} %collective-permute-done.21.refs_6_), channel_id=1, source_target_pairs={{0,1},{1,0},{2,3},{3,2},{4,5},{5,4},{6,7},{7,6},{8,9},{9,8},{10,11... | collective-permute-start | bytes 1572872 | tf_op jit(solution)/shard_map/ppermute | solution.py:456
  329.5 5.4 %collective-permute-start.20 = (bf16[8,8,32,128]{3,2,1,0:T(8,128)(2,1)S(1)}, bf16[8,8,32,128]{3,2,1,0:T(8,128)(2,1)S(1)}, u32[]{:S(2)}, u32[]{:S(2)}) collective-permute-start(bf16[8,8,32,128]{3,2,1,0:T(8,128)(2,1)S(1)} %collective-permute-done.19.refs_4_), channel_id=1, source_target_pairs={{0,1},{1,0},{2,3},{3,2},{4,5},{5,4},{6,7},{7,6},{8,9},{9,8},{10,11... | collective-permute-start | bytes 1572872 | tf_op jit(solution)/shard_map/ppermute | solution.py:456
  332.2 3.9 %collective-permute-start.18 = (bf16[8,8,32,128]{3,2,1,0:T(8,128)(2,1)S(1)}, bf16[8,8,32,128]{3,2,1,0:T(8,128)(2,1)S(1)}, u32[]{:S(2)}, u32[]{:S(2)}) collective-permute-start(bf16[8,8,32,128]{3,2,1,0:T(8,128)(2,1)S(1)} %collective-permute-done.17.refs_2_), channel_id=1, source_target_pairs={{0,1},{1,0},{2,3},{3,2},{4,5},{5,4},{6,7},{7,6},{8,9},{9,8},{10,11... | collective-permute-start | bytes 1572872 | tf_op jit(solution)/shard_map/ppermute | solution.py:456
  336.1 1.0 copy-start.1
  337.2 1.0 copy-start.7
  338.2 1.0 copy-start.11
  339.3 3.7 %copy-start.17 = (bf16[128,1024]{1,0:T(8,128)(2,1)S(1)}, bf16[128,1024]{1,0:T(8,128)(2,1)}, u32[]{:S(2)}) copy-start(bf16[128,1024]{1,0:T(8,128)(2,1)} %keys.3) | copy-start | bytes 786436
  339.3 3.7 %copy-start.19 = (bf16[128,1024]{1,0:T(8,128)(2,1)S(1)}, bf16[128,1024]{1,0:T(8,128)(2,1)}, u32[]{:S(2)}) copy-start(bf16[128,1024]{1,0:T(8,128)(2,1)} %values.3) | copy-start | bytes 786436
  347.5 1.0 copy-start.12

commit v4 on v3

--- a/solution.py
+++ b/solution.py
@@ -13,12 +13,14 @@
 SPLIT = (4, 8, 2)
 LANES = 128
 VMEM_LIMIT = 24 << 20
+VMEM_MOST = 61 << 20
 
 
 epsilon = 1e-06
 masked = -1e30
 VMEM = pl.BlockSpec(memory_space=pltpu.VMEM)
 SMEM = pl.BlockSpec(memory_space=pltpu.SMEM)
+ANY = pl.BlockSpec(memory_space=pl.ANY)
 
 
 def contract_last(left, right):
@@ -27,14 +29,14 @@
     )
 
 
-def call(body, outs, scratch, specs):
+def call(body, outs, scratch, specs, limit=VMEM_LIMIT):
     return pl.pallas_call(
         body,
         out_shape=outs,
         in_specs=specs,
         out_specs=jax.tree.map(lambda _: VMEM, outs),
         scratch_shapes=scratch,
-        compiler_params=pltpu.CompilerParams(vmem_limit_bytes=VMEM_LIMIT),
+        compiler_params=pltpu.CompilerParams(vmem_limit_bytes=limit),
     )
 
 
@@ -83,6 +85,7 @@
         shape_of(slots * parts, LANES),
         [pltpu.VMEM((tok * parts, LANES), jnp.float32)],
         [SMEM, SMEM, VMEM],
+        VMEM_MOST,
     )(dest, gate, grad)
 
 
@@ -164,6 +167,7 @@
             pltpu.VMEM((tok * parts, LANES), jnp.bfloat16),
         ],
         [SMEM, SMEM] + [VMEM] * (len(mine) + 3),
+        VMEM_MOST,
     )(dest, place, *mine, other, hidden, gain[None])
 
 
@@ -178,25 +182,34 @@
     to_rows(tiled, count, parts, put)
 
 
-def act_grad_kernel(place, source, *refs):
-    pieces, (out, gate_w, up_w, down_w, tiled, rows) = refs[:-6], refs[-6:]
-    count, depth = down_w.shape[0], down_w.shape[1]
+def fetch(place, pieces, kinds, targets, sems):
+    count, depth, _ = targets[0].shape
     half = depth // 2
     me = place[2]
-
-    def keep(piece, at, first, size):
-        row = pl.multiple_of(at * depth + first, half)
-        gate_w[pl.ds(row, size), :] = piece[0]
-        up_w[pl.ds(row, size), :] = piece[1]
-        down_w[at, first : first + size] = piece[2]
-
-    for n, piece in enumerate(pieces[:-2]):
-        turn = (n + 1) // 2
-        keep(piece, lax.rem(me + (turn if n % 2 == 0 else count - turn), count), 0, depth)
     opposite = lax.rem(me + count // 2, count)
-    keep(pieces[-2], opposite, 0, half)
-    keep(pieces[-1], opposite, half, half)
+    copies = []
+
+    def add(source, target):
+        copies.append(pltpu.make_async_copy(source, target, sems.at[len(copies)]))
+        copies[-1].start()
+
+    for kind, target in zip(kinds, targets):
+        for n, piece in enumerate(pieces[:-2]):
+            turn = (n + 1) // 2
+            at = lax.rem(me + (turn if n % 2 == 0 else count - turn), count)
+            add(piece.at[kind], target.at[at])
+        add(pieces[-2].at[kind], target.at[opposite, pl.ds(0, half)])
+        add(pieces[-1].at[kind], target.at[opposite, pl.ds(half, half)])
+    return copies
+
+
+def act_grad_kernel(place, source, *refs):
+    pieces, (out, tiled, rows, down_w, sems) = refs[:-5], refs[-5:]
+    copies = fetch(place, pieces, (2,), (down_w,), sems)
     load_rows(source, tiled, rows)
+    for copy in copies:
+        copy.wait()
+    count, depth, _ = down_w.shape
     for part in range(2):
         some = slice(part * depth, (part + 1) * depth)
         total = None
@@ -206,28 +219,42 @@
         out[:, some] = total
 
 
+def weight_scratch(pieces, width, kinds):
+    _, depth, hidden = pieces[0].shape
+    target = pltpu.VMEM((width // depth, depth, hidden), jnp.bfloat16)
+    return [target] * kinds + [pltpu.SemaphoreType.DMA((kinds * len(pieces),))]
+
+
 def act_grad_of(place, source, pieces, width):
     slots = source.shape[0] * LANES // width
-    _, depth, hidden = pieces[0].shape
+    hidden = pieces[0].shape[2]
     return call(
         act_grad_kernel,
-        (
-            shape_of(slots, hidden, jnp.float32),
-            shape_of(width, hidden),
-            shape_of(width, hidden),
-            jax.ShapeDtypeStruct((width // depth, depth, hidden), jnp.bfloat16),
-        ),
-        [pltpu.VMEM(source.shape, jnp.float32), pltpu.VMEM((slots, width), jnp.bfloat16)],
-        [SMEM, VMEM] + [VMEM] * len(pieces),
+        shape_of(slots, hidden, jnp.float32),
+        [pltpu.VMEM(source.shape, jnp.float32), pltpu.VMEM((slots, width), jnp.bfloat16)]
+        + weight_scratch(pieces, width, 1),
+        [SMEM, VMEM] + [ANY] * len(pieces),
+        VMEM_MOST,
     )(place, source, *pieces)
 
 
-def expert_kernel(source, gate_w, up_w, act_grad, in_grad, act, tiled, rows):
+def expert_kernel(place, source, act_grad, *refs):
+    pieces, (in_grad, act, tiled, rows, gate_w, up_w, sems) = refs[:-7], refs[-7:]
+    copies = fetch(place, pieces, (0, 1), (gate_w, up_w), sems)
     load_rows(source, tiled, rows)
+    for copy in copies[: len(pieces)]:
+        copy.wait()
     count, width = rows.shape
+    slices, depth, hidden = gate_w.shape
     values = rows[...]
-    pre_gate = jnp.dot(values, gate_w[...], preferred_element_type=jnp.float32)
-    pre_up = jnp.dot(values, up_w[...], preferred_element_type=jnp.float32)
+    pre_gate = jnp.dot(
+        values, gate_w[...].reshape(width, hidden), preferred_element_type=jnp.float32
+    )
+    for copy in copies[len(pieces) :]:
+        copy.wait()
+    pre_up = jnp.dot(
+        values, up_w[...].reshape(width, hidden), preferred_element_type=jnp.float32
+    )
     sig = jax.nn.sigmoid(pre_gate)
     silu = pre_gate * sig
     act[...] = (silu * pre_up).astype(jnp.bfloat16)
@@ -235,28 +262,32 @@
     gate_grad = (back * pre_up * sig * (1.0 + pre_gate * (1.0 - sig))).astype(jnp.bfloat16)
     up_grad = (back * silu).astype(jnp.bfloat16)
     parts = width // LANES
-    depth = 256
-    for d in range(0, width, depth):
-        entry = contract_last(gate_grad, gate_w[d : d + depth]) + contract_last(
-            up_grad, up_w[d : d + depth]
-        )
-        for p in range(depth // LANES):
-            tiled[pl.ds(d // LANES + p, count, stride=parts), :] = entry[:, lanes_of(p)]
+    each = depth // LANES
+    for d in range(slices):
+        entry = contract_last(gate_grad, gate_w[d]) + contract_last(up_grad, up_w[d])
+        for p in range(each):
+            tiled[pl.ds(d * each + p, count, stride=parts), :] = entry[:, lanes_of(p)]
     in_grad[...] = tiled[...].astype(jnp.bfloat16)
 
 
-def expert_back(source, gate_w, up_w, act_grad):
+def expert_back(place, source, act_grad, pieces):
     slots, hidden = act_grad.shape
-    width = gate_w.shape[0]
+    width = source.shape[0] * LANES // slots
     return call(
         expert_kernel,
         (shape_of(*source.shape), shape_of(slots, hidden)),
-        [pltpu.VMEM(source.shape, jnp.float32), pltpu.VMEM((slots, width), jnp.bfloat16)],
-        [VMEM] * 4,
-    )(source, gate_w, up_w, act_grad)
-
-
-def out_kernel(act, down, out, tiled):
+        [pltpu.VMEM(source.shape, jnp.float32), pltpu.VMEM((slots, width), jnp.bfloat16)]
+        + weight_scratch(pieces, width, 2),
+        [SMEM, VMEM, VMEM] + [ANY] * len(pieces),
+        VMEM_MOST,
+    )(place, source, act_grad, *pieces)
+
+
+def out_kernel(place, act, *refs):
+    pieces, (out, tiled, down, sems) = refs[:-4], refs[-4:]
+    copies = fetch(place, pieces, (2,), (down,), sems)
+    for copy in copies:
+        copy.wait()
     slices, depth, _ = down.shape
     count = act.shape[0]
     parts = slices * depth // LANES
@@ -272,12 +303,15 @@
     out[...] = tiled[...].astype(jnp.bfloat16)
 
 
-def expert_out(act, down):
-    slices, depth, _ = down.shape
-    rows = act.shape[0] * slices * depth // LANES
-    return call(
-        out_kernel, shape_of(rows, LANES), [pltpu.VMEM((rows, LANES), jnp.float32)], [VMEM, VMEM]
-    )(act, down)
+def expert_out(place, act, pieces, width):
+    rows = act.shape[0] * width // LANES
+    return call(
+        out_kernel,
+        shape_of(rows, LANES),
+        [pltpu.VMEM((rows, LANES), jnp.float32)] + weight_scratch(pieces, width, 1),
+        [SMEM, VMEM] + [ANY] * len(pieces),
+        VMEM_MOST,
+    )(place, act, *pieces)
 
 
 def resid_grad_kernel(dest, place, source, resid, gain, grad, *refs):
@@ -550,10 +584,10 @@
     )
     pieces = gather_pieces(near)
     recv_rows = exchange(rows)
-    act_grad, gate_full, up_full, down_full = act_grad_of(place, recv_grads, slices, width)
-    in_grad, act = expert_back(recv_rows, gate_full, up_full, act_grad)
+    act_grad = act_grad_of(place, recv_grads, slices, width)
+    in_grad, act = expert_back(place, recv_rows, act_grad, slices)
     back_grad = exchange(in_grad)
-    back_grad, out = lax.optimization_barrier((back_grad, expert_out(act, down_full)))
+    back_grad, out = lax.optimization_barrier((back_grad, expert_out(place, act, slices, width)))
     back_out = exchange(out)
     resid_grad, context_grad = resid_grad_of(
         dest, place, back_grad, resid, norm_gain, grad_out, pieces

time: 353 us -> 349 us (0.989)
  local copies, waits for them, and re-layouts: 23.9 us -> 8.95 us
  Pallas kernels: 31 us -> 42.3 us
  starting transfers between devices: 140 us -> 135 us
    ppermute x3, waiting for transfers between devices: 0.01 us -> 43.2 us  [ring_experts(): left = lax.ppermute(left, 'dp', ahead)]
    ppermute x3, waiting for transfers between devices: 42.4 us -> 0.01 us  [ring_experts(): right = lax.ppermute(right, 'dp', behind)]
    ppermute x4, starting transfers between devices: 27.8 us -> 11.9 us  [gather_pieces(): pieces += [part, lax.ppermute(part, 'core', [(0, 1), (1, 0)])]]
    ppermute x3, waiting for transfers between devices: 11.7 us -> 26.3 us  [gather_pieces(): lax.ppermute(near, 'x', [(i, (i + k) % xs) for i in range(xs)])]
    unnamed x63 -> x61, local copies, waits for them, and re-layouts: 20.7 us -> 6.2 us
    ppermute x6, waiting for transfers between devices: 38.8 us -> 32.5 us  [move_x(): return lax.ppermute(block, 'x', [(i, (i + turn) % xs) for i in range(xs)])]
    ppermute x6, starting transfers between devices: 16.8 us -> 21.4 us  [move_x(): return lax.ppermute(block, 'x', [(i, (i + turn) % xs) for i in range(xs)])]
    pallas_call x1, Pallas kernels: 5.27 us -> 9.15 us  [expert_back(): call(expert_kernel, (shape_of(*source.shape), shape_of(slots, hidden)), [...]
  transfers between devices with their start and end apart: 28 -> 28, of which waited for: 17 -> 16; matrix products, arithmetic and copies ran while one was open for 1% -> 1% of each run, Pallas kernels for 7% -> 9%
where the time goes in v4:
time: 349 us; the launch traced here: 348 us
  waiting for transfers between devices  157 us (45%)
  starting transfers between devices  135 us (39%)
  Pallas kernels  42.3 us (12%)
  local copies, waits for them, and re-layouts  8.95 us (3%)
    all_to_all x5, starting transfers between devices, spread(): return lax.all_to_all(rows, axes, split_axis=0, concat_axis=0, tiled=True)  58.7 us
    all_to_all x5, waiting for transfers between devices, spread(): return lax.all_to_all(rows, axes, split_axis=0, concat_axis=0, tiled=True)  46.5 us
    ppermute x3, waiting for transfers between devices, ring_experts(): left = lax.ppermute(left, 'dp', ahead)  43.2 us
    ppermute x6, waiting for transfers between devices, move_x(): return lax.ppermute(block, 'x', [(i, (i + turn) % xs) for i in range(xs)])  32.5 us
    ppermute x3, waiting for transfers between devices, gather_pieces(): lax.ppermute(near, 'x', [(i, (i + k) % xs) for i in range(xs)])  26.3 us
    ppermute x6, starting transfers between devices, move_x(): return lax.ppermute(block, 'x', [(i, (i + turn) % xs) for i in range(xs)])  21.4 us
    ppermute x3, starting transfers between devices, ring_experts(): right = lax.ppermute(right, 'dp', behind)  13.3 us
    ppermute x4, starting transfers between devices, gather_pieces(): pieces += [part, lax.ppermute(part, 'core', [(0, 1), (1, 0)])]  11.9 us
  transfers between devices with their start and end apart: 28, of which 16 were waited for; matrix products, arithmetic and copies ran while one was open for 1% of the time, Pallas kernels for 9%

profile of v4, /device:TPU:1, one launch (start us, length us, event | category | flops | bytes accessed | tf_op | source)
XLA Modules:
  0.0 347.5 jit_solution(14959374825880801565)
XLA Ops:
  0.7 1.6 broadcast_in_dim.8
  2.2 17.1 %all-to-all-start = ((bf16[64,32,128]{2,1,0:T(8,128)(2,1)}), bf16[64,32,128]{2,1,0:T(8,128)(2,1)S(1)}, u32[]{:S(2)}, u32[]{:S(2)}) async-start(bf16[64,32,128]{2,1,0:T(8,128)(2,1)} %broadcast_in_dim.8), calls=%async_computation | async-start | bytes 1048576 | tf_op jit(solution)/shard_map/all_to_all | solution.py:472
  19.8 0.7 div.10.gate
  20.7 0.6 convert_add_fusion.dest
  21.3 3.5 %shard_map.164 = bf16[6144,128]{1,0:T(8,128)(2,1)} custom-call(s32[256]{0:T(256)} %convert_add_fusion.dest, f32[256]{0:T(256)} %div.10.gate, bf16[128,2048]{1,0:T(8,128)(2,1)} %grad.3), custom_call_target="tpu_custom_call" | custom-call | tf_op jit(solution)/shard_map/pallas_call | solution.py:83
  24.8 12.0 %all-to-all-done = bf16[64,32,128]{2,1,0:T(8,128)(2,1)S(1)} async-done(((bf16[64,32,128]{2,1,0:T(8,128)(2,1)}), bf16[64,32,128]{2,1,0:T(8,128)(2,1)S(1)}, u32[]{:S(2)}, u32[]{:S(2)}) %all-to-all-start) | async-done | bytes 524320 | tf_op jit(solution)/shard_map/all_to_all | solution.py:472
  36.8 10.0 %all-to-all-start.2 = ((bf16[64,96,128]{2,1,0:T(8,128)(2,1)}), bf16[64,96,128]{2,1,0:T(8,128)(2,1)S(1)}, u32[]{:S(2)}, u32[]{:S(2)}) async-start(bf16[64,96,128]{2,1,0:T(8,128)(2,1)} %bitcast.38), calls=%async_computation.2 | async-start | bytes 3145728 | tf_op jit(solution)/shard_map/all_to_all | solution.py:472
  47.0 2.7 shard_map.165
  49.7 2.4 collective-permute-start
  52.0 1.1 collective-permute-done
  53.2 3.2 collective-permute-start.1
  56.4 4.5 %collective-permute-start.2 = (bf16[2,128,1024]{2,1,0:T(8,128)(2,1)S(1)}, bf16[2,128,1024]{2,1,0:T(8,128)(2,1)S(1)}, u32[]{:S(2)}, u32[]{:S(2)}) collective-permute-start(bf16[2,128,1024]{2,1,0:T(8,128)(2,1)S(1)} %pad_maximum_fusion.1.refs_0_), channel_id=1, source_target_pairs={{0,32},{16,48},{32,0},{48,16},{1,33},{17,49},{33,1},{49,17},{2,34}... | collective-permute-start | bytes 1572872 | tf_op jit(solution)/shard_map/ppermute | solution.py:500
  61.0 3.0 collective-permute-start.3
  63.9 14.8 %collective-permute-done.1.refs_1_ = bf16[2,128,1024]{2,1,0:T(8,128)(2,1)S(1)} collective-permute-done((bf16[2,128,1024]{2,1,0:T(8,128)(2,1)S(1)}, bf16[2,128,1024]{2,1,0:T(8,128)(2,1)S(1)}, u32[]{:S(2)}, u32[]{:S(2)}) %collective-permute-start.1) | collective-permute-done | bytes 524320 | tf_op jit(solution)/shard_map/ppermute | solution.py:500
  78.7 15.1 %collective-permute-done.2.refs_2_ = bf16[2,128,1024]{2,1,0:T(8,128)(2,1)S(1)} collective-permute-done((bf16[2,128,1024]{2,1,0:T(8,128)(2,1)S(1)}, bf16[2,128,1024]{2,1,0:T(8,128)(2,1)S(1)}, u32[]{:S(2)}, u32[]{:S(2)}) %collective-permute-start.2) | collective-permute-done | bytes 524320 | tf_op jit(solution)/shard_map/ppermute | solution.py:500
  93.8 1.5 shard_map.166
  95.3 4.4 %collective-permute-start.6 = (bf16[2,128,256]{2,1,0:T(8,128)(2,1)S(1)}, bf16[2,128,256]{2,1,0:T(8,128)(2,1)S(1)}, u32[]{:S(2)}, u32[]{:S(2)}) collective-permute-start(bf16[2,128,256]{2,1,0:T(8,128)(2,1)S(1)} %get-tuple-element.26), channel_id=1, source_target_pairs={{0,16},{16,32},{32,48},{48,0},{1,17},{17,33},{33,49},{49,1},{2,18}... | collective-permute-start | bytes 393224 | tf_op jit(solution)/shard_map/ppermute | solution.py:500
  99.7 3.4 collective-permute-start.5
  103.1 3.0 collective-permute-start.4
  106.1 1.3 collective-permute-done.5.refs_2_
  107.4 1.4 collective-permute-done.4.refs_1_
  108.8 0.7 copy-done.26
  109.5 4.1 %collective-permute-start.7 = (bf16[4,128,256]{2,1,0:T(8,128)(2,1)S(1)}, bf16[4,128,256]{2,1,0:T(8,128)(2,1)}, u32[]{:S(2)}, u32[]{:S(2)}) collective-permute-start(bf16[4,128,256]{2,1,0:T(8,128)(2,1)S(1)} %pad_maximum_fusion.2), channel_id=1, source_target_pairs={{0,1},{1,0},{2,3},{3,2},{4,5},{5,4},{6,7},{7,6},{8,9},{9,8},{10,11... | collective-permute-start | bytes 786440 | tf_op jit(solution)/shard_map/ppermute | solution.py:495
  114.2 0.7 collective-permute-done.7.refs_4_
  114.9 4.6 %shard_map.167 = (bf16[128,2048]{1,0:T(8,128)(2,1)}, bf16[6144,128]{1,0:T(8,128)(2,1)}) custom-call(s32[256]{0:T(256)} %convert_add_fusion.dest, s32[3]{0:T(128)} %pad_add_fusion.place, bf16[2,128,256]{2,1,0:T(8,128)(2,1)} %copy-done.10, bf16[2,128,256]{2,1,0:T(8,128)(2,1)} %copy-done.26, bf16[2,128,256]{2,1,0:T(8,128)(2,1)} %copy-done.25, ...), custom_call_target="tpu_custom_call" | custom-call | tf_op jit(solution)/shard_map/pallas_call | solution.py:162
  119.5 1.2 copy-done.23
  120.7 11.1 %all-to-all-start.1 = ((bf16[64,96,128]{2,1,0:T(8,128)(2,1)}), bf16[64,96,128]{2,1,0:T(8,128)(2,1)}, u32[]{:S(2)}, u32[]{:S(2)}) async-start(bf16[64,96,128]{2,1,0:T(8,128)(2,1)} %bitcast.41), calls=%async_computation.1 | async-start | bytes 3145728 | tf_op jit(solution)/shard_map/all_to_all | solution.py:472
  131.9 1.1 pad_maximum_fusion.refs_0_
  133.0 2.3 collective-permute-start.8
  135.3 4.2 %collective-permute-start.9 = (bf16[3,256,512]{2,1,0:T(8,128)(2,1)S(1)}, bf16[3,256,512]{2,1,0:T(8,128)(2,1)S(1)}, u32[]{:S(2)}, u32[]{:S(2)}) collective-permute-start(bf16[3,256,512]{2,1,0:T(8,128)(2,1)S(1)} %pad_maximum_fusion.refs_0_), channel_id=1, source_target_pairs={{0,448},{64,0},{128,64},{192,128},{256,192},{320,256},{384,320},{4... | collective-permute-start | bytes 2359304 | tf_op jit(solution)/shard_map/ppermute | solution.py:529
  139.5 15.3 %collective-permute-done.8.refs_1_ = bf16[3,256,512]{2,1,0:T(8,128)(2,1)S(1)} collective-permute-done((bf16[3,256,512]{2,1,0:T(8,128)(2,1)S(1)}, bf16[3,256,512]{2,1,0:T(8,128)(2,1)S(1)}, u32[]{:S(2)}, u32[]{:S(2)}) %collective-permute-start.8) | collective-permute-done | bytes 786464 | tf_op jit(solution)/shard_map/ppermute | solution.py:528
  154.8 1.9 collective-permute-start.10
  156.7 4.6 %collective-permute-start.11 = (bf16[3,256,512]{2,1,0:T(8,128)(2,1)S(1)}, bf16[3,256,512]{2,1,0:T(8,128)(2,1)S(1)}, u32[]{:S(2)}, u32[]{:S(2)}) collective-permute-start(bf16[3,256,512]{2,1,0:T(8,128)(2,1)S(1)} %collective-permute-done.9.refs_2_), channel_id=1, source_target_pairs={{0,448},{64,0},{128,64},{192,128},{256,192},{320,256},{384,320},{4... | collective-permute-start | bytes 2359304 | tf_op jit(solution)/shard_map/ppermute | solution.py:529
  161.3 14.4 %collective-permute-done.10.refs_3_ = bf16[3,256,512]{2,1,0:T(8,128)(2,1)S(1)} collective-permute-done((bf16[3,256,512]{2,1,0:T(8,128)(2,1)S(1)}, bf16[3,256,512]{2,1,0:T(8,128)(2,1)S(1)}, u32[]{:S(2)}, u32[]{:S(2)}) %collective-permute-start.10) | collective-permute-done | bytes 786464 | tf_op jit(solution)/shard_map/ppermute | solution.py:528
  175.7 1.9 collective-permute-start.12
  177.7 4.6 %collective-permute-start.13 = (bf16[3,256,512]{2,1,0:T(8,128)(2,1)S(1)}, bf16[3,256,512]{2,1,0:T(8,128)(2,1)S(1)}, u32[]{:S(2)}, u32[]{:S(2)}) collective-permute-start(bf16[3,256,512]{2,1,0:T(8,128)(2,1)S(1)} %collective-permute-done.11.refs_4_), channel_id=1, source_target_pairs={{0,448},{64,0},{128,64},{192,128},{256,192},{320,256},{384,320},{4... | collective-permute-start | bytes 2359304 | tf_op jit(solution)/shard_map/ppermute | solution.py:529
  182.2 13.5 %collective-permute-done.12.refs_5_ = bf16[3,256,512]{2,1,0:T(8,128)(2,1)S(1)} collective-permute-done((bf16[3,256,512]{2,1,0:T(8,128)(2,1)S(1)}, bf16[3,256,512]{2,1,0:T(8,128)(2,1)S(1)}, u32[]{:S(2)}, u32[]{:S(2)}) %collective-permute-start.12) | collective-permute-done | bytes 786464 | tf_op jit(solution)/shard_map/ppermute | solution.py:528
  195.8 1.9 collective-permute-start.14
  197.8 4.8 %collective-permute-start.15 = (bf16[3,128,512]{2,1,0:T(8,128)(2,1)S(1)}, bf16[3,128,512]{2,1,0:T(8,128)(2,1)}, u32[]{:S(2)}, u32[]{:S(2)}) collective-permute-start(bf16[3,128,512]{2,1,0:T(8,128)(2,1)S(1)} %slice.36), channel_id=1, source_target_pairs={{0,448},{64,0},{128,64},{192,128},{256,192},{320,256},{384,320},{4... | collective-permute-start | bytes 1179656 | tf_op jit(solution)/shard_map/ppermute | solution.py:532
  202.6 4.1 %collective-permute-done.14.refs_7_ = bf16[3,128,512]{2,1,0:T(8,128)(2,1)} collective-permute-done((bf16[3,128,512]{2,1,0:T(8,128)(2,1)S(1)}, bf16[3,128,512]{2,1,0:T(8,128)(2,1)}, u32[]{:S(2)}, u32[]{:S(2)}) %collective-permute-start.14) | collective-permute-done | bytes 393248 | tf_op jit(solution)/shard_map/ppermute | solution.py:531
  206.7 0.9 collective-permute-done.15.refs_8_
  207.6 5.1 %shard_map.168.act_grad = f32[384,512]{1,0:T(8,128)} custom-call(s32[3]{0:T(128)} %pad_add_fusion.place, bf16[6144,128]{1,0:T(8,128)(2,1)} %bitcast.40, bf16[3,256,512]{2,1,0:T(8,128)(2,1)} %copy-done.16, bf16[3,256,512]{2,1,0:T(8,128)(2,1)} %copy-done.19, bf16[3,256,512]{2,1,0:T(8,128)(2,1)} %copy-done.20, bf16[3,256,512]{2,1,0:T(8,128)(2,1)} %copy-done.21, ...), custom_call_target="tpu_custom_call" | custom-call | tf_op jit(solution)/shard_map/pallas_call | solution.py:231
  212.7 9.2 %shard_map.169 = (bf16[6144,128]{1,0:T(8,128)(2,1)}, bf16[384,512]{1,0:T(8,128)(2,1)}) custom-call(s32[3]{0:T(128)} %pad_add_fusion.place, bf16[6144,128]{1,0:T(8,128)(2,1)} %bitcast.11.source, f32[384,512]{1,0:T(8,128)} %shard_map.168.act_grad, bf16[3,256,512]{2,1,0:T(8,128)(2,1)} %copy-done.16, bf16[3,256,512]{2,1,0:T(8,128)(2,1)} %copy-done.19, ...), custom_call_target="tpu_custom_call" | custom-call | tf_op jit(solution)/shard_map/pallas_call | solution.py:276
  221.8 14.3 %all-to-all-start.3 = ((bf16[64,96,128]{2,1,0:T(8,128)(2,1)}), bf16[64,96,128]{2,1,0:T(8,128)(2,1)S(1)}, u32[]{:S(2)}, u32[]{:S(2)}) async-start(bf16[64,96,128]{2,1,0:T(8,128)(2,1)} %bitcast.42), calls=%async_computation.3 | async-start | bytes 3145728 | tf_op jit(solution)/shard_map/all_to_all | solution.py:472
  236.1 5.3 %shard_map.170 = bf16[6144,128]{1,0:T(8,128)(2,1)} custom-call(s32[3]{0:T(128)} %pad_add_fusion.place, bf16[384,512]{1,0:T(8,128)(2,1)} %get-tuple-element.30.act, bf16[3,256,512]{2,1,0:T(8,128)(2,1)} %copy-done.16, bf16[3,256,512]{2,1,0:T(8,128)(2,1)} %copy-done.19, bf16[3,256,512]{2,1,0:T(8,128)(2,1)} %copy-done.20, bf16[3,256,512]{2,1,0:T(8,128)(2,1)} %copy-done.21, ...), custom_call_target="tpu_custom_call" | custom-call | tf_op jit(solution)/shard_map/pallas_call | solution.py:308
  241.4 34.5 %all-to-all-done.3 = bf16[64,96,128]{2,1,0:T(8,128)(2,1)S(1)} async-done(((bf16[64,96,128]{2,1,0:T(8,128)(2,1)}), bf16[64,96,128]{2,1,0:T(8,128)(2,1)S(1)}, u32[]{:S(2)}, u32[]{:S(2)}) %all-to-all-start.3) | async-done | bytes 1572896 | tf_op jit(solution)/shard_map/all_to_all | solution.py:472
  275.9 6.2 %all-to-all-start.4 = ((bf16[64,96,128]{2,1,0:T(8,128)(2,1)}), bf16[64,96,128]{2,1,0:T(8,128)(2,1)S(1)}, u32[]{:S(2)}, u32[]{:S(2)}) async-start(bf16[64,96,128]{2,1,0:T(8,128)(2,1)} %bitcast.39), calls=%async_computation.4 | async-start | bytes 3145728 | tf_op jit(solution)/shard_map/all_to_all | solution.py:472
  282.1 3.3 collective-permute-start.17
  285.4 4.5 %collective-permute-start.19 = (bf16[8,8,32,128]{3,2,1,0:T(8,128)(2,1)}, bf16[8,8,32,128]{3,2,1,0:T(8,128)(2,1)S(1)}, u32[]{:S(2)}, u32[]{:S(2)}) collective-permute-start(bf16[8,8,32,128]{3,2,1,0:T(8,128)(2,1)} %bitcast.28), channel_id=1, source_target_pairs={{0,32},{16,48},{32,0},{48,16},{1,33},{17,49},{33,1},{49,17},{2,34}... | collective-permute-start | bytes 1572872 | tf_op jit(solution)/shard_map/ppermute | solution.py:485
  289.9 3.0 collective-permute-start.21
  292.9 3.1 collective-permute-start.16
  296.0 11.7 %collective-permute-done.17.refs_2_ = bf16[8,8,32,128]{3,2,1,0:T(8,128)(2,1)S(1)} collective-permute-done((bf16[8,8,32,128]{3,2,1,0:T(8,128)(2,1)}, bf16[8,8,32,128]{3,2,1,0:T(8,128)(2,1)S(1)}, u32[]{:S(2)}, u32[]{:S(2)}) %collective-permute-start.17) | collective-permute-done | bytes 524320 | tf_op jit(solution)/shard_map/ppermute | solution.py:485
  307.8 3.7 %collective-permute-start.18 = (bf16[8,8,32,128]{3,2,1,0:T(8,128)(2,1)S(1)}, bf16[8,8,32,128]{3,2,1,0:T(8,128)(2,1)S(1)}, u32[]{:S(2)}, u32[]{:S(2)}) collective-permute-start(bf16[8,8,32,128]{3,2,1,0:T(8,128)(2,1)S(1)} %collective-permute-done.17.refs_2_), channel_id=1, source_target_pairs={{0,1},{1,0},{2,3},{3,2},{4,5},{5,4},{6,7},{7,6},{8,9},{9,8},{10,11... | collective-permute-start | bytes 1572872 | tf_op jit(solution)/shard_map/ppermute | solution.py:490
  311.5 14.6 %collective-permute-done.19.refs_4_ = bf16[8,8,32,128]{3,2,1,0:T(8,128)(2,1)S(1)} collective-permute-done((bf16[8,8,32,128]{3,2,1,0:T(8,128)(2,1)}, bf16[8,8,32,128]{3,2,1,0:T(8,128)(2,1)S(1)}, u32[]{:S(2)}, u32[]{:S(2)}) %collective-permute-start.19) | collective-permute-done | bytes 524320 | tf_op jit(solution)/shard_map/ppermute | solution.py:485
  326.0 2.9 collective-permute-start.20
  328.9 2.1 collective-permute-start.22
  331.1 1.6 collective-permute-done.22.refs_7_
  332.8 1.0 copy-done.1
  333.8 1.0 copy-done.2
  334.8 1.0 copy-done.3
  335.9 3.6 %shard_map.172 = (bf16[128,2048]{1,0:T(8,128)(2,1)}, bf16[128,1024]{1,0:T(8,128)(2,1)S(1)}) custom-call(s32[256]{0:T(256)S(1)} %copy-done.12, s32[3]{0:T(128)S(1)} %copy-done.13, bf16[6144,128]{1,0:T(8,128)(2,1)S(1)} %bitcast.25, bf16[128,2048]{1,0:T(8,128)(2,1)S(1)} %copy-done.3, f32[1,2048]{1,0:T(1,128)S(1)} %bitcast.34, bf16[128,2048]{1,0:T(8,128)(2,1)S(1)} %copy-done.2, ...), custom_call_target="tpu_custom_call" | custom-call | tf_op jit(solution)/shard_map/pallas_call | solution.py:367
  339.5 4.5 %shard_map.173 = (bf16[128,1024]{1,0:T(8,128)(2,1)}, bf16[128,1024]{1,0:T(8,128)(2,1)}, bf16[128,1024]{1,0:T(8,128)(2,1)}) custom-call(s32[1,128]{1,0:T(1,128)S(1)} %bitcast.37, s32[128,1]{1,0:T(8,128)S(1)} %copy.22.seg_col, bf16[128,1024]{1,0:T(8,128)(2,1)S(1)} %copy-done.5, bf16[128,1024]{1,0:T(8,128)(2,1)S(1)} %copy-done.7, ...), custom_call_target="tpu_custom_call" | custom-call | tf_op jit(solution)/shard_map/pallas_call | solution.py:466
  344.0 1.0 copy-done.4
  345.1 2.4 shard_map.171
  (83 shorter events, 1.6 us)
Async XLA Ops:
  0.6 18.7 %copy-start.28 = (s32[128,2]{0,1:T(2,128)S(1)}, s32[128,2]{0,1:T(2,128)}, u32[]{:S(2)}) copy-start(s32[128,2]{0,1:T(2,128)} %param.23) | copy-start | bytes 3076
  0.6 19.0 %copy-start.29 = (s32[128,2]{0,1:T(2,128)S(1)}, s32[128,2]{0,1:T(2,128)}, u32[]{:S(2)}) copy-start(s32[128,2]{0,1:T(2,128)} %param.24) | copy-start | bytes 3076
  2.2 34.6 %all-to-all-start = ((bf16[64,32,128]{2,1,0:T(8,128)(2,1)}), bf16[64,32,128]{2,1,0:T(8,128)(2,1)S(1)}, u32[]{:S(2)}, u32[]{:S(2)}) async-start(bf16[64,32,128]{2,1,0:T(8,128)(2,1)} %broadcast_in_dim.8), calls=%async_computation | async-start | bytes 1048576 | tf_op jit(solution)/shard_map/all_to_all | solution.py:472
  36.8 82.7 %copy-start = (bf16[64,32,128]{2,1,0:T(8,128)(2,1)}, bf16[64,32,128]{2,1,0:T(8,128)(2,1)S(1)}, u32[]{:S(2)}) copy-start(bf16[64,32,128]{2,1,0:T(8,128)(2,1)S(1)} %all-to-all-done) | copy-start | bytes 1572868
  36.8 10.1 %copy-start.15 = (s32[128]{0:T(128)S(1)}, s32[128]{0:T(128)}, u32[]{:S(2)}) copy-start(s32[128]{0:T(128)} %param.17) | copy-start | bytes 1540
  36.8 10.2 %copy-start.5 = (bf16[128,1024]{1,0:T(8,128)(2,1)S(1)}, bf16[128,1024]{1,0:T(8,128)(2,1)}, u32[]{:S(2)}) copy-start(bf16[128,1024]{1,0:T(8,128)(2,1)} %queries.3) | copy-start | bytes 786436
  36.8 10.2 %copy-start.6 = (bf16[128,1024]{1,0:T(8,128)(2,1)S(1)}, bf16[128,1024]{1,0:T(8,128)(2,1)}, u32[]{:S(2)}) copy-start(bf16[128,1024]{1,0:T(8,128)(2,1)} %keys.3) | copy-start | bytes 786436
  36.8 10.2 %copy-start.8 = (bf16[128,1024]{1,0:T(8,128)(2,1)S(1)}, bf16[128,1024]{1,0:T(8,128)(2,1)}, u32[]{:S(2)}) copy-start(bf16[128,1024]{1,0:T(8,128)(2,1)} %values.3) | copy-start | bytes 786436
  36.8 82.7 %all-to-all-start.2 = ((bf16[64,96,128]{2,1,0:T(8,128)(2,1)}), bf16[64,96,128]{2,1,0:T(8,128)(2,1)S(1)}, u32[]{:S(2)}, u32[]{:S(2)}) async-start(bf16[64,96,128]{2,1,0:T(8,128)(2,1)} %bitcast.38), calls=%async_computation.2 | async-start | bytes 3145728 | tf_op jit(solution)/shard_map/all_to_all | solution.py:472
  49.7 3.5 %collective-permute-start = (bf16[128,1024]{1,0:T(8,128)(2,1)S(1)}, bf16[128,1024]{1,0:T(8,128)(2,1)S(1)}, u32[]{:S(2)}, u32[]{:S(2)}) collective-permute-start(bf16[128,1024]{1,0:T(8,128)(2,1)S(1)} %shard_map.165), channel_id=1, source_target_pairs={{0,1},{1,0},{2,3},{3,2},{4,5},{5,4},{6,7},{7,6},{8,9},{9,8},{10,11... | collective-permute-start | bytes 786440 | tf_op jit(solution)/shard_map/ppermute | solution.py:495
  53.2 25.5 %collective-permute-start.1 = (bf16[2,128,1024]{2,1,0:T(8,128)(2,1)S(1)}, bf16[2,128,1024]{2,1,0:T(8,128)(2,1)S(1)}, u32[]{:S(2)}, u32[]{:S(2)}) collective-permute-start(bf16[2,128,1024]{2,1,0:T(8,128)(2,1)S(1)} %pad_maximum_fusion.1.refs_0_), channel_id=1, source_target_pairs={{0,16},{16,32},{32,48},{48,0},{1,17},{17,33},{33,49},{49,1},{2,18}... | collective-permute-start | bytes 1572872 | tf_op jit(solution)/shard_map/ppermute | solution.py:500
  56.4 37.3 %collective-permute-start.2 = (bf16[2,128,1024]{2,1,0:T(8,128)(2,1)S(1)}, bf16[2,128,1024]{2,1,0:T(8,128)(2,1)S(1)}, u32[]{:S(2)}, u32[]{:S(2)}) collective-permute-start(bf16[2,128,1024]{2,1,0:T(8,128)(2,1)S(1)} %pad_maximum_fusion.1.refs_0_), channel_id=1, source_target_pairs={{0,32},{16,48},{32,0},{48,16},{1,33},{17,49},{33,1},{49,17},{2,34}... | collective-permute-start | bytes 1572872 | tf_op jit(solution)/shard_map/ppermute | solution.py:500
  61.0 32.8 %collective-permute-start.3 = (bf16[2,128,1024]{2,1,0:T(8,128)(2,1)S(1)}, bf16[2,128,1024]{2,1,0:T(8,128)(2,1)S(1)}, u32[]{:S(2)}, u32[]{:S(2)}) collective-permute-start(bf16[2,128,1024]{2,1,0:T(8,128)(2,1)S(1)} %pad_maximum_fusion.1.refs_0_), channel_id=1, source_target_pairs={{0,48},{16,0},{32,16},{48,32},{1,49},{17,1},{33,17},{49,33},{2,50}... | collective-permute-start | bytes 1572872 | tf_op jit(solution)/shard_map/ppermute | solution.py:500
  95.3 19.6 %copy-start.10 = (bf16[2,128,256]{2,1,0:T(8,128)(2,1)}, bf16[2,128,256]{2,1,0:T(8,128)(2,1)S(1)}, u32[]{:S(2)}) copy-start(bf16[2,128,256]{2,1,0:T(8,128)(2,1)S(1)} %get-tuple-element.23.refs_0_) | copy-start | bytes 393220
  95.3 10.8 %collective-permute-start.6 = (bf16[2,128,256]{2,1,0:T(8,128)(2,1)S(1)}, bf16[2,128,256]{2,1,0:T(8,128)(2,1)S(1)}, u32[]{:S(2)}, u32[]{:S(2)}) collective-permute-start(bf16[2,128,256]{2,1,0:T(8,128)(2,1)S(1)} %get-tuple-element.26), channel_id=1, source_target_pairs={{0,16},{16,32},{32,48},{48,0},{1,17},{17,33},{33,49},{49,1},{2,18}... | collective-permute-start | bytes 393224 | tf_op jit(solution)/shard_map/ppermute | solution.py:500
  99.7 7.6 %collective-permute-start.5 = (bf16[2,128,256]{2,1,0:T(8,128)(2,1)S(1)}, bf16[2,128,256]{2,1,0:T(8,128)(2,1)S(1)}, u32[]{:S(2)}, u32[]{:S(2)}) collective-permute-start(bf16[2,128,256]{2,1,0:T(8,128)(2,1)S(1)} %get-tuple-element.25), channel_id=1, source_target_pairs={{0,32},{16,48},{32,0},{48,16},{1,33},{17,49},{33,1},{49,17},{2,34}... | collective-permute-start | bytes 393224 | tf_op jit(solution)/shard_map/ppermute | solution.py:500
  103.1 5.7 %collective-permute-start.4 = (bf16[2,128,256]{2,1,0:T(8,128)(2,1)S(1)}, bf16[2,128,256]{2,1,0:T(8,128)(2,1)S(1)}, u32[]{:S(2)}, u32[]{:S(2)}) collective-permute-start(bf16[2,128,256]{2,1,0:T(8,128)(2,1)S(1)} %get-tuple-element.24), channel_id=1, source_target_pairs={{0,48},{16,0},{32,16},{48,32},{1,49},{17,1},{33,17},{49,33},{2,50}... | collective-permute-start | bytes 393224 | tf_op jit(solution)/shard_map/ppermute | solution.py:500
  106.1 8.8 %copy-start.24 = (bf16[2,128,256]{2,1,0:T(8,128)(2,1)}, bf16[2,128,256]{2,1,0:T(8,128)(2,1)S(1)}, u32[]{:S(2)}) copy-start(bf16[2,128,256]{2,1,0:T(8,128)(2,1)S(1)} %collective-permute-done.6.refs_3_) | copy-start | bytes 393220
  107.4 7.5 %copy-start.25 = (bf16[2,128,256]{2,1,0:T(8,128)(2,1)}, bf16[2,128,256]{2,1,0:T(8,128)(2,1)S(1)}, u32[]{:S(2)}) copy-start(bf16[2,128,256]{2,1,0:T(8,128)(2,1)S(1)} %collective-permute-done.5.refs_2_) | copy-start | bytes 393220
  108.8 0.7 copy-start.26
  109.5 5.4 %collective-permute-start.7 = (bf16[4,128,256]{2,1,0:T(8,128)(2,1)S(1)}, bf16[4,128,256]{2,1,0:T(8,128)(2,1)}, u32[]{:S(2)}, u32[]{:S(2)}) collective-permute-start(bf16[4,128,256]{2,1,0:T(8,128)(2,1)S(1)} %pad_maximum_fusion.2), channel_id=1, source_target_pairs={{0,1},{1,0},{2,3},{3,2},{4,5},{5,4},{6,7},{7,6},{8,9},{9,8},{10,11... | collective-permute-start | bytes 786440 | tf_op jit(solution)/shard_map/ppermute | solution.py:495
  119.5 1.2 copy-start.23
  119.5 12.3 %copy-start.27 = (bf16[1,512,256]{2,1,0:T(8,128)(2,1)S(1)}, bf16[1,512,256]{2,1,0:T(8,128)(2,1)}, u32[]{:S(2)}) copy-start(bf16[1,512,256]{2,1,0:T(8,128)(2,1)} %param.22) | copy-start | bytes 786436
  120.7 92.0 %all-to-all-start.1 = ((bf16[64,96,128]{2,1,0:T(8,128)(2,1)}), bf16[64,96,128]{2,1,0:T(8,128)(2,1)}, u32[]{:S(2)}, u32[]{:S(2)}) async-start(bf16[64,96,128]{2,1,0:T(8,128)(2,1)} %bitcast.41), calls=%async_computation.1 | async-start | bytes 3145728 | tf_op jit(solution)/shard_map/all_to_all | solution.py:472
  133.0 74.6 %copy-start.16 = (bf16[3,256,512]{2,1,0:T(8,128)(2,1)}, bf16[3,256,512]{2,1,0:T(8,128)(2,1)S(1)}, u32[]{:S(2)}) copy-start(bf16[3,256,512]{2,1,0:T(8,128)(2,1)S(1)} %pad_maximum_fusion.refs_0_) | copy-start | bytes 2359300
  133.0 21.8 %collective-permute-start.8 = (bf16[3,256,512]{2,1,0:T(8,128)(2,1)S(1)}, bf16[3,256,512]{2,1,0:T(8,128)(2,1)S(1)}, u32[]{:S(2)}, u32[]{:S(2)}) collective-permute-start(bf16[3,256,512]{2,1,0:T(8,128)(2,1)S(1)} %pad_maximum_fusion.refs_0_), channel_id=1, source_target_pairs={{0,64},{64,128},{128,192},{192,256},{256,320},{320,384},{384,448},... | collective-permute-start | bytes 2359304 | tf_op jit(solution)/shard_map/ppermute | solution.py:528
  135.3 21.4 %collective-permute-start.9 = (bf16[3,256,512]{2,1,0:T(8,128)(2,1)S(1)}, bf16[3,256,512]{2,1,0:T(8,128)(2,1)S(1)}, u32[]{:S(2)}, u32[]{:S(2)}) collective-permute-start(bf16[3,256,512]{2,1,0:T(8,128)(2,1)S(1)} %pad_maximum_fusion.refs_0_), channel_id=1, source_target_pairs={{0,448},{64,0},{128,64},{192,128},{256,192},{320,256},{384,320},{4... | collective-permute-start | bytes 2359304 | tf_op jit(solution)/shard_map/ppermute | solution.py:529
  154.8 6.5 %copy-start.19 = (bf16[3,256,512]{2,1,0:T(8,128)(2,1)}, bf16[3,256,512]{2,1,0:T(8,128)(2,1)S(1)}, u32[]{:S(2)}) copy-start(bf16[3,256,512]{2,1,0:T(8,128)(2,1)S(1)} %collective-permute-done.8.refs_1_) | copy-start | bytes 2359300
  154.8 20.9 %collective-permute-start.10 = (bf16[3,256,512]{2,1,0:T(8,128)(2,1)S(1)}, bf16[3,256,512]{2,1,0:T(8,128)(2,1)S(1)}, u32[]{:S(2)}, u32[]{:S(2)}) collective-permute-start(bf16[3,256,512]{2,1,0:T(8,128)(2,1)S(1)} %collective-permute-done.8.refs_1_), channel_id=1, source_target_pairs={{0,64},{64,128},{128,192},{192,256},{256,320},{320,384},{384,448},... | collective-permute-start | bytes 2359304 | tf_op jit(solution)/shard_map/ppermute | solution.py:528
  156.7 20.9 %copy-start.20 = (bf16[3,256,512]{2,1,0:T(8,128)(2,1)}, bf16[3,256,512]{2,1,0:T(8,128)(2,1)S(1)}, u32[]{:S(2)}) copy-start(bf16[3,256,512]{2,1,0:T(8,128)(2,1)S(1)} %collective-permute-done.9.refs_2_) | copy-start | bytes 2359300
  156.7 20.9 %collective-permute-start.11 = (bf16[3,256,512]{2,1,0:T(8,128)(2,1)S(1)}, bf16[3,256,512]{2,1,0:T(8,128)(2,1)S(1)}, u32[]{:S(2)}, u32[]{:S(2)}) collective-permute-start(bf16[3,256,512]{2,1,0:T(8,128)(2,1)S(1)} %collective-permute-done.9.refs_2_), channel_id=1, source_target_pairs={{0,448},{64,0},{128,64},{192,128},{256,192},{320,256},{384,320},{4... | collective-permute-start | bytes 2359304 | tf_op jit(solution)/shard_map/ppermute | solution.py:529
  175.7 1.9 copy-start.21
  175.7 20.1 %collective-permute-start.12 = (bf16[3,256,512]{2,1,0:T(8,128)(2,1)S(1)}, bf16[3,256,512]{2,1,0:T(8,128)(2,1)S(1)}, u32[]{:S(2)}, u32[]{:S(2)}) collective-permute-start(bf16[3,256,512]{2,1,0:T(8,128)(2,1)S(1)} %collective-permute-done.10.refs_3_), channel_id=1, source_target_pairs={{0,64},{64,128},{128,192},{192,256},{256,320},{320,384},{384,448},... | collective-permute-start | bytes 2359304 | tf_op jit(solution)/shard_map/ppermute | solution.py:528
  177.6 20.1 %copy-start.22 = (bf16[3,256,512]{2,1,0:T(8,128)(2,1)}, bf16[3,256,512]{2,1,0:T(8,128)(2,1)S(1)}, u32[]{:S(2)}) copy-start(bf16[3,256,512]{2,1,0:T(8,128)(2,1)S(1)} %collective-permute-done.11.refs_4_) | copy-start | bytes 2359300
  177.7 20.1 %collective-permute-start.13 = (bf16[3,256,512]{2,1,0:T(8,128)(2,1)S(1)}, bf16[3,256,512]{2,1,0:T(8,128)(2,1)S(1)}, u32[]{:S(2)}, u32[]{:S(2)}) collective-permute-start(bf16[3,256,512]{2,1,0:T(8,128)(2,1)S(1)} %collective-permute-done.11.refs_4_), channel_id=1, source_target_pairs={{0,448},{64,0},{128,64},{192,128},{256,192},{320,256},{384,320},{4... | collective-permute-start | bytes 2359304 | tf_op jit(solution)/shard_map/ppermute | solution.py:529
  195.8 11.8 %copy-start.17 = (bf16[3,256,512]{2,1,0:T(8,128)(2,1)}, bf16[3,256,512]{2,1,0:T(8,128)(2,1)S(1)}, u32[]{:S(2)}) copy-start(bf16[3,256,512]{2,1,0:T(8,128)(2,1)S(1)} %collective-permute-done.12.refs_5_) | copy-start | bytes 2359300
  195.8 10.9 %collective-permute-start.14 = (bf16[3,128,512]{2,1,0:T(8,128)(2,1)S(1)}, bf16[3,128,512]{2,1,0:T(8,128)(2,1)}, u32[]{:S(2)}, u32[]{:S(2)}) collective-permute-start(bf16[3,128,512]{2,1,0:T(8,128)(2,1)S(1)} %slice.35), channel_id=1, source_target_pairs={{0,64},{64,128},{128,192},{192,256},{256,320},{320,384},{384,448},... | collective-permute-start | bytes 1179656 | tf_op jit(solution)/shard_map/ppermute | solution.py:531
  197.7 9.8 %copy-start.18 = (bf16[3,256,512]{2,1,0:T(8,128)(2,1)}, bf16[3,256,512]{2,1,0:T(8,128)(2,1)S(1)}, u32[]{:S(2)}) copy-start(bf16[3,256,512]{2,1,0:T(8,128)(2,1)S(1)} %collective-permute-done.13.refs_6_) | copy-start | bytes 2359300
  197.8 9.8 %collective-permute-start.15 = (bf16[3,128,512]{2,1,0:T(8,128)(2,1)S(1)}, bf16[3,128,512]{2,1,0:T(8,128)(2,1)}, u32[]{:S(2)}, u32[]{:S(2)}) collective-permute-start(bf16[3,128,512]{2,1,0:T(8,128)(2,1)S(1)} %slice.36), channel_id=1, source_target_pairs={{0,448},{64,0},{128,64},{192,128},{256,192},{320,256},{384,320},{4... | collective-permute-start | bytes 1179656 | tf_op jit(solution)/shard_map/ppermute | solution.py:532
  221.8 54.0 %all-to-all-start.3 = ((bf16[64,96,128]{2,1,0:T(8,128)(2,1)}), bf16[64,96,128]{2,1,0:T(8,128)(2,1)S(1)}, u32[]{:S(2)}, u32[]{:S(2)}) async-start(bf16[64,96,128]{2,1,0:T(8,128)(2,1)} %bitcast.42), calls=%async_computation.3 | async-start | bytes 3145728 | tf_op jit(solution)/shard_map/all_to_all | solution.py:472
  275.9 56.9 %copy-start.11 = (f32[2048]{0:T(1024)S(1)}, f32[2048]{0:T(1024)}, u32[]{:S(2)}) copy-start(f32[2048]{0:T(1024)} %param.19) | copy-start | bytes 24580
  275.9 56.9 %copy-start.12 = (s32[256]{0:T(256)S(1)}, s32[256]{0:T(256)}, u32[]{:S(2)}) copy-start(s32[256]{0:T(256)} %convert_add_fusion.dest) | copy-start | bytes 3076
  275.9 56.9 %copy-start.13 = (s32[3]{0:T(128)S(1)}, s32[3]{0:T(128)}, u32[]{:S(2)}) copy-start(s32[3]{0:T(128)} %pad_add_fusion.place) | copy-start | bytes 40
  275.9 68.2 %all-to-all-start.4 = ((bf16[64,96,128]{2,1,0:T(8,128)(2,1)}), bf16[64,96,128]{2,1,0:T(8,128)(2,1)S(1)}, u32[]{:S(2)}, u32[]{:S(2)}) async-start(bf16[64,96,128]{2,1,0:T(8,128)(2,1)} %bitcast.39), calls=%async_computation.4 | async-start | bytes 3145728 | tf_op jit(solution)/shard_map/all_to_all | solution.py:472
  282.1 25.6 %collective-permute-start.17 = (bf16[8,8,32,128]{3,2,1,0:T(8,128)(2,1)}, bf16[8,8,32,128]{3,2,1,0:T(8,128)(2,1)S(1)}, u32[]{:S(2)}, u32[]{:S(2)}) collective-permute-start(bf16[8,8,32,128]{3,2,1,0:T(8,128)(2,1)} %bitcast.27), channel_id=1, source_target_pairs={{0,16},{16,32},{32,48},{48,0},{1,17},{17,33},{33,49},{49,1},{2,18}... | collective-permute-start | bytes 1572872 | tf_op jit(solution)/shard_map/ppermute | solution.py:485
  285.4 40.7 %collective-permute-start.19 = (bf16[8,8,32,128]{3,2,1,0:T(8,128)(2,1)}, bf16[8,8,32,128]{3,2,1,0:T(8,128)(2,1)S(1)}, u32[]{:S(2)}, u32[]{:S(2)}) collective-permute-start(bf16[8,8,32,128]{3,2,1,0:T(8,128)(2,1)} %bitcast.28), channel_id=1, source_target_pairs={{0,32},{16,48},{32,0},{48,16},{1,33},{17,49},{33,1},{49,17},{2,34}... | collective-permute-start | bytes 1572872 | tf_op jit(solution)/shard_map/ppermute | solution.py:485
  289.9 39.0 %collective-permute-start.21 = (bf16[8,8,32,128]{3,2,1,0:T(8,128)(2,1)}, bf16[8,8,32,128]{3,2,1,0:T(8,128)(2,1)S(1)}, u32[]{:S(2)}, u32[]{:S(2)}) collective-permute-start(bf16[8,8,32,128]{3,2,1,0:T(8,128)(2,1)} %bitcast.29), channel_id=1, source_target_pairs={{0,48},{16,0},{32,16},{48,32},{1,49},{17,1},{33,17},{49,33},{2,50}... | collective-permute-start | bytes 1572872 | tf_op jit(solution)/shard_map/ppermute | solution.py:485
  292.9 38.2 %collective-permute-start.16 = (bf16[8,8,32,128]{3,2,1,0:T(8,128)(2,1)}, bf16[8,8,32,128]{3,2,1,0:T(8,128)(2,1)S(1)}, u32[]{:S(2)}, u32[]{:S(2)}) collective-permute-start(bf16[8,8,32,128]{3,2,1,0:T(8,128)(2,1)} %bitcast.30), channel_id=1, source_target_pairs={{0,1},{1,0},{2,3},{3,2},{4,5},{5,4},{6,7},{7,6},{8,9},{9,8},{10,11... | collective-permute-start | bytes 1572872 | tf_op jit(solution)/shard_map/ppermute | solution.py:490
  307.8 23.4 %collective-permute-start.18 = (bf16[8,8,32,128]{3,2,1,0:T(8,128)(2,1)S(1)}, bf16[8,8,32,128]{3,2,1,0:T(8,128)(2,1)S(1)}, u32[]{:S(2)}, u32[]{:S(2)}) collective-permute-start(bf16[8,8,32,128]{3,2,1,0:T(8,128)(2,1)S(1)} %collective-permute-done.17.refs_2_), channel_id=1, source_target_pairs={{0,1},{1,0},{2,3},{3,2},{4,5},{5,4},{6,7},{7,6},{8,9},{9,8},{10,11... | collective-permute-start | bytes 1572872 | tf_op jit(solution)/shard_map/ppermute | solution.py:490
  326.0 5.1 %collective-permute-start.20 = (bf16[8,8,32,128]{3,2,1,0:T(8,128)(2,1)S(1)}, bf16[8,8,32,128]{3,2,1,0:T(8,128)(2,1)S(1)}, u32[]{:S(2)}, u32[]{:S(2)}) collective-permute-start(bf16[8,8,32,128]{3,2,1,0:T(8,128)(2,1)S(1)} %collective-permute-done.19.refs_4_), channel_id=1, source_target_pairs={{0,1},{1,0},{2,3},{3,2},{4,5},{5,4},{6,7},{7,6},{8,9},{9,8},{10,11... | collective-permute-start | bytes 1572872 | tf_op jit(solution)/shard_map/ppermute | solution.py:490
  328.9 3.8 %collective-permute-start.22 = (bf16[8,8,32,128]{3,2,1,0:T(8,128)(2,1)S(1)}, bf16[8,8,32,128]{3,2,1,0:T(8,128)(2,1)S(1)}, u32[]{:S(2)}, u32[]{:S(2)}) collective-permute-start(bf16[8,8,32,128]{3,2,1,0:T(8,128)(2,1)S(1)} %collective-permute-done.21.refs_6_), channel_id=1, source_target_pairs={{0,1},{1,0},{2,3},{3,2},{4,5},{5,4},{6,7},{7,6},{8,9},{9,8},{10,11... | collective-permute-start | bytes 1572872 | tf_op jit(solution)/shard_map/ppermute | solution.py:490
  332.8 1.0 copy-start.1
  333.8 1.0 copy-start.2
  334.8 1.0 copy-start.3
  335.9 3.6 %copy-start.7 = (bf16[128,1024]{1,0:T(8,128)(2,1)S(1)}, bf16[128,1024]{1,0:T(8,128)(2,1)}, u32[]{:S(2)}) copy-start(bf16[128,1024]{1,0:T(8,128)(2,1)} %keys.3) | copy-start | bytes 786436
  335.9 3.6 %copy-start.9 = (bf16[128,1024]{1,0:T(8,128)(2,1)S(1)}, bf16[128,1024]{1,0:T(8,128)(2,1)}, u32[]{:S(2)}) copy-start(bf16[128,1024]{1,0:T(8,128)(2,1)} %values.3) | copy-start | bytes 786436
  335.9 8.2 %copy-start.14 = (f32[256]{0:T(256)S(1)}, f32[256]{0:T(256)}, u32[]{:S(2)}) copy-start(f32[256]{0:T(256)} %div.10.gate) | copy-start | bytes 3076
  344.0 1.0 copy-start.4

commit v5 on v4

--- a/solution.py
+++ b/solution.py
@@ -182,33 +182,20 @@
     to_rows(tiled, count, parts, put)
 
 
-def fetch(place, pieces, kinds, targets, sems):
-    count, depth, _ = targets[0].shape
-    half = depth // 2
-    me = place[2]
-    opposite = lax.rem(me + count // 2, count)
-    copies = []
-
-    def add(source, target):
-        copies.append(pltpu.make_async_copy(source, target, sems.at[len(copies)]))
-        copies[-1].start()
-
-    for kind, target in zip(kinds, targets):
-        for n, piece in enumerate(pieces[:-2]):
-            turn = (n + 1) // 2
-            at = lax.rem(me + (turn if n % 2 == 0 else count - turn), count)
-            add(piece.at[kind], target.at[at])
-        add(pieces[-2].at[kind], target.at[opposite, pl.ds(0, half)])
-        add(pieces[-1].at[kind], target.at[opposite, pl.ds(half, half)])
+def fetch(weights, kinds, targets, sems):
+    copies = [
+        pltpu.make_async_copy(weights.at[:, kind], target, sems.at[n])
+        for n, (kind, target) in enumerate(zip(kinds, targets))
+    ]
+    for copy in copies:
+        copy.start()
     return copies
 
 
-def act_grad_kernel(place, source, *refs):
-    pieces, (out, tiled, rows, down_w, sems) = refs[:-5], refs[-5:]
-    copies = fetch(place, pieces, (2,), (down_w,), sems)
+def act_grad_kernel(source, weights, out, tiled, rows, down_w, sems):
+    (copy,) = fetch(weights, (2,), (down_w,), sems)
     load_rows(source, tiled, rows)
-    for copy in copies:
-        copy.wait()
+    copy.wait()
     count, depth, _ = down_w.shape
     for part in range(2):
         some = slice(part * depth, (part + 1) * depth)
@@ -219,39 +206,37 @@
         out[:, some] = total
 
 
-def weight_scratch(pieces, width, kinds):
-    _, depth, hidden = pieces[0].shape
-    target = pltpu.VMEM((width // depth, depth, hidden), jnp.bfloat16)
-    return [target] * kinds + [pltpu.SemaphoreType.DMA((kinds * len(pieces),))]
-
-
-def act_grad_of(place, source, pieces, width):
+def weight_scratch(weights, kinds):
+    slices, _, depth, hidden = weights.shape
+    target = pltpu.VMEM((slices, depth, hidden), jnp.bfloat16)
+    return [target] * kinds + [pltpu.SemaphoreType.DMA((kinds,))]
+
+
+def act_grad_of(source, weights, width):
     slots = source.shape[0] * LANES // width
-    hidden = pieces[0].shape[2]
     return call(
         act_grad_kernel,
-        shape_of(slots, hidden, jnp.float32),
+        shape_of(slots, weights.shape[3], jnp.float32),
         [pltpu.VMEM(source.shape, jnp.float32), pltpu.VMEM((slots, width), jnp.bfloat16)]
-        + weight_scratch(pieces, width, 1),
-        [SMEM, VMEM] + [ANY] * len(pieces),
+        + weight_scratch(weights, 1),
+        [VMEM, ANY],
         VMEM_MOST,
-    )(place, source, *pieces)
-
-
-def expert_kernel(place, source, act_grad, *refs):
-    pieces, (in_grad, act, tiled, rows, gate_w, up_w, sems) = refs[:-7], refs[-7:]
-    copies = fetch(place, pieces, (0, 1), (gate_w, up_w), sems)
+    )(source, weights)
+
+
+def expert_kernel(
+    source, act_grad, weights, in_grad, act, tiled, rows, gate_w, up_w, sems
+):
+    gate_copy, up_copy = fetch(weights, (0, 1), (gate_w, up_w), sems)
     load_rows(source, tiled, rows)
-    for copy in copies[: len(pieces)]:
-        copy.wait()
+    gate_copy.wait()
     count, width = rows.shape
     slices, depth, hidden = gate_w.shape
     values = rows[...]
     pre_gate = jnp.dot(
         values, gate_w[...].reshape(width, hidden), preferred_element_type=jnp.float32
     )
-    for copy in copies[len(pieces) :]:
-        copy.wait()
+    up_copy.wait()
     pre_up = jnp.dot(
         values, up_w[...].reshape(width, hidden), preferred_element_type=jnp.float32
     )
@@ -270,24 +255,22 @@
     in_grad[...] = tiled[...].astype(jnp.bfloat16)
 
 
-def expert_back(place, source, act_grad, pieces):
+def expert_back(source, act_grad, weights):
     slots, hidden = act_grad.shape
     width = source.shape[0] * LANES // slots
     return call(
         expert_kernel,
         (shape_of(*source.shape), shape_of(slots, hidden)),
         [pltpu.VMEM(source.shape, jnp.float32), pltpu.VMEM((slots, width), jnp.bfloat16)]
-        + weight_scratch(pieces, width, 2),
-        [SMEM, VMEM, VMEM] + [ANY] * len(pieces),
+        + weight_scratch(weights, 2),
+        [VMEM, VMEM, ANY],
         VMEM_MOST,
-    )(place, source, act_grad, *pieces)
-
-
-def out_kernel(place, act, *refs):
-    pieces, (out, tiled, down, sems) = refs[:-4], refs[-4:]
-    copies = fetch(place, pieces, (2,), (down,), sems)
-    for copy in copies:
-        copy.wait()
+    )(source, act_grad, weights)
+
+
+def out_kernel(act, weights, out, tiled, down, sems):
+    (copy,) = fetch(weights, (2,), (down,), sems)
+    copy.wait()
     slices, depth, _ = down.shape
     count = act.shape[0]
     parts = slices * depth // LANES
@@ -303,15 +286,15 @@
     out[...] = tiled[...].astype(jnp.bfloat16)
 
 
-def expert_out(place, act, pieces, width):
+def expert_out(act, weights, width):
     rows = act.shape[0] * width // LANES
     return call(
         out_kernel,
         shape_of(rows, LANES),
-        [pltpu.VMEM((rows, LANES), jnp.float32)] + weight_scratch(pieces, width, 1),
-        [SMEM, VMEM] + [ANY] * len(pieces),
+        [pltpu.VMEM((rows, LANES), jnp.float32)] + weight_scratch(weights, 1),
+        [VMEM, ANY],
         VMEM_MOST,
-    )(place, act, *pieces)
+    )(act, weights)
 
 
 def resid_grad_kernel(dest, place, source, resid, gain, grad, *refs):
@@ -512,25 +495,11 @@
     return mine, other
 
 
-def pack_experts(w_gate, w_up, w_down):
+def gather_experts(w_gate, w_up, w_down):
     rows = w_gate.shape[1]
     down = jnp.concatenate([w_down[0, :rows], w_down[0, rows:]], axis=1)
-    return jnp.stack([w_gate[0], w_up[0], down])
-
-
-def ring_experts(mine):
-    count, half = lax.axis_size("dp"), mine.shape[1] // 2
-    ahead = [(i, (i + 1) % count) for i in range(count)]
-    behind = [(i, (i - 1) % count) for i in range(count)]
-    left = right = mine
-    slices = [mine]
-    for _ in range(count // 2 - 1):
-        left = lax.ppermute(left, "dp", ahead)
-        right = lax.ppermute(right, "dp", behind)
-        slices += [left, right]
-    slices.append(lax.ppermute(left[:, :half], "dp", ahead))
-    slices.append(lax.ppermute(right[:, half:], "dp", behind))
-    return slices
+    mine = jnp.stack([w_gate[0], w_up[0], down])
+    return lax.all_gather(mine, "dp", axis=0, tiled=False)
 
 
 def slots_of(expert_ids, experts, capacity):
@@ -565,14 +534,14 @@
     capacity = 3 * tok // experts
     slots = experts * capacity
     lanes = (experts, capacity * width // LANES, LANES)
-    place = jnp.stack([lax.axis_index(axis) for axis in ("x", "core", "dp")]).astype(jnp.int32)
+    place = jnp.stack([lax.axis_index(axis) for axis in ("x", "core")]).astype(jnp.int32)
 
     def exchange(tiles):
         return spread(tiles.reshape(lanes), EXPERT).reshape(-1, LANES)
 
     gates = gate_fixed.reshape(-1).astype(jnp.float32) / 4096.0
     dest = slots_of(expert_ids, experts, capacity)
-    slices = ring_experts(pack_experts(w_gate, w_up, w_down))
+    weights = gather_experts(w_gate, w_up, w_down)
     to_send = send_grads(dest, gates, grad_out, slots)
     context = context_of(segment_ids, queries, keys, values)
     contexts = gather_contexts(context)
@@ -584,10 +553,10 @@
     )
     pieces = gather_pieces(near)
     recv_rows = exchange(rows)
-    act_grad = act_grad_of(place, recv_grads, slices, width)
-    in_grad, act = expert_back(place, recv_rows, act_grad, slices)
+    act_grad = act_grad_of(recv_grads, weights, width)
+    in_grad, act = expert_back(recv_rows, act_grad, weights)
     back_grad = exchange(in_grad)
-    back_grad, out = lax.optimization_barrier((back_grad, expert_out(place, act, slices, width)))
+    back_grad, out = lax.optimization_barrier((back_grad, expert_out(act, weights, width)))
     back_out = exchange(out)
     resid_grad, context_grad = resid_grad_of(
         dest, place, back_grad, resid, norm_gain, grad_out, pieces

time: 349 us -> 316 us (0.905)
  starting transfers between devices: 135 us -> 99.7 us
  between operations: 1.26 us -> 14.5 us
  waiting for transfers between devices: 157 us -> 146 us
    ppermute x8 -> x0, waiting for transfers between devices: 48.2 us -> none  [the longest x3 43.2 us: ring_experts(): left = lax.ppermute(left, 'dp', ahead)]
    all_to_all x5, waiting for transfers between devices: 46.5 us -> 81 us  [spread(): return lax.all_to_all(rows, axes, split_axis=0, concat_axis=0, tiled=True)]
    ppermute x8 -> x0, starting transfers between devices: 26.1 us -> none  [the longest x3 13.3 us: ring_experts(): right = lax.ppermute(right, 'dp', behind)]
    all_to_all x5, starting transfers between devices: 58.7 us -> 49.9 us  [spread(): return lax.all_to_all(rows, axes, split_axis=0, concat_axis=0, tiled=True)]
  transfers between devices with their start and end apart: 28 -> 21, of which waited for: 16 -> 12; matrix products, arithmetic and copies ran while one was open for 1% -> 1% of each run, Pallas kernels for 9% -> 10%
where the time goes in v5:
time: 316 us; the launch traced here: 315 us
  waiting for transfers between devices  146 us (46%)
  starting transfers between devices  99.7 us (32%)
  Pallas kernels  42.3 us (13%)
  between operations  14.5 us (5%)
  local copies, waits for them, and re-layouts  9.09 us (3%)
  other arithmetic  3.25 us (1%)
    all_to_all x5, waiting for transfers between devices, spread(): return lax.all_to_all(rows, axes, split_axis=0, concat_axis=0, tiled=True)  81 us
    all_to_all x5, starting transfers between devices, spread(): return lax.all_to_all(rows, axes, split_axis=0, concat_axis=0, tiled=True)  49.9 us
    ppermute x6, waiting for transfers between devices, move_x(): return lax.ppermute(block, 'x', [(i, (i + turn) % xs) for i in range(xs)])  34.9 us
    ppermute x3, waiting for transfers between devices, gather_pieces(): lax.ppermute(near, 'x', [(i, (i + k) % xs) for i in range(xs)])  26.3 us
    ppermute x6, starting transfers between devices, move_x(): return lax.ppermute(block, 'x', [(i, (i + turn) % xs) for i in range(xs)])  20.7 us
    ppermute x4, starting transfers between devices, gather_pieces(): pieces += [part, lax.ppermute(part, 'core', [(0, 1), (1, 0)])]  11.9 us
    ppermute x3, starting transfers between devices, gather_pieces(): lax.ppermute(near, 'x', [(i, (i + k) % xs) for i in range(xs)])  10.8 us
    pallas_call x1, Pallas kernels, expert_back(): call(expert_kernel, (shape_of(*source.shape), shape_of(slots, hidden)), [...  8.99 us
  transfers between devices with their start and end apart: 21, of which 12 were waited for; matrix products, arithmetic and copies ran while one was open for 1% of the time, Pallas kernels for 10%

profile of v5, /device:TPU:1, one launch (start us, length us, event | category | flops | bytes accessed | tf_op | source)
XLA Modules:
  0.0 314.7 jit_solution(5334048893238835957)
XLA Ops:
  7.2 0.0 all-gather.3.cloned.1.call-start
  7.2 1.0 slice_bitcast_fusion.1
  8.2 2.0 pad_maximum_fusion
  10.3 0.0 all-gather.3.cloned.1.call-update
  10.3 0.9 broadcast_in_dim.8
  11.2 17.1 %all-to-all-start = ((bf16[64,32,128]{2,1,0:T(8,128)(2,1)}), bf16[64,32,128]{2,1,0:T(8,128)(2,1)S(1)}, u32[]{:S(2)}, u32[]{:S(2)}) async-start(bf16[64,32,128]{2,1,0:T(8,128)(2,1)} %broadcast_in_dim.8), calls=%async_computation | async-start | bytes 1048576 | tf_op jit(solution)/shard_map/all_to_all | solution.py:455
  28.3 0.1 copy.24
  28.4 0.1 reshape.46
  28.6 0.1 copy.25
  28.7 0.7 div.10.gate
  29.4 0.2 fusion
  29.6 0.5 convert_add_fusion.dest
  30.2 3.6 %shard_map.164 = bf16[6144,128]{1,0:T(8,128)(2,1)} custom-call(s32[256]{0:T(256)} %convert_add_fusion.dest, f32[256]{0:T(256)} %div.10.gate, bf16[128,2048]{1,0:T(8,128)(2,1)} %grad.3), custom_call_target="tpu_custom_call" | custom-call | tf_op jit(solution)/shard_map/pallas_call | solution.py:83
  33.8 12.0 %all-to-all-done = bf16[64,32,128]{2,1,0:T(8,128)(2,1)S(1)} async-done(((bf16[64,32,128]{2,1,0:T(8,128)(2,1)}), bf16[64,32,128]{2,1,0:T(8,128)(2,1)S(1)}, u32[]{:S(2)}, u32[]{:S(2)}) %all-to-all-start) | async-done | bytes 524320 | tf_op jit(solution)/shard_map/all_to_all | solution.py:455
  45.8 0.0 copy-start.8
  45.8 10.8 %all-to-all-start.2 = ((bf16[64,96,128]{2,1,0:T(8,128)(2,1)}), bf16[64,96,128]{2,1,0:T(8,128)(2,1)S(1)}, u32[]{:S(2)}, u32[]{:S(2)}) async-start(bf16[64,96,128]{2,1,0:T(8,128)(2,1)} %bitcast.41), calls=%async_computation.2 | async-start | bytes 3145728 | tf_op jit(solution)/shard_map/all_to_all | solution.py:455
  56.6 0.1 copy.26.seg_col
  56.7 2.7 shard_map.165
  59.4 2.4 collective-permute-start
  61.8 1.1 collective-permute-done
  62.9 0.1 pad_maximum_fusion.1.refs_0_
  62.9 3.2 %collective-permute-start.1 = (bf16[2,128,1024]{2,1,0:T(8,128)(2,1)S(1)}, bf16[2,128,1024]{2,1,0:T(8,128)(2,1)S(1)}, u32[]{:S(2)}, u32[]{:S(2)}) collective-permute-start(bf16[2,128,1024]{2,1,0:T(8,128)(2,1)S(1)} %pad_maximum_fusion.1.refs_0_), channel_id=1, source_target_pairs={{0,16},{16,32},{32,48},{48,0},{1,17},{17,33},{33,49},{49,1},{2,18}... | collective-permute-start | bytes 1572872 | tf_op jit(solution)/shard_map/ppermute | solution.py:483
  66.2 4.5 %collective-permute-start.2 = (bf16[2,128,1024]{2,1,0:T(8,128)(2,1)S(1)}, bf16[2,128,1024]{2,1,0:T(8,128)(2,1)S(1)}, u32[]{:S(2)}, u32[]{:S(2)}) collective-permute-start(bf16[2,128,1024]{2,1,0:T(8,128)(2,1)S(1)} %pad_maximum_fusion.1.refs_0_), channel_id=1, source_target_pairs={{0,32},{16,48},{32,0},{48,16},{1,33},{17,49},{33,1},{49,17},{2,34}... | collective-permute-start | bytes 1572872 | tf_op jit(solution)/shard_map/ppermute | solution.py:483
  70.7 3.0 collective-permute-start.3
  73.7 14.9 %collective-permute-done.1.refs_1_ = bf16[2,128,1024]{2,1,0:T(8,128)(2,1)S(1)} collective-permute-done((bf16[2,128,1024]{2,1,0:T(8,128)(2,1)S(1)}, bf16[2,128,1024]{2,1,0:T(8,128)(2,1)S(1)}, u32[]{:S(2)}, u32[]{:S(2)}) %collective-permute-start.1) | collective-permute-done | bytes 524320 | tf_op jit(solution)/shard_map/ppermute | solution.py:483
  88.5 15.0 %collective-permute-done.2.refs_2_ = bf16[2,128,1024]{2,1,0:T(8,128)(2,1)S(1)} collective-permute-done((bf16[2,128,1024]{2,1,0:T(8,128)(2,1)S(1)}, bf16[2,128,1024]{2,1,0:T(8,128)(2,1)S(1)}, u32[]{:S(2)}, u32[]{:S(2)}) %collective-permute-start.2) | collective-permute-done | bytes 524320 | tf_op jit(solution)/shard_map/ppermute | solution.py:483
  103.5 1.5 shard_map.166
  105.0 4.7 %collective-permute-start.4 = (bf16[2,128,256]{2,1,0:T(8,128)(2,1)S(1)}, bf16[2,128,256]{2,1,0:T(8,128)(2,1)S(1)}, u32[]{:S(2)}, u32[]{:S(2)}) collective-permute-start(bf16[2,128,256]{2,1,0:T(8,128)(2,1)S(1)} %get-tuple-element.24), channel_id=1, source_target_pairs={{0,48},{16,0},{32,16},{48,32},{1,49},{17,1},{33,17},{49,33},{2,50}... | collective-permute-start | bytes 393224 | tf_op jit(solution)/shard_map/ppermute | solution.py:483
  109.7 3.4 %collective-permute-start.5 = (bf16[2,128,256]{2,1,0:T(8,128)(2,1)S(1)}, bf16[2,128,256]{2,1,0:T(8,128)(2,1)S(1)}, u32[]{:S(2)}, u32[]{:S(2)}) collective-permute-start(bf16[2,128,256]{2,1,0:T(8,128)(2,1)S(1)} %get-tuple-element.25), channel_id=1, source_target_pairs={{0,32},{16,48},{32,0},{48,16},{1,33},{17,49},{33,1},{49,17},{2,34}... | collective-permute-start | bytes 393224 | tf_op jit(solution)/shard_map/ppermute | solution.py:483
  113.2 1.9 collective-permute-start.6
  115.2 2.2 collective-permute-done.5.refs_2_
  117.4 2.8 collective-permute-done.6.refs_3_
  120.2 0.7 copy-done.19
  120.9 4.0 %collective-permute-start.7 = (bf16[4,128,256]{2,1,0:T(8,128)(2,1)S(1)}, bf16[4,128,256]{2,1,0:T(8,128)(2,1)}, u32[]{:S(2)}, u32[]{:S(2)}) collective-permute-start(bf16[4,128,256]{2,1,0:T(8,128)(2,1)S(1)} %pad_maximum_fusion.2), channel_id=1, source_target_pairs={{0,1},{1,0},{2,3},{3,2},{4,5},{5,4},{6,7},{7,6},{8,9},{9,8},{10,11... | collective-permute-start | bytes 786440 | tf_op jit(solution)/shard_map/ppermute | solution.py:478
  124.9 0.6 pad_add_fusion.place
  125.5 0.7 collective-permute-done.7.refs_4_
  126.2 4.6 %shard_map.167 = (bf16[128,2048]{1,0:T(8,128)(2,1)}, bf16[6144,128]{1,0:T(8,128)(2,1)}) custom-call(s32[256]{0:T(256)} %convert_add_fusion.dest, s32[2]{0:T(128)} %pad_add_fusion.place, bf16[2,128,256]{2,1,0:T(8,128)(2,1)} %copy-done.10, bf16[2,128,256]{2,1,0:T(8,128)(2,1)} %copy-done.17, bf16[2,128,256]{2,1,0:T(8,128)(2,1)} %copy-done.18, ...), custom_call_target="tpu_custom_call" | custom-call | tf_op jit(solution)/shard_map/pallas_call | solution.py:162
  130.8 1.1 copy-done.16
  131.9 9.7 %all-to-all-start.1 = ((bf16[64,96,128]{2,1,0:T(8,128)(2,1)}), bf16[64,96,128]{2,1,0:T(8,128)(2,1)}, u32[]{:S(2)}, u32[]{:S(2)}) async-start(bf16[64,96,128]{2,1,0:T(8,128)(2,1)} %bitcast.44), calls=%async_computation.1 | async-start | bytes 3145728 | tf_op jit(solution)/shard_map/all_to_all | solution.py:455
  141.6 0.0 all-gather.3.cloned.1.call-done
  141.7 5.0 %shard_map.168.act_grad = f32[384,512]{1,0:T(8,128)} custom-call(bf16[6144,128]{1,0:T(8,128)(2,1)} %bitcast.42, bf16[8,3,256,512]{3,2,1,0:T(8,128)(2,1)} %bitcast.38), custom_call_target="tpu_custom_call" | custom-call | tf_op jit(solution)/shard_map/pallas_call | solution.py:217
  146.7 34.6 %all-to-all-done.1 = bf16[64,96,128]{2,1,0:T(8,128)(2,1)} async-done(((bf16[64,96,128]{2,1,0:T(8,128)(2,1)}), bf16[64,96,128]{2,1,0:T(8,128)(2,1)}, u32[]{:S(2)}, u32[]{:S(2)}) %all-to-all-start.1) | async-done | bytes 1572896 | tf_op jit(solution)/shard_map/all_to_all | solution.py:455
  181.3 9.0 %shard_map.169 = (bf16[6144,128]{1,0:T(8,128)(2,1)}, bf16[384,512]{1,0:T(8,128)(2,1)}) custom-call(bf16[6144,128]{1,0:T(8,128)(2,1)} %bitcast.10.source, f32[384,512]{1,0:T(8,128)} %shard_map.168.act_grad, bf16[8,3,256,512]{3,2,1,0:T(8,128)(2,1)} %bitcast.39), custom_call_target="tpu_custom_call" | custom-call | tf_op jit(solution)/shard_map/pallas_call | solution.py:261
  190.3 6.1 %all-to-all-start.3 = ((bf16[64,96,128]{2,1,0:T(8,128)(2,1)}), bf16[64,96,128]{2,1,0:T(8,128)(2,1)S(1)}, u32[]{:S(2)}, u32[]{:S(2)}) async-start(bf16[64,96,128]{2,1,0:T(8,128)(2,1)} %bitcast.45), calls=%async_computation.3 | async-start | bytes 3145728 | tf_op jit(solution)/shard_map/all_to_all | solution.py:455
  196.4 5.3 %shard_map.170 = bf16[6144,128]{1,0:T(8,128)(2,1)} custom-call(bf16[384,512]{1,0:T(8,128)(2,1)} %get-tuple-element.30.act, bf16[8,3,256,512]{3,2,1,0:T(8,128)(2,1)} %bitcast.40), custom_call_target="tpu_custom_call" | custom-call | tf_op jit(solution)/shard_map/pallas_call | solution.py:291
  201.8 34.4 %all-to-all-done.3 = bf16[64,96,128]{2,1,0:T(8,128)(2,1)S(1)} async-done(((bf16[64,96,128]{2,1,0:T(8,128)(2,1)}), bf16[64,96,128]{2,1,0:T(8,128)(2,1)S(1)}, u32[]{:S(2)}, u32[]{:S(2)}) %all-to-all-start.3) | async-done | bytes 1572896 | tf_op jit(solution)/shard_map/all_to_all | solution.py:455
  236.2 6.2 %all-to-all-start.4 = ((bf16[64,96,128]{2,1,0:T(8,128)(2,1)}), bf16[64,96,128]{2,1,0:T(8,128)(2,1)S(1)}, u32[]{:S(2)}, u32[]{:S(2)}) async-start(bf16[64,96,128]{2,1,0:T(8,128)(2,1)} %bitcast.43), calls=%async_computation.4 | async-start | bytes 3145728 | tf_op jit(solution)/shard_map/all_to_all | solution.py:455
  242.4 3.3 %collective-permute-start.9 = (bf16[8,8,32,128]{3,2,1,0:T(8,128)(2,1)}, bf16[8,8,32,128]{3,2,1,0:T(8,128)(2,1)S(1)}, u32[]{:S(2)}, u32[]{:S(2)}) collective-permute-start(bf16[8,8,32,128]{3,2,1,0:T(8,128)(2,1)} %bitcast.27), channel_id=1, source_target_pairs={{0,16},{16,32},{32,48},{48,0},{1,17},{17,33},{33,49},{49,1},{2,18}... | collective-permute-start | bytes 1572872 | tf_op jit(solution)/shard_map/ppermute | solution.py:468
  245.7 4.5 %collective-permute-start.11 = (bf16[8,8,32,128]{3,2,1,0:T(8,128)(2,1)}, bf16[8,8,32,128]{3,2,1,0:T(8,128)(2,1)S(1)}, u32[]{:S(2)}, u32[]{:S(2)}) collective-permute-start(bf16[8,8,32,128]{3,2,1,0:T(8,128)(2,1)} %bitcast.28), channel_id=1, source_target_pairs={{0,32},{16,48},{32,0},{48,16},{1,33},{17,49},{33,1},{49,17},{2,34}... | collective-permute-start | bytes 1572872 | tf_op jit(solution)/shard_map/ppermute | solution.py:468
  250.2 3.0 collective-permute-start.13
  253.2 3.1 collective-permute-start.8
  256.4 11.7 %collective-permute-done.9.refs_2_ = bf16[8,8,32,128]{3,2,1,0:T(8,128)(2,1)S(1)} collective-permute-done((bf16[8,8,32,128]{3,2,1,0:T(8,128)(2,1)}, bf16[8,8,32,128]{3,2,1,0:T(8,128)(2,1)S(1)}, u32[]{:S(2)}, u32[]{:S(2)}) %collective-permute-start.9) | collective-permute-done | bytes 524320 | tf_op jit(solution)/shard_map/ppermute | solution.py:468
  268.1 3.7 %collective-permute-start.10 = (bf16[8,8,32,128]{3,2,1,0:T(8,128)(2,1)S(1)}, bf16[8,8,32,128]{3,2,1,0:T(8,128)(2,1)S(1)}, u32[]{:S(2)}, u32[]{:S(2)}) collective-permute-start(bf16[8,8,32,128]{3,2,1,0:T(8,128)(2,1)S(1)} %collective-permute-done.9.refs_2_), channel_id=1, source_target_pairs={{0,1},{1,0},{2,3},{3,2},{4,5},{5,4},{6,7},{7,6},{8,9},{9,8},{10,11... | collective-permute-start | bytes 1572872 | tf_op jit(solution)/shard_map/ppermute | solution.py:473
  271.8 14.6 %collective-permute-done.11.refs_4_ = bf16[8,8,32,128]{3,2,1,0:T(8,128)(2,1)S(1)} collective-permute-done((bf16[8,8,32,128]{3,2,1,0:T(8,128)(2,1)}, bf16[8,8,32,128]{3,2,1,0:T(8,128)(2,1)S(1)}, u32[]{:S(2)}, u32[]{:S(2)}) %collective-permute-start.11) | collective-permute-done | bytes 524320 | tf_op jit(solution)/shard_map/ppermute | solution.py:468
  286.4 2.9 collective-permute-start.12
  289.3 2.1 collective-permute-start.14
  291.4 1.6 collective-permute-done.14.refs_7_
  293.1 1.0 copy-done.1
  294.1 1.0 copy-done.2
  295.2 1.0 copy-done.3
  296.2 3.6 %shard_map.172 = (bf16[128,2048]{1,0:T(8,128)(2,1)}, bf16[128,1024]{1,0:T(8,128)(2,1)S(1)}) custom-call(s32[256]{0:T(256)S(1)} %copy-done.12, s32[2]{0:T(128)S(1)} %copy-done.15, bf16[6144,128]{1,0:T(8,128)(2,1)S(1)} %bitcast.25, bf16[128,2048]{1,0:T(8,128)(2,1)S(1)} %copy-done.3, f32[1,2048]{1,0:T(1,128)S(1)} %bitcast.34, bf16[128,2048]{1,0:T(8,128)(2,1)S(1)} %copy-done.2, ...), custom_call_target="tpu_custom_call" | custom-call | tf_op jit(solution)/shard_map/pallas_call | solution.py:350
  299.9 4.5 %shard_map.173 = (bf16[128,1024]{1,0:T(8,128)(2,1)}, bf16[128,1024]{1,0:T(8,128)(2,1)}, bf16[128,1024]{1,0:T(8,128)(2,1)}) custom-call(s32[1,128]{1,0:T(1,128)S(1)} %bitcast.37, s32[128,1]{1,0:T(8,128)S(1)} %copy.26.seg_col, bf16[128,1024]{1,0:T(8,128)(2,1)S(1)} %copy-done.5, bf16[128,1024]{1,0:T(8,128)(2,1)S(1)} %copy-done.7, ...), custom_call_target="tpu_custom_call" | custom-call | tf_op jit(solution)/shard_map/pallas_call | solution.py:449
  304.4 1.0 copy-done.4
  305.4 2.4 shard_map.171
  (54 shorter events, 0.2 us)
Async XLA Ops:
  7.2 134.5 %all-gather.3.cloned.1.call-start = ((), (), s32[]{:S(2)}) async-start(), calls=%async_computation.5 | async-start | bytes 7077888 | tf_op jit(solution)/shard_map/all_gather | solution.py:502
  8.2 2.1 copy-start.20
  10.3 18.0 %copy-start.21 = (s32[128,2]{0,1:T(2,128)S(1)}, s32[128,2]{0,1:T(2,128)}, u32[]{:S(2)}) copy-start(s32[128,2]{0,1:T(2,128)} %param.23) | copy-start | bytes 3076
  10.3 18.3 %copy-start.22 = (s32[128,2]{0,1:T(2,128)S(1)}, s32[128,2]{0,1:T(2,128)}, u32[]{:S(2)}) copy-start(s32[128,2]{0,1:T(2,128)} %param.24) | copy-start | bytes 3076
  11.2 34.6 %all-to-all-start = ((bf16[64,32,128]{2,1,0:T(8,128)(2,1)}), bf16[64,32,128]{2,1,0:T(8,128)(2,1)S(1)}, u32[]{:S(2)}, u32[]{:S(2)}) async-start(bf16[64,32,128]{2,1,0:T(8,128)(2,1)} %broadcast_in_dim.8), calls=%async_computation | async-start | bytes 1048576 | tf_op jit(solution)/shard_map/all_to_all | solution.py:455
  45.8 85.0 %copy-start = (bf16[64,32,128]{2,1,0:T(8,128)(2,1)}, bf16[64,32,128]{2,1,0:T(8,128)(2,1)S(1)}, u32[]{:S(2)}) copy-start(bf16[64,32,128]{2,1,0:T(8,128)(2,1)S(1)} %all-to-all-done) | copy-start | bytes 1572868
  45.8 10.8 %copy-start.14 = (s32[128]{0:T(128)S(1)}, s32[128]{0:T(128)}, u32[]{:S(2)}) copy-start(s32[128]{0:T(128)} %param.17) | copy-start | bytes 1540
  45.8 10.9 %copy-start.5 = (bf16[128,1024]{1,0:T(8,128)(2,1)S(1)}, bf16[128,1024]{1,0:T(8,128)(2,1)}, u32[]{:S(2)}) copy-start(bf16[128,1024]{1,0:T(8,128)(2,1)} %queries.3) | copy-start | bytes 786436
  45.8 10.9 %copy-start.6 = (bf16[128,1024]{1,0:T(8,128)(2,1)S(1)}, bf16[128,1024]{1,0:T(8,128)(2,1)}, u32[]{:S(2)}) copy-start(bf16[128,1024]{1,0:T(8,128)(2,1)} %keys.3) | copy-start | bytes 786436
  45.8 10.9 %copy-start.8 = (bf16[128,1024]{1,0:T(8,128)(2,1)S(1)}, bf16[128,1024]{1,0:T(8,128)(2,1)}, u32[]{:S(2)}) copy-start(bf16[128,1024]{1,0:T(8,128)(2,1)} %values.3) | copy-start | bytes 786436
  45.8 85.0 %all-to-all-start.2 = ((bf16[64,96,128]{2,1,0:T(8,128)(2,1)}), bf16[64,96,128]{2,1,0:T(8,128)(2,1)S(1)}, u32[]{:S(2)}, u32[]{:S(2)}) async-start(bf16[64,96,128]{2,1,0:T(8,128)(2,1)} %bitcast.41), calls=%async_computation.2 | async-start | bytes 3145728 | tf_op jit(solution)/shard_map/all_to_all | solution.py:455
  59.4 3.5 %collective-permute-start = (bf16[128,1024]{1,0:T(8,128)(2,1)S(1)}, bf16[128,1024]{1,0:T(8,128)(2,1)S(1)}, u32[]{:S(2)}, u32[]{:S(2)}) collective-permute-start(bf16[128,1024]{1,0:T(8,128)(2,1)S(1)} %shard_map.165), channel_id=1, source_target_pairs={{0,1},{1,0},{2,3},{3,2},{4,5},{5,4},{6,7},{7,6},{8,9},{9,8},{10,11... | collective-permute-start | bytes 786440 | tf_op jit(solution)/shard_map/ppermute | solution.py:478
  62.9 25.6 %collective-permute-start.1 = (bf16[2,128,1024]{2,1,0:T(8,128)(2,1)S(1)}, bf16[2,128,1024]{2,1,0:T(8,128)(2,1)S(1)}, u32[]{:S(2)}, u32[]{:S(2)}) collective-permute-start(bf16[2,128,1024]{2,1,0:T(8,128)(2,1)S(1)} %pad_maximum_fusion.1.refs_0_), channel_id=1, source_target_pairs={{0,16},{16,32},{32,48},{48,0},{1,17},{17,33},{33,49},{49,1},{2,18}... | collective-permute-start | bytes 1572872 | tf_op jit(solution)/shard_map/ppermute | solution.py:483
  66.2 37.4 %collective-permute-start.2 = (bf16[2,128,1024]{2,1,0:T(8,128)(2,1)S(1)}, bf16[2,128,1024]{2,1,0:T(8,128)(2,1)S(1)}, u32[]{:S(2)}, u32[]{:S(2)}) collective-permute-start(bf16[2,128,1024]{2,1,0:T(8,128)(2,1)S(1)} %pad_maximum_fusion.1.refs_0_), channel_id=1, source_target_pairs={{0,32},{16,48},{32,0},{48,16},{1,33},{17,49},{33,1},{49,17},{2,34}... | collective-permute-start | bytes 1572872 | tf_op jit(solution)/shard_map/ppermute | solution.py:483
  70.7 32.8 %collective-permute-start.3 = (bf16[2,128,1024]{2,1,0:T(8,128)(2,1)S(1)}, bf16[2,128,1024]{2,1,0:T(8,128)(2,1)S(1)}, u32[]{:S(2)}, u32[]{:S(2)}) collective-permute-start(bf16[2,128,1024]{2,1,0:T(8,128)(2,1)S(1)} %pad_maximum_fusion.1.refs_0_), channel_id=1, source_target_pairs={{0,48},{16,0},{32,16},{48,32},{1,49},{17,1},{33,17},{49,33},{2,50}... | collective-permute-start | bytes 1572872 | tf_op jit(solution)/shard_map/ppermute | solution.py:483
  105.0 21.2 %copy-start.10 = (bf16[2,128,256]{2,1,0:T(8,128)(2,1)}, bf16[2,128,256]{2,1,0:T(8,128)(2,1)S(1)}, u32[]{:S(2)}) copy-start(bf16[2,128,256]{2,1,0:T(8,128)(2,1)S(1)} %get-tuple-element.23.refs_0_) | copy-start | bytes 393220
  105.0 10.1 %collective-permute-start.4 = (bf16[2,128,256]{2,1,0:T(8,128)(2,1)S(1)}, bf16[2,128,256]{2,1,0:T(8,128)(2,1)S(1)}, u32[]{:S(2)}, u32[]{:S(2)}) collective-permute-start(bf16[2,128,256]{2,1,0:T(8,128)(2,1)S(1)} %get-tuple-element.24), channel_id=1, source_target_pairs={{0,48},{16,0},{32,16},{48,32},{1,49},{17,1},{33,17},{49,33},{2,50}... | collective-permute-start | bytes 393224 | tf_op jit(solution)/shard_map/ppermute | solution.py:483
  109.7 7.7 %collective-permute-start.5 = (bf16[2,128,256]{2,1,0:T(8,128)(2,1)S(1)}, bf16[2,128,256]{2,1,0:T(8,128)(2,1)S(1)}, u32[]{:S(2)}, u32[]{:S(2)}) collective-permute-start(bf16[2,128,256]{2,1,0:T(8,128)(2,1)S(1)} %get-tuple-element.25), channel_id=1, source_target_pairs={{0,32},{16,48},{32,0},{48,16},{1,33},{17,49},{33,1},{49,17},{2,34}... | collective-permute-start | bytes 393224 | tf_op jit(solution)/shard_map/ppermute | solution.py:483
  113.2 7.0 %collective-permute-start.6 = (bf16[2,128,256]{2,1,0:T(8,128)(2,1)S(1)}, bf16[2,128,256]{2,1,0:T(8,128)(2,1)S(1)}, u32[]{:S(2)}, u32[]{:S(2)}) collective-permute-start(bf16[2,128,256]{2,1,0:T(8,128)(2,1)S(1)} %get-tuple-element.26), channel_id=1, source_target_pairs={{0,16},{16,32},{32,48},{48,0},{1,17},{17,33},{33,49},{49,1},{2,18}... | collective-permute-start | bytes 393224 | tf_op jit(solution)/shard_map/ppermute | solution.py:483
  115.1 11.1 %copy-start.17 = (bf16[2,128,256]{2,1,0:T(8,128)(2,1)}, bf16[2,128,256]{2,1,0:T(8,128)(2,1)S(1)}, u32[]{:S(2)}) copy-start(bf16[2,128,256]{2,1,0:T(8,128)(2,1)S(1)} %collective-permute-done.4.refs_1_) | copy-start | bytes 393220
  117.4 8.8 %copy-start.18 = (bf16[2,128,256]{2,1,0:T(8,128)(2,1)}, bf16[2,128,256]{2,1,0:T(8,128)(2,1)S(1)}, u32[]{:S(2)}) copy-start(bf16[2,128,256]{2,1,0:T(8,128)(2,1)S(1)} %collective-permute-done.5.refs_2_) | copy-start | bytes 393220
  120.2 0.7 copy-start.19
  120.9 5.3 %collective-permute-start.7 = (bf16[4,128,256]{2,1,0:T(8,128)(2,1)S(1)}, bf16[4,128,256]{2,1,0:T(8,128)(2,1)}, u32[]{:S(2)}, u32[]{:S(2)}) collective-permute-start(bf16[4,128,256]{2,1,0:T(8,128)(2,1)S(1)} %pad_maximum_fusion.2), channel_id=1, source_target_pairs={{0,1},{1,0},{2,3},{3,2},{4,5},{5,4},{6,7},{7,6},{8,9},{9,8},{10,11... | collective-permute-start | bytes 786440 | tf_op jit(solution)/shard_map/ppermute | solution.py:478
  130.8 1.1 copy-start.16
  131.9 49.4 %all-to-all-start.1 = ((bf16[64,96,128]{2,1,0:T(8,128)(2,1)}), bf16[64,96,128]{2,1,0:T(8,128)(2,1)}, u32[]{:S(2)}, u32[]{:S(2)}) async-start(bf16[64,96,128]{2,1,0:T(8,128)(2,1)} %bitcast.44), calls=%async_computation.1 | async-start | bytes 3145728 | tf_op jit(solution)/shard_map/all_to_all | solution.py:455
  190.3 45.9 %all-to-all-start.3 = ((bf16[64,96,128]{2,1,0:T(8,128)(2,1)}), bf16[64,96,128]{2,1,0:T(8,128)(2,1)S(1)}, u32[]{:S(2)}, u32[]{:S(2)}) async-start(bf16[64,96,128]{2,1,0:T(8,128)(2,1)} %bitcast.45), calls=%async_computation.3 | async-start | bytes 3145728 | tf_op jit(solution)/shard_map/all_to_all | solution.py:455
  236.2 56.9 %copy-start.11 = (f32[2048]{0:T(1024)S(1)}, f32[2048]{0:T(1024)}, u32[]{:S(2)}) copy-start(f32[2048]{0:T(1024)} %param.19) | copy-start | bytes 24580
  236.2 56.9 %copy-start.12 = (s32[256]{0:T(256)S(1)}, s32[256]{0:T(256)}, u32[]{:S(2)}) copy-start(s32[256]{0:T(256)} %convert_add_fusion.dest) | copy-start | bytes 3076
  236.2 56.9 %copy-start.15 = (s32[2]{0:T(128)S(1)}, s32[2]{0:T(128)}, u32[]{:S(2)}) copy-start(s32[2]{0:T(128)} %pad_add_fusion.place) | copy-start | bytes 28
  236.2 68.2 %all-to-all-start.4 = ((bf16[64,96,128]{2,1,0:T(8,128)(2,1)}), bf16[64,96,128]{2,1,0:T(8,128)(2,1)S(1)}, u32[]{:S(2)}, u32[]{:S(2)}) async-start(bf16[64,96,128]{2,1,0:T(8,128)(2,1)} %bitcast.43), calls=%async_computation.4 | async-start | bytes 3145728 | tf_op jit(solution)/shard_map/all_to_all | solution.py:455
  242.4 25.6 %collective-permute-start.9 = (bf16[8,8,32,128]{3,2,1,0:T(8,128)(2,1)}, bf16[8,8,32,128]{3,2,1,0:T(8,128)(2,1)S(1)}, u32[]{:S(2)}, u32[]{:S(2)}) collective-permute-start(bf16[8,8,32,128]{3,2,1,0:T(8,128)(2,1)} %bitcast.27), channel_id=1, source_target_pairs={{0,16},{16,32},{32,48},{48,0},{1,17},{17,33},{33,49},{49,1},{2,18}... | collective-permute-start | bytes 1572872 | tf_op jit(solution)/shard_map/ppermute | solution.py:468
  245.7 40.7 %collective-permute-start.11 = (bf16[8,8,32,128]{3,2,1,0:T(8,128)(2,1)}, bf16[8,8,32,128]{3,2,1,0:T(8,128)(2,1)S(1)}, u32[]{:S(2)}, u32[]{:S(2)}) collective-permute-start(bf16[8,8,32,128]{3,2,1,0:T(8,128)(2,1)} %bitcast.28), channel_id=1, source_target_pairs={{0,32},{16,48},{32,0},{48,16},{1,33},{17,49},{33,1},{49,17},{2,34}... | collective-permute-start | bytes 1572872 | tf_op jit(solution)/shard_map/ppermute | solution.py:468
  250.2 39.0 %collective-permute-start.13 = (bf16[8,8,32,128]{3,2,1,0:T(8,128)(2,1)}, bf16[8,8,32,128]{3,2,1,0:T(8,128)(2,1)S(1)}, u32[]{:S(2)}, u32[]{:S(2)}) collective-permute-start(bf16[8,8,32,128]{3,2,1,0:T(8,128)(2,1)} %bitcast.29), channel_id=1, source_target_pairs={{0,48},{16,0},{32,16},{48,32},{1,49},{17,1},{33,17},{49,33},{2,50}... | collective-permute-start | bytes 1572872 | tf_op jit(solution)/shard_map/ppermute | solution.py:468
  253.2 38.2 %collective-permute-start.8 = (bf16[8,8,32,128]{3,2,1,0:T(8,128)(2,1)}, bf16[8,8,32,128]{3,2,1,0:T(8,128)(2,1)S(1)}, u32[]{:S(2)}, u32[]{:S(2)}) collective-permute-start(bf16[8,8,32,128]{3,2,1,0:T(8,128)(2,1)} %bitcast.30), channel_id=1, source_target_pairs={{0,1},{1,0},{2,3},{3,2},{4,5},{5,4},{6,7},{7,6},{8,9},{9,8},{10,11... | collective-permute-start | bytes 1572872 | tf_op jit(solution)/shard_map/ppermute | solution.py:473
  268.1 23.4 %collective-permute-start.10 = (bf16[8,8,32,128]{3,2,1,0:T(8,128)(2,1)S(1)}, bf16[8,8,32,128]{3,2,1,0:T(8,128)(2,1)S(1)}, u32[]{:S(2)}, u32[]{:S(2)}) collective-permute-start(bf16[8,8,32,128]{3,2,1,0:T(8,128)(2,1)S(1)} %collective-permute-done.9.refs_2_), channel_id=1, source_target_pairs={{0,1},{1,0},{2,3},{3,2},{4,5},{5,4},{6,7},{7,6},{8,9},{9,8},{10,11... | collective-permute-start | bytes 1572872 | tf_op jit(solution)/shard_map/ppermute | solution.py:473
  286.4 5.1 %collective-permute-start.12 = (bf16[8,8,32,128]{3,2,1,0:T(8,128)(2,1)S(1)}, bf16[8,8,32,128]{3,2,1,0:T(8,128)(2,1)S(1)}, u32[]{:S(2)}, u32[]{:S(2)}) collective-permute-start(bf16[8,8,32,128]{3,2,1,0:T(8,128)(2,1)S(1)} %collective-permute-done.11.refs_4_), channel_id=1, source_target_pairs={{0,1},{1,0},{2,3},{3,2},{4,5},{5,4},{6,7},{7,6},{8,9},{9,8},{10,11... | collective-permute-start | bytes 1572872 | tf_op jit(solution)/shard_map/ppermute | solution.py:473
  289.3 3.8 %collective-permute-start.14 = (bf16[8,8,32,128]{3,2,1,0:T(8,128)(2,1)S(1)}, bf16[8,8,32,128]{3,2,1,0:T(8,128)(2,1)S(1)}, u32[]{:S(2)}, u32[]{:S(2)}) collective-permute-start(bf16[8,8,32,128]{3,2,1,0:T(8,128)(2,1)S(1)} %collective-permute-done.13.refs_6_), channel_id=1, source_target_pairs={{0,1},{1,0},{2,3},{3,2},{4,5},{5,4},{6,7},{7,6},{8,9},{9,8},{10,11... | collective-permute-start | bytes 1572872 | tf_op jit(solution)/shard_map/ppermute | solution.py:473
  293.1 1.0 copy-start.1
  294.1 1.0 copy-start.2
  295.2 1.0 copy-start.3
  296.2 3.6 %copy-start.7 = (bf16[128,1024]{1,0:T(8,128)(2,1)S(1)}, bf16[128,1024]{1,0:T(8,128)(2,1)}, u32[]{:S(2)}) copy-start(bf16[128,1024]{1,0:T(8,128)(2,1)} %keys.3) | copy-start | bytes 786436
  296.2 3.6 %copy-start.9 = (bf16[128,1024]{1,0:T(8,128)(2,1)S(1)}, bf16[128,1024]{1,0:T(8,128)(2,1)}, u32[]{:S(2)}) copy-start(bf16[128,1024]{1,0:T(8,128)(2,1)} %values.3) | copy-start | bytes 786436
  296.2 8.2 %copy-start.13 = (f32[256]{0:T(256)S(1)}, f32[256]{0:T(256)}, u32[]{:S(2)}) copy-start(f32[256]{0:T(256)} %div.10.gate) | copy-start | bytes 3076
  304.4 1.0 copy-start.4
Sparse Core Ops, SparseCore 0:
  10.4 93.2 all-gather.2

commit v6 on v5

--- a/solution.py
+++ b/solution.py
@@ -260,11 +260,10 @@
     width = source.shape[0] * LANES // slots
     return call(
         expert_kernel,
-        (shape_of(*source.shape), shape_of(slots, hidden)),
+        (pltpu.HBM(source.shape, jnp.bfloat16), pltpu.HBM((slots, hidden), jnp.bfloat16)),
         [pltpu.VMEM(source.shape, jnp.float32), pltpu.VMEM((slots, width), jnp.bfloat16)]
         + weight_scratch(weights, 2),
         [VMEM, VMEM, ANY],
-        VMEM_MOST,
     )(source, act_grad, weights)
 
 
@@ -385,6 +384,7 @@
         shape_of(tok, width),
         [pltpu.VMEM((tok * width // LANES, LANES), jnp.float32)],
         [SMEM, SMEM, VMEM, VMEM],
+        VMEM_MOST,
     )(dest, gate, source, resid)
 
 
@@ -541,7 +541,9 @@
 
     gates = gate_fixed.reshape(-1).astype(jnp.float32) / 4096.0
     dest = slots_of(expert_ids, experts, capacity)
-    weights = gather_experts(w_gate, w_up, w_down)
+    weights = pltpu.with_memory_space_constraint(
+        gather_experts(w_gate, w_up, w_down), pltpu.HBM
+    )
     to_send = send_grads(dest, gates, grad_out, slots)
     context = context_of(segment_ids, queries, keys, values)
     contexts = gather_contexts(context)
@@ -553,7 +555,9 @@
     )
     pieces = gather_pieces(near)
     recv_rows = exchange(rows)
-    act_grad = act_grad_of(recv_grads, weights, width)
+    act_grad = pltpu.with_memory_space_constraint(
+        act_grad_of(recv_grads, weights, width), pltpu.HBM
+    )
     in_grad, act = expert_back(recv_rows, act_grad, weights)
     back_grad = exchange(in_grad)
     back_grad, out = lax.optimization_barrier((back_grad, expert_out(act, weights, width)))

time: 316 us -> 313 us (level)
  local copies, waits for them, and re-layouts: 9.09 us -> 5.33 us
    unnamed x47 -> x39, local copies, waits for them, and re-layouts: 6.13 us -> 2.43 us
where the time goes in v6:
time: 313 us; the launch traced here: 311 us
  waiting for transfers between devices  146 us (47%)
  starting transfers between devices  99.6 us (32%)
  Pallas kernels  42.8 us (14%)
  between operations  14.5 us (5%)
  local copies, waits for them, and re-layouts  5.33 us (2%)
  other arithmetic  3.26 us (1%)
    all_to_all x5, waiting for transfers between devices, spread(): return lax.all_to_all(rows, axes, split_axis=0, concat_axis=0, tiled=True)  81.2 us
    all_to_all x5, starting transfers between devices, spread(): return lax.all_to_all(rows, axes, split_axis=0, concat_axis=0, tiled=True)  49.9 us
    ppermute x6, waiting for transfers between devices, move_x(): return lax.ppermute(block, 'x', [(i, (i + turn) % xs) for i in range(xs)])  34.9 us
    ppermute x3, waiting for transfers between devices, gather_pieces(): lax.ppermute(near, 'x', [(i, (i + k) % xs) for i in range(xs)])  26.2 us
    ppermute x6, starting transfers between devices, move_x(): return lax.ppermute(block, 'x', [(i, (i + turn) % xs) for i in range(xs)])  20.7 us
    ppermute x4, starting transfers between devices, gather_pieces(): pieces += [part, lax.ppermute(part, 'core', [(0, 1), (1, 0)])]  11.7 us
    ppermute x3, starting transfers between devices, gather_pieces(): lax.ppermute(near, 'x', [(i, (i + k) % xs) for i in range(xs)])  10.8 us
    pallas_call x1, Pallas kernels, expert_back(): call(expert_kernel, (pltpu.HBM(source.shape, jnp.bfloat16), pltpu.HBM((sl...  8.52 us
  transfers between devices with their start and end apart: 21, of which 12 were waited for; matrix products, arithmetic and copies ran while one was open for 1% of the time, Pallas kernels for 10%

profile of v6, /device:TPU:1, one launch (start us, length us, event | category | flops | bytes accessed | tf_op | source)
XLA Modules:
  0.0 311.3 jit_solution(14066078825786182289)
XLA Ops:
  7.2 0.0 all-gather.3.cloned.1.call-start
  7.2 1.0 slice_bitcast_fusion.1
  8.2 0.0 copy-start.16
  8.2 2.0 pad_maximum_fusion
  10.3 0.0 all-gather.3.cloned.1.call-update
  10.3 0.9 broadcast_in_dim.8
  11.2 17.1 %all-to-all-start = ((bf16[64,32,128]{2,1,0:T(8,128)(2,1)}), bf16[64,32,128]{2,1,0:T(8,128)(2,1)S(1)}, u32[]{:S(2)}, u32[]{:S(2)}) async-start(bf16[64,32,128]{2,1,0:T(8,128)(2,1)} %broadcast_in_dim.8), calls=%async_computation | async-start | bytes 1048576 | tf_op jit(solution)/shard_map/all_to_all | solution.py:455
  28.3 0.1 copy.24
  28.4 0.1 reshape.46
  28.6 0.1 copy.25
  28.7 0.7 div.10.gate
  29.4 0.2 fusion
  29.6 0.5 convert_add_fusion.dest
  30.1 3.6 %shard_map.164 = bf16[6144,128]{1,0:T(8,128)(2,1)} custom-call(s32[256]{0:T(256)} %convert_add_fusion.dest, f32[256]{0:T(256)} %div.10.gate, bf16[128,2048]{1,0:T(8,128)(2,1)} %grad.3), custom_call_target="tpu_custom_call" | custom-call | tf_op jit(solution)/shard_map/pallas_call | solution.py:83
  33.7 12.0 %all-to-all-done = bf16[64,32,128]{2,1,0:T(8,128)(2,1)S(1)} async-done(((bf16[64,32,128]{2,1,0:T(8,128)(2,1)}), bf16[64,32,128]{2,1,0:T(8,128)(2,1)S(1)}, u32[]{:S(2)}, u32[]{:S(2)}) %all-to-all-start) | async-done | bytes 524320 | tf_op jit(solution)/shard_map/all_to_all | solution.py:455
  45.7 10.8 %all-to-all-start.2 = ((bf16[64,96,128]{2,1,0:T(8,128)(2,1)}), bf16[64,96,128]{2,1,0:T(8,128)(2,1)S(1)}, u32[]{:S(2)}, u32[]{:S(2)}) async-start(bf16[64,96,128]{2,1,0:T(8,128)(2,1)} %bitcast.41), calls=%async_computation.2 | async-start | bytes 3145728 | tf_op jit(solution)/shard_map/all_to_all | solution.py:455
  56.5 0.1 copy.26.seg_col
  56.7 2.7 shard_map.165
  59.4 2.4 collective-permute-start
  61.7 1.1 collective-permute-done
  62.9 0.1 pad_maximum_fusion.1.refs_0_
  62.9 3.2 %collective-permute-start.1 = (bf16[2,128,1024]{2,1,0:T(8,128)(2,1)S(1)}, bf16[2,128,1024]{2,1,0:T(8,128)(2,1)S(1)}, u32[]{:S(2)}, u32[]{:S(2)}) collective-permute-start(bf16[2,128,1024]{2,1,0:T(8,128)(2,1)S(1)} %pad_maximum_fusion.1.refs_0_), channel_id=1, source_target_pairs={{0,16},{16,32},{32,48},{48,0},{1,17},{17,33},{33,49},{49,1},{2,18}... | collective-permute-start | bytes 1572872 | tf_op jit(solution)/shard_map/ppermute | solution.py:483
  66.1 4.5 %collective-permute-start.2 = (bf16[2,128,1024]{2,1,0:T(8,128)(2,1)S(1)}, bf16[2,128,1024]{2,1,0:T(8,128)(2,1)S(1)}, u32[]{:S(2)}, u32[]{:S(2)}) collective-permute-start(bf16[2,128,1024]{2,1,0:T(8,128)(2,1)S(1)} %pad_maximum_fusion.1.refs_0_), channel_id=1, source_target_pairs={{0,32},{16,48},{32,0},{48,16},{1,33},{17,49},{33,1},{49,17},{2,34}... | collective-permute-start | bytes 1572872 | tf_op jit(solution)/shard_map/ppermute | solution.py:483
  70.6 3.0 collective-permute-start.3
  73.6 14.9 %collective-permute-done.1.refs_1_ = bf16[2,128,1024]{2,1,0:T(8,128)(2,1)S(1)} collective-permute-done((bf16[2,128,1024]{2,1,0:T(8,128)(2,1)S(1)}, bf16[2,128,1024]{2,1,0:T(8,128)(2,1)S(1)}, u32[]{:S(2)}, u32[]{:S(2)}) %collective-permute-start.1) | collective-permute-done | bytes 524320 | tf_op jit(solution)/shard_map/ppermute | solution.py:483
  88.5 15.0 %collective-permute-done.2.refs_2_ = bf16[2,128,1024]{2,1,0:T(8,128)(2,1)S(1)} collective-permute-done((bf16[2,128,1024]{2,1,0:T(8,128)(2,1)S(1)}, bf16[2,128,1024]{2,1,0:T(8,128)(2,1)S(1)}, u32[]{:S(2)}, u32[]{:S(2)}) %collective-permute-start.2) | collective-permute-done | bytes 524320 | tf_op jit(solution)/shard_map/ppermute | solution.py:483
  103.5 0.0 collective-permute-done.3.refs_3_
  103.5 1.5 shard_map.166
  105.0 0.0 copy-start.7
  105.0 4.7 %collective-permute-start.4 = (bf16[2,128,256]{2,1,0:T(8,128)(2,1)S(1)}, bf16[2,128,256]{2,1,0:T(8,128)(2,1)S(1)}, u32[]{:S(2)}, u32[]{:S(2)}) collective-permute-start(bf16[2,128,256]{2,1,0:T(8,128)(2,1)S(1)} %get-tuple-element.24), channel_id=1, source_target_pairs={{0,48},{16,0},{32,16},{48,32},{1,49},{17,1},{33,17},{49,33},{2,50}... | collective-permute-start | bytes 393224 | tf_op jit(solution)/shard_map/ppermute | solution.py:483
  109.7 3.4 %collective-permute-start.5 = (bf16[2,128,256]{2,1,0:T(8,128)(2,1)S(1)}, bf16[2,128,256]{2,1,0:T(8,128)(2,1)S(1)}, u32[]{:S(2)}, u32[]{:S(2)}) collective-permute-start(bf16[2,128,256]{2,1,0:T(8,128)(2,1)S(1)} %get-tuple-element.25), channel_id=1, source_target_pairs={{0,32},{16,48},{32,0},{48,16},{1,33},{17,49},{33,1},{49,17},{2,34}... | collective-permute-start | bytes 393224 | tf_op jit(solution)/shard_map/ppermute | solution.py:483
  113.1 1.9 collective-permute-start.6
  115.1 0.0 copy-start.13
  115.1 2.3 collective-permute-done.5.refs_2_
  117.4 2.8 collective-permute-done.6.refs_3_
  120.2 4.0 %collective-permute-start.7 = (bf16[4,128,256]{2,1,0:T(8,128)(2,1)S(1)}, bf16[4,128,256]{2,1,0:T(8,128)(2,1)}, u32[]{:S(2)}, u32[]{:S(2)}) collective-permute-start(bf16[4,128,256]{2,1,0:T(8,128)(2,1)S(1)} %pad_maximum_fusion.2), channel_id=1, source_target_pairs={{0,1},{1,0},{2,3},{3,2},{4,5},{5,4},{6,7},{7,6},{8,9},{9,8},{10,11... | collective-permute-start | bytes 786440 | tf_op jit(solution)/shard_map/ppermute | solution.py:478
  124.3 0.6 pad_add_fusion.place
  124.9 0.7 collective-permute-done.7.refs_4_
  125.6 4.6 %shard_map.167 = (bf16[128,2048]{1,0:T(8,128)(2,1)}, bf16[6144,128]{1,0:T(8,128)(2,1)}) custom-call(s32[256]{0:T(256)} %convert_add_fusion.dest, s32[2]{0:T(128)} %pad_add_fusion.place, bf16[2,128,256]{2,1,0:T(8,128)(2,1)} %copy-done.7, bf16[2,128,256]{2,1,0:T(8,128)(2,1)} %copy-done.13, bf16[2,128,256]{2,1,0:T(8,128)(2,1)} %copy-done.14, ...), custom_call_target="tpu_custom_call" | custom-call | tf_op jit(solution)/shard_map/pallas_call | solution.py:162
  130.1 1.2 copy-done.12
  131.3 9.5 %all-to-all-start.1 = ((bf16[64,96,128]{2,1,0:T(8,128)(2,1)}), bf16[64,96,128]{2,1,0:T(8,128)(2,1)S(1)}, u32[]{:S(2)}, u32[]{:S(2)}) async-start(bf16[64,96,128]{2,1,0:T(8,128)(2,1)} %bitcast.44), calls=%async_computation.1 | async-start | bytes 3145728 | tf_op jit(solution)/shard_map/all_to_all | solution.py:455
  140.9 0.0 all-gather.3.cloned.1.call-done
  140.9 5.0 %shard_map.168.act_grad = f32[384,512]{1,0:T(8,128)} custom-call(bf16[6144,128]{1,0:T(8,128)(2,1)} %bitcast.42, bf16[8,3,256,512]{3,2,1,0:T(8,128)(2,1)} %bitcast.38), custom_call_target="tpu_custom_call" | custom-call | tf_op jit(solution)/shard_map/pallas_call | solution.py:217
  145.9 34.7 %all-to-all-done.1 = bf16[64,96,128]{2,1,0:T(8,128)(2,1)S(1)} async-done(((bf16[64,96,128]{2,1,0:T(8,128)(2,1)}), bf16[64,96,128]{2,1,0:T(8,128)(2,1)S(1)}, u32[]{:S(2)}, u32[]{:S(2)}) %all-to-all-start.1) | async-done | bytes 1572896 | tf_op jit(solution)/shard_map/all_to_all | solution.py:455
  180.6 8.5 %shard_map.169 = (bf16[6144,128]{1,0:T(8,128)(2,1)}, bf16[384,512]{1,0:T(8,128)(2,1)}) custom-call(bf16[6144,128]{1,0:T(8,128)(2,1)S(1)} %bitcast.25, f32[384,512]{1,0:T(8,128)} %shard_map.168.act_grad, bf16[8,3,256,512]{3,2,1,0:T(8,128)(2,1)} %bitcast.39), custom_call_target="tpu_custom_call" | custom-call | tf_op jit(solution)/shard_map/pallas_call | solution.py:261
  189.1 6.1 %all-to-all-start.3 = ((bf16[64,96,128]{2,1,0:T(8,128)(2,1)}), bf16[64,96,128]{2,1,0:T(8,128)(2,1)S(1)}, u32[]{:S(2)}, u32[]{:S(2)}) async-start(bf16[64,96,128]{2,1,0:T(8,128)(2,1)} %bitcast.45), calls=%async_computation.3 | async-start | bytes 3145728 | tf_op jit(solution)/shard_map/all_to_all | solution.py:455
  195.3 5.3 %shard_map.170 = bf16[6144,128]{1,0:T(8,128)(2,1)} custom-call(bf16[384,512]{1,0:T(8,128)(2,1)} %get-tuple-element.30.act, bf16[8,3,256,512]{3,2,1,0:T(8,128)(2,1)} %bitcast.40), custom_call_target="tpu_custom_call" | custom-call | tf_op jit(solution)/shard_map/pallas_call | solution.py:290
  200.6 34.4 %all-to-all-done.3 = bf16[64,96,128]{2,1,0:T(8,128)(2,1)S(1)} async-done(((bf16[64,96,128]{2,1,0:T(8,128)(2,1)}), bf16[64,96,128]{2,1,0:T(8,128)(2,1)S(1)}, u32[]{:S(2)}, u32[]{:S(2)}) %all-to-all-start.3) | async-done | bytes 1572896 | tf_op jit(solution)/shard_map/all_to_all | solution.py:455
  235.0 6.4 %all-to-all-start.4 = ((bf16[64,96,128]{2,1,0:T(8,128)(2,1)}), bf16[64,96,128]{2,1,0:T(8,128)(2,1)}, u32[]{:S(2)}, u32[]{:S(2)}) async-start(bf16[64,96,128]{2,1,0:T(8,128)(2,1)} %bitcast.43), calls=%async_computation.4 | async-start | bytes 3145728 | tf_op jit(solution)/shard_map/all_to_all | solution.py:455
  241.4 3.3 %collective-permute-start.9 = (bf16[8,8,32,128]{3,2,1,0:T(8,128)(2,1)S(1)}, bf16[8,8,32,128]{3,2,1,0:T(8,128)(2,1)S(1)}, u32[]{:S(2)}, u32[]{:S(2)}) collective-permute-start(bf16[8,8,32,128]{3,2,1,0:T(8,128)(2,1)S(1)} %bitcast.27), channel_id=1, source_target_pairs={{0,16},{16,32},{32,48},{48,0},{1,17},{17,33},{33,49},{49,1},{2,18}... | collective-permute-start | bytes 1572872 | tf_op jit(solution)/shard_map/ppermute | solution.py:468
  244.7 4.5 %collective-permute-start.11 = (bf16[8,8,32,128]{3,2,1,0:T(8,128)(2,1)S(1)}, bf16[8,8,32,128]{3,2,1,0:T(8,128)(2,1)S(1)}, u32[]{:S(2)}, u32[]{:S(2)}) collective-permute-start(bf16[8,8,32,128]{3,2,1,0:T(8,128)(2,1)S(1)} %bitcast.28), channel_id=1, source_target_pairs={{0,32},{16,48},{32,0},{48,16},{1,33},{17,49},{33,1},{49,17},{2,34}... | collective-permute-start | bytes 1572872 | tf_op jit(solution)/shard_map/ppermute | solution.py:468
  249.2 3.0 collective-permute-start.13
  252.2 3.1 %collective-permute-start.8 = (bf16[8,8,32,128]{3,2,1,0:T(8,128)(2,1)S(1)}, bf16[8,8,32,128]{3,2,1,0:T(8,128)(2,1)S(1)}, u32[]{:S(2)}, u32[]{:S(2)}) collective-permute-start(bf16[8,8,32,128]{3,2,1,0:T(8,128)(2,1)S(1)} %bitcast.30), channel_id=1, source_target_pairs={{0,1},{1,0},{2,3},{3,2},{4,5},{5,4},{6,7},{7,6},{8,9},{9,8},{10,11... | collective-permute-start | bytes 1572872 | tf_op jit(solution)/shard_map/ppermute | solution.py:473
  255.4 11.7 %collective-permute-done.9.refs_2_ = bf16[8,8,32,128]{3,2,1,0:T(8,128)(2,1)S(1)} collective-permute-done((bf16[8,8,32,128]{3,2,1,0:T(8,128)(2,1)S(1)}, bf16[8,8,32,128]{3,2,1,0:T(8,128)(2,1)S(1)}, u32[]{:S(2)}, u32[]{:S(2)}) %collective-permute-start.9) | collective-permute-done | bytes 524320 | tf_op jit(solution)/shard_map/ppermute | solution.py:468
  267.1 3.6 %collective-permute-start.10 = (bf16[8,8,32,128]{3,2,1,0:T(8,128)(2,1)S(1)}, bf16[8,8,32,128]{3,2,1,0:T(8,128)(2,1)S(1)}, u32[]{:S(2)}, u32[]{:S(2)}) collective-permute-start(bf16[8,8,32,128]{3,2,1,0:T(8,128)(2,1)S(1)} %collective-permute-done.9.refs_2_), channel_id=1, source_target_pairs={{0,1},{1,0},{2,3},{3,2},{4,5},{5,4},{6,7},{7,6},{8,9},{9,8},{10,11... | collective-permute-start | bytes 1572872 | tf_op jit(solution)/shard_map/ppermute | solution.py:473
  270.7 14.5 %collective-permute-done.11.refs_4_ = bf16[8,8,32,128]{3,2,1,0:T(8,128)(2,1)S(1)} collective-permute-done((bf16[8,8,32,128]{3,2,1,0:T(8,128)(2,1)S(1)}, bf16[8,8,32,128]{3,2,1,0:T(8,128)(2,1)S(1)}, u32[]{:S(2)}, u32[]{:S(2)}) %collective-permute-start.11) | collective-permute-done | bytes 524320 | tf_op jit(solution)/shard_map/ppermute | solution.py:468
  285.2 2.9 collective-permute-start.12
  288.1 2.1 collective-permute-start.14
  290.2 0.0 collective-permute-done.12.refs_5_
  290.2 1.6 collective-permute-done.14.refs_7_
  291.9 1.0 copy-done.1
  292.9 3.7 %shard_map.172 = (bf16[128,2048]{1,0:T(8,128)(2,1)}, bf16[128,1024]{1,0:T(8,128)(2,1)S(1)}) custom-call(s32[256]{0:T(256)S(1)} %copy-done.9, s32[2]{0:T(128)S(1)} %copy-done.11, bf16[6144,128]{1,0:T(8,128)(2,1)S(1)} %bitcast.24, bf16[128,2048]{1,0:T(8,128)(2,1)S(1)} %copy-done.1, f32[1,2048]{1,0:T(1,128)S(1)} %bitcast.34, bf16[128,2048]{1,0:T(8,128)(2,1)S(1)} %copy-done, ...), custom_call_target="tpu_custom_call" | custom-call | tf_op jit(solution)/shard_map/pallas_call | solution.py:349
  296.6 4.5 %shard_map.173 = (bf16[128,1024]{1,0:T(8,128)(2,1)}, bf16[128,1024]{1,0:T(8,128)(2,1)}, bf16[128,1024]{1,0:T(8,128)(2,1)}) custom-call(s32[1,128]{1,0:T(1,128)S(1)} %bitcast.37, s32[128,1]{1,0:T(8,128)S(1)} %copy.26.seg_col, bf16[128,1024]{1,0:T(8,128)(2,1)S(1)} %copy-done.2, bf16[128,1024]{1,0:T(8,128)(2,1)S(1)} %copy-done.4, ...), custom_call_target="tpu_custom_call" | custom-call | tf_op jit(solution)/shard_map/pallas_call | solution.py:449
  301.1 3.4 %shard_map.171 = bf16[128,2048]{1,0:T(8,128)(2,1)} custom-call(s32[256]{0:T(256)} %convert_add_fusion.dest, f32[256]{0:T(256)} %div.10.gate, bf16[6144,128]{1,0:T(8,128)(2,1)} %bitcast.20.source, bf16[128,2048]{1,0:T(8,128)(2,1)} %get-tuple-element.32.resid), custom_call_target="tpu_custom_call" | custom-call | tf_op jit(solution)/shard_map/pallas_call | solution.py:382
  (46 shorter events, 0.2 us)
Async XLA Ops:
  7.2 133.7 %all-gather.3.cloned.1.call-start = ((), (), s32[]{:S(2)}) async-start(), calls=%async_computation.5 | async-start | bytes 7077888 | tf_op jit(solution)/shard_map/all_gather | solution.py:502
  8.2 2.1 copy-start.16
  10.3 18.0 %copy-start.17 = (s32[128,2]{0,1:T(2,128)S(1)}, s32[128,2]{0,1:T(2,128)}, u32[]{:S(2)}) copy-start(s32[128,2]{0,1:T(2,128)} %param.23) | copy-start | bytes 3076
  10.3 18.3 %copy-start.18 = (s32[128,2]{0,1:T(2,128)S(1)}, s32[128,2]{0,1:T(2,128)}, u32[]{:S(2)}) copy-start(s32[128,2]{0,1:T(2,128)} %param.24) | copy-start | bytes 3076
  11.2 34.6 %all-to-all-start = ((bf16[64,32,128]{2,1,0:T(8,128)(2,1)}), bf16[64,32,128]{2,1,0:T(8,128)(2,1)S(1)}, u32[]{:S(2)}, u32[]{:S(2)}) async-start(bf16[64,32,128]{2,1,0:T(8,128)(2,1)} %broadcast_in_dim.8), calls=%async_computation | async-start | bytes 1048576 | tf_op jit(solution)/shard_map/all_to_all | solution.py:455
  45.7 10.8 %copy-start.10 = (s32[128]{0:T(128)S(1)}, s32[128]{0:T(128)}, u32[]{:S(2)}) copy-start(s32[128]{0:T(128)} %param.17) | copy-start | bytes 1540
  45.7 10.9 %copy-start.2 = (bf16[128,1024]{1,0:T(8,128)(2,1)S(1)}, bf16[128,1024]{1,0:T(8,128)(2,1)}, u32[]{:S(2)}) copy-start(bf16[128,1024]{1,0:T(8,128)(2,1)} %queries.3) | copy-start | bytes 786436
  45.7 10.9 %copy-start.3 = (bf16[128,1024]{1,0:T(8,128)(2,1)S(1)}, bf16[128,1024]{1,0:T(8,128)(2,1)}, u32[]{:S(2)}) copy-start(bf16[128,1024]{1,0:T(8,128)(2,1)} %keys.3) | copy-start | bytes 786436
  45.7 10.9 %copy-start.5 = (bf16[128,1024]{1,0:T(8,128)(2,1)S(1)}, bf16[128,1024]{1,0:T(8,128)(2,1)}, u32[]{:S(2)}) copy-start(bf16[128,1024]{1,0:T(8,128)(2,1)} %values.3) | copy-start | bytes 786436
  45.7 84.4 %all-to-all-start.2 = ((bf16[64,96,128]{2,1,0:T(8,128)(2,1)}), bf16[64,96,128]{2,1,0:T(8,128)(2,1)S(1)}, u32[]{:S(2)}, u32[]{:S(2)}) async-start(bf16[64,96,128]{2,1,0:T(8,128)(2,1)} %bitcast.41), calls=%async_computation.2 | async-start | bytes 3145728 | tf_op jit(solution)/shard_map/all_to_all | solution.py:455
  59.4 3.5 %collective-permute-start = (bf16[128,1024]{1,0:T(8,128)(2,1)S(1)}, bf16[128,1024]{1,0:T(8,128)(2,1)S(1)}, u32[]{:S(2)}, u32[]{:S(2)}) collective-permute-start(bf16[128,1024]{1,0:T(8,128)(2,1)S(1)} %shard_map.165), channel_id=1, source_target_pairs={{0,1},{1,0},{2,3},{3,2},{4,5},{5,4},{6,7},{7,6},{8,9},{9,8},{10,11... | collective-permute-start | bytes 786440 | tf_op jit(solution)/shard_map/ppermute | solution.py:478
  62.9 25.6 %collective-permute-start.1 = (bf16[2,128,1024]{2,1,0:T(8,128)(2,1)S(1)}, bf16[2,128,1024]{2,1,0:T(8,128)(2,1)S(1)}, u32[]{:S(2)}, u32[]{:S(2)}) collective-permute-start(bf16[2,128,1024]{2,1,0:T(8,128)(2,1)S(1)} %pad_maximum_fusion.1.refs_0_), channel_id=1, source_target_pairs={{0,16},{16,32},{32,48},{48,0},{1,17},{17,33},{33,49},{49,1},{2,18}... | collective-permute-start | bytes 1572872 | tf_op jit(solution)/shard_map/ppermute | solution.py:483
  66.1 37.4 %collective-permute-start.2 = (bf16[2,128,1024]{2,1,0:T(8,128)(2,1)S(1)}, bf16[2,128,1024]{2,1,0:T(8,128)(2,1)S(1)}, u32[]{:S(2)}, u32[]{:S(2)}) collective-permute-start(bf16[2,128,1024]{2,1,0:T(8,128)(2,1)S(1)} %pad_maximum_fusion.1.refs_0_), channel_id=1, source_target_pairs={{0,32},{16,48},{32,0},{48,16},{1,33},{17,49},{33,1},{49,17},{2,34}... | collective-permute-start | bytes 1572872 | tf_op jit(solution)/shard_map/ppermute | solution.py:483
  70.6 32.8 %collective-permute-start.3 = (bf16[2,128,1024]{2,1,0:T(8,128)(2,1)S(1)}, bf16[2,128,1024]{2,1,0:T(8,128)(2,1)S(1)}, u32[]{:S(2)}, u32[]{:S(2)}) collective-permute-start(bf16[2,128,1024]{2,1,0:T(8,128)(2,1)S(1)} %pad_maximum_fusion.1.refs_0_), channel_id=1, source_target_pairs={{0,48},{16,0},{32,16},{48,32},{1,49},{17,1},{33,17},{49,33},{2,50}... | collective-permute-start | bytes 1572872 | tf_op jit(solution)/shard_map/ppermute | solution.py:483
  105.0 20.5 %copy-start.7 = (bf16[2,128,256]{2,1,0:T(8,128)(2,1)}, bf16[2,128,256]{2,1,0:T(8,128)(2,1)S(1)}, u32[]{:S(2)}) copy-start(bf16[2,128,256]{2,1,0:T(8,128)(2,1)S(1)} %get-tuple-element.23.refs_0_) | copy-start | bytes 393220
  105.0 10.1 %collective-permute-start.4 = (bf16[2,128,256]{2,1,0:T(8,128)(2,1)S(1)}, bf16[2,128,256]{2,1,0:T(8,128)(2,1)S(1)}, u32[]{:S(2)}, u32[]{:S(2)}) collective-permute-start(bf16[2,128,256]{2,1,0:T(8,128)(2,1)S(1)} %get-tuple-element.24), channel_id=1, source_target_pairs={{0,48},{16,0},{32,16},{48,32},{1,49},{17,1},{33,17},{49,33},{2,50}... | collective-permute-start | bytes 393224 | tf_op jit(solution)/shard_map/ppermute | solution.py:483
  109.7 7.7 %collective-permute-start.5 = (bf16[2,128,256]{2,1,0:T(8,128)(2,1)S(1)}, bf16[2,128,256]{2,1,0:T(8,128)(2,1)S(1)}, u32[]{:S(2)}, u32[]{:S(2)}) collective-permute-start(bf16[2,128,256]{2,1,0:T(8,128)(2,1)S(1)} %get-tuple-element.25), channel_id=1, source_target_pairs={{0,32},{16,48},{32,0},{48,16},{1,33},{17,49},{33,1},{49,17},{2,34}... | collective-permute-start | bytes 393224 | tf_op jit(solution)/shard_map/ppermute | solution.py:483
  113.1 7.0 %collective-permute-start.6 = (bf16[2,128,256]{2,1,0:T(8,128)(2,1)S(1)}, bf16[2,128,256]{2,1,0:T(8,128)(2,1)S(1)}, u32[]{:S(2)}, u32[]{:S(2)}) collective-permute-start(bf16[2,128,256]{2,1,0:T(8,128)(2,1)S(1)} %get-tuple-element.26), channel_id=1, source_target_pairs={{0,16},{16,32},{32,48},{48,0},{1,17},{17,33},{33,49},{49,1},{2,18}... | collective-permute-start | bytes 393224 | tf_op jit(solution)/shard_map/ppermute | solution.py:483
  115.1 10.5 %copy-start.13 = (bf16[2,128,256]{2,1,0:T(8,128)(2,1)}, bf16[2,128,256]{2,1,0:T(8,128)(2,1)S(1)}, u32[]{:S(2)}) copy-start(bf16[2,128,256]{2,1,0:T(8,128)(2,1)S(1)} %collective-permute-done.4.refs_1_) | copy-start | bytes 393220
  117.4 8.2 %copy-start.14 = (bf16[2,128,256]{2,1,0:T(8,128)(2,1)}, bf16[2,128,256]{2,1,0:T(8,128)(2,1)S(1)}, u32[]{:S(2)}) copy-start(bf16[2,128,256]{2,1,0:T(8,128)(2,1)S(1)} %collective-permute-done.5.refs_2_) | copy-start | bytes 393220
  120.2 5.4 %copy-start.15 = (bf16[2,128,256]{2,1,0:T(8,128)(2,1)}, bf16[2,128,256]{2,1,0:T(8,128)(2,1)S(1)}, u32[]{:S(2)}) copy-start(bf16[2,128,256]{2,1,0:T(8,128)(2,1)S(1)} %collective-permute-done.6.refs_3_) | copy-start | bytes 393220
  120.2 5.3 %collective-permute-start.7 = (bf16[4,128,256]{2,1,0:T(8,128)(2,1)S(1)}, bf16[4,128,256]{2,1,0:T(8,128)(2,1)}, u32[]{:S(2)}, u32[]{:S(2)}) collective-permute-start(bf16[4,128,256]{2,1,0:T(8,128)(2,1)S(1)} %pad_maximum_fusion.2), channel_id=1, source_target_pairs={{0,1},{1,0},{2,3},{3,2},{4,5},{5,4},{6,7},{7,6},{8,9},{9,8},{10,11... | collective-permute-start | bytes 786440 | tf_op jit(solution)/shard_map/ppermute | solution.py:478
  130.1 1.2 copy-start.12
  131.3 49.3 %all-to-all-start.1 = ((bf16[64,96,128]{2,1,0:T(8,128)(2,1)}), bf16[64,96,128]{2,1,0:T(8,128)(2,1)S(1)}, u32[]{:S(2)}, u32[]{:S(2)}) async-start(bf16[64,96,128]{2,1,0:T(8,128)(2,1)} %bitcast.44), calls=%async_computation.1 | async-start | bytes 3145728 | tf_op jit(solution)/shard_map/all_to_all | solution.py:455
  189.1 45.9 %all-to-all-start.3 = ((bf16[64,96,128]{2,1,0:T(8,128)(2,1)}), bf16[64,96,128]{2,1,0:T(8,128)(2,1)S(1)}, u32[]{:S(2)}, u32[]{:S(2)}) async-start(bf16[64,96,128]{2,1,0:T(8,128)(2,1)} %bitcast.45), calls=%async_computation.3 | async-start | bytes 3145728 | tf_op jit(solution)/shard_map/all_to_all | solution.py:455
  235.0 56.9 %copy-start = (bf16[128,2048]{1,0:T(8,128)(2,1)S(1)}, bf16[128,2048]{1,0:T(8,128)(2,1)}, u32[]{:S(2)}) copy-start(bf16[128,2048]{1,0:T(8,128)(2,1)} %grad.3) | copy-start | bytes 1572868
  235.0 56.9 %copy-start.8 = (f32[2048]{0:T(1024)S(1)}, f32[2048]{0:T(1024)}, u32[]{:S(2)}) copy-start(f32[2048]{0:T(1024)} %param.19) | copy-start | bytes 24580
  235.0 56.9 %copy-start.9 = (s32[256]{0:T(256)S(1)}, s32[256]{0:T(256)}, u32[]{:S(2)}) copy-start(s32[256]{0:T(256)} %convert_add_fusion.dest) | copy-start | bytes 3076
  235.0 56.9 %copy-start.11 = (s32[2]{0:T(128)S(1)}, s32[2]{0:T(128)}, u32[]{:S(2)}) copy-start(s32[2]{0:T(128)} %pad_add_fusion.place) | copy-start | bytes 28
  235.0 66.1 %all-to-all-start.4 = ((bf16[64,96,128]{2,1,0:T(8,128)(2,1)}), bf16[64,96,128]{2,1,0:T(8,128)(2,1)}, u32[]{:S(2)}, u32[]{:S(2)}) async-start(bf16[64,96,128]{2,1,0:T(8,128)(2,1)} %bitcast.43), calls=%async_computation.4 | async-start | bytes 3145728 | tf_op jit(solution)/shard_map/all_to_all | solution.py:455
  241.4 25.6 %collective-permute-start.9 = (bf16[8,8,32,128]{3,2,1,0:T(8,128)(2,1)S(1)}, bf16[8,8,32,128]{3,2,1,0:T(8,128)(2,1)S(1)}, u32[]{:S(2)}, u32[]{:S(2)}) collective-permute-start(bf16[8,8,32,128]{3,2,1,0:T(8,128)(2,1)S(1)} %bitcast.27), channel_id=1, source_target_pairs={{0,16},{16,32},{32,48},{48,0},{1,17},{17,33},{33,49},{49,1},{2,18}... | collective-permute-start | bytes 1572872 | tf_op jit(solution)/shard_map/ppermute | solution.py:468
  244.7 40.5 %collective-permute-start.11 = (bf16[8,8,32,128]{3,2,1,0:T(8,128)(2,1)S(1)}, bf16[8,8,32,128]{3,2,1,0:T(8,128)(2,1)S(1)}, u32[]{:S(2)}, u32[]{:S(2)}) collective-permute-start(bf16[8,8,32,128]{3,2,1,0:T(8,128)(2,1)S(1)} %bitcast.28), channel_id=1, source_target_pairs={{0,32},{16,48},{32,0},{48,16},{1,33},{17,49},{33,1},{49,17},{2,34}... | collective-permute-start | bytes 1572872 | tf_op jit(solution)/shard_map/ppermute | solution.py:468
  249.2 38.8 %collective-permute-start.13 = (bf16[8,8,32,128]{3,2,1,0:T(8,128)(2,1)S(1)}, bf16[8,8,32,128]{3,2,1,0:T(8,128)(2,1)S(1)}, u32[]{:S(2)}, u32[]{:S(2)}) collective-permute-start(bf16[8,8,32,128]{3,2,1,0:T(8,128)(2,1)S(1)} %bitcast.29), channel_id=1, source_target_pairs={{0,48},{16,0},{32,16},{48,32},{1,49},{17,1},{33,17},{49,33},{2,50}... | collective-permute-start | bytes 1572872 | tf_op jit(solution)/shard_map/ppermute | solution.py:468
  252.2 38.0 %collective-permute-start.8 = (bf16[8,8,32,128]{3,2,1,0:T(8,128)(2,1)S(1)}, bf16[8,8,32,128]{3,2,1,0:T(8,128)(2,1)S(1)}, u32[]{:S(2)}, u32[]{:S(2)}) collective-permute-start(bf16[8,8,32,128]{3,2,1,0:T(8,128)(2,1)S(1)} %bitcast.30), channel_id=1, source_target_pairs={{0,1},{1,0},{2,3},{3,2},{4,5},{5,4},{6,7},{7,6},{8,9},{9,8},{10,11... | collective-permute-start | bytes 1572872 | tf_op jit(solution)/shard_map/ppermute | solution.py:473
  267.1 23.2 %collective-permute-start.10 = (bf16[8,8,32,128]{3,2,1,0:T(8,128)(2,1)S(1)}, bf16[8,8,32,128]{3,2,1,0:T(8,128)(2,1)S(1)}, u32[]{:S(2)}, u32[]{:S(2)}) collective-permute-start(bf16[8,8,32,128]{3,2,1,0:T(8,128)(2,1)S(1)} %collective-permute-done.9.refs_2_), channel_id=1, source_target_pairs={{0,1},{1,0},{2,3},{3,2},{4,5},{5,4},{6,7},{7,6},{8,9},{9,8},{10,11... | collective-permute-start | bytes 1572872 | tf_op jit(solution)/shard_map/ppermute | solution.py:473
  285.2 5.1 %collective-permute-start.12 = (bf16[8,8,32,128]{3,2,1,0:T(8,128)(2,1)S(1)}, bf16[8,8,32,128]{3,2,1,0:T(8,128)(2,1)S(1)}, u32[]{:S(2)}, u32[]{:S(2)}) collective-permute-start(bf16[8,8,32,128]{3,2,1,0:T(8,128)(2,1)S(1)} %collective-permute-done.11.refs_4_), channel_id=1, source_target_pairs={{0,1},{1,0},{2,3},{3,2},{4,5},{5,4},{6,7},{7,6},{8,9},{9,8},{10,11... | collective-permute-start | bytes 1572872 | tf_op jit(solution)/shard_map/ppermute | solution.py:473
  288.1 3.8 %collective-permute-start.14 = (bf16[8,8,32,128]{3,2,1,0:T(8,128)(2,1)S(1)}, bf16[8,8,32,128]{3,2,1,0:T(8,128)(2,1)S(1)}, u32[]{:S(2)}, u32[]{:S(2)}) collective-permute-start(bf16[8,8,32,128]{3,2,1,0:T(8,128)(2,1)S(1)} %collective-permute-done.13.refs_6_), channel_id=1, source_target_pairs={{0,1},{1,0},{2,3},{3,2},{4,5},{5,4},{6,7},{7,6},{8,9},{9,8},{10,11... | collective-permute-start | bytes 1572872 | tf_op jit(solution)/shard_map/ppermute | solution.py:473
  291.9 1.0 copy-start.1
  292.9 3.7 %copy-start.4 = (bf16[128,1024]{1,0:T(8,128)(2,1)S(1)}, bf16[128,1024]{1,0:T(8,128)(2,1)}, u32[]{:S(2)}) copy-start(bf16[128,1024]{1,0:T(8,128)(2,1)} %keys.3) | copy-start | bytes 786436
  292.9 3.7 %copy-start.6 = (bf16[128,1024]{1,0:T(8,128)(2,1)S(1)}, bf16[128,1024]{1,0:T(8,128)(2,1)}, u32[]{:S(2)}) copy-start(bf16[128,1024]{1,0:T(8,128)(2,1)} %values.3) | copy-start | bytes 786436
Sparse Core Ops, SparseCore 0:
  10.4 93.2 all-gather.2

commit v7 on v6

--- a/solution.py
+++ b/solution.py
@@ -89,27 +89,28 @@
     )(dest, gate, grad)
 
 
-def slab_kernel(near, *refs):
-    pairs, outs, slab = refs[:4], refs[4:8], refs[8]
+def slab_kernel(near, other, *refs):
+    count = other.shape[0]
+    mine, outs, slab = refs[:count], refs[count : 2 * count], refs[2 * count]
     heads, ys, cols, depth = near.shape
     for y in range(ys):
         for h in range(heads):
             slab[y * cols : (y + 1) * cols, h * depth : (h + 1) * depth] = near[h, y]
-    for pair, out in zip(pairs, outs):
-        for n in range(2):
-            out[n] = contract_last(pair[n], slab[...]).astype(jnp.bfloat16)
-
-
-def slab_products(near, contexts):
+    for k in range(count):
+        outs[k][0] = contract_last(mine[k][...], slab[...]).astype(jnp.bfloat16)
+        outs[k][1] = contract_last(other[k], slab[...]).astype(jnp.bfloat16)
+
+
+def slab_products(near, mine, other):
     heads, ys, cols, depth = near.shape
-    tok = contexts[0].shape[1]
+    tok = other.shape[1]
     out = jax.ShapeDtypeStruct((2, tok, ys * cols), jnp.bfloat16)
     return call(
         slab_kernel,
-        (out,) * len(contexts),
+        (out,) * len(mine),
         [pltpu.VMEM((ys * cols, heads * depth), jnp.bfloat16)],
-        [VMEM] * (1 + len(contexts)),
-    )(near, *contexts)
+        [VMEM] * (2 + len(mine)),
+    )(near, other, *mine)
 
 
 def spread_matrix(core, rows, cols):
@@ -484,8 +485,8 @@
 
 
 def gather_contexts(context):
-    pair = jnp.stack([context, swap_cores(context)])
-    return [pair] + [move_x(pair, k) for k in range(1, lax.axis_size("x"))]
+    mine = [context] + [move_x(context, k) for k in range(1, lax.axis_size("x"))]
+    return mine, swap_cores(jnp.stack(mine))
 
 
 def return_products(products):
@@ -546,10 +547,10 @@
     )
     to_send = send_grads(dest, gates, grad_out, slots)
     context = context_of(segment_ids, queries, keys, values)
-    contexts = gather_contexts(context)
+    own_contexts, other_contexts = gather_contexts(context)
     near, to_send = lax.optimization_barrier((gather_near(out_proj), to_send))
     recv_grads = exchange(to_send)
-    mine, other = return_products(slab_products(near, contexts))
+    mine, other = return_products(slab_products(near, own_contexts, other_contexts))
     resid, rows = make_resid(
         dest, place, mine, other, hidden_in, norm_gain, slots, out_proj.shape[1]
     )

time: 313 us -> 303 us (0.968)
  waiting for transfers between devices: 146 us -> 134 us
    ppermute x6, waiting for transfers between devices: 34.9 us -> 22.1 us  [move_x(): return lax.ppermute(block, 'x', [(i, (i + turn) % xs) for i in range(xs)])]
  transfers between devices with their start and end apart: 21 -> 21, of which waited for: 12 -> 13; matrix products, arithmetic and copies ran while one was open for 1% -> 1% of each run, Pallas kernels for 10% -> 10%
where the time goes in v7:
time: 303 us; the launch traced here: 302 us
  waiting for transfers between devices  134 us (44%)
  starting transfers between devices  102 us (34%)
  Pallas kernels  42.7 us (14%)
  between operations  14.5 us (5%)
  local copies, waits for them, and re-layouts  5.33 us (2%)
  other arithmetic  3.34 us (1%)
    all_to_all x5, waiting for transfers between devices, spread(): return lax.all_to_all(rows, axes, split_axis=0, concat_axis=0, tiled=True)  81.2 us
    all_to_all x5, starting transfers between devices, spread(): return lax.all_to_all(rows, axes, split_axis=0, concat_axis=0, tiled=True)  51.5 us
    ppermute x3, waiting for transfers between devices, gather_pieces(): lax.ppermute(near, 'x', [(i, (i + k) % xs) for i in range(xs)])  26.2 us
    ppermute x6, waiting for transfers between devices, move_x(): return lax.ppermute(block, 'x', [(i, (i + turn) % xs) for i in range(xs)])  22.1 us
    ppermute x6, starting transfers between devices, move_x(): return lax.ppermute(block, 'x', [(i, (i + turn) % xs) for i in range(xs)])  21.5 us
    ppermute x4, starting transfers between devices, gather_pieces(): pieces += [part, lax.ppermute(part, 'core', [(0, 1), (1, 0)])]  11.7 us
    ppermute x3, starting transfers between devices, gather_pieces(): lax.ppermute(near, 'x', [(i, (i + k) % xs) for i in range(xs)])  10.8 us
    pallas_call x1, Pallas kernels, expert_back(): call(expert_kernel, (pltpu.HBM(source.shape, jnp.bfloat16), pltpu.HBM((sl...  8.52 us
  transfers between devices with their start and end apart: 21, of which 13 were waited for; matrix products, arithmetic and copies ran while one was open for 1% of the time, Pallas kernels for 10%

profile of v7, /device:TPU:1, one launch (start us, length us, event | category | flops | bytes accessed | tf_op | source)
XLA Modules:
  0.0 302.2 jit_solution(5235415988260987483)
XLA Ops:
  7.2 0.0 all-gather.3.cloned.1.call-start
  7.2 1.0 slice_bitcast_fusion.1
  8.2 0.0 copy-start.16
  8.2 2.0 pad_maximum_fusion.1
  10.3 0.0 all-gather.3.cloned.1.call-update
  10.3 0.9 broadcast_in_dim.8
  11.2 17.1 %all-to-all-start = ((bf16[64,32,128]{2,1,0:T(8,128)(2,1)}), bf16[64,32,128]{2,1,0:T(8,128)(2,1)S(1)}, u32[]{:S(2)}, u32[]{:S(2)}) async-start(bf16[64,32,128]{2,1,0:T(8,128)(2,1)} %broadcast_in_dim.8), calls=%async_computation | async-start | bytes 1048576 | tf_op jit(solution)/shard_map/all_to_all | solution.py:456
  28.3 0.1 copy.24
  28.4 0.1 reshape.46
  28.6 0.1 copy.25
  28.7 0.7 div.10.gate
  29.4 0.2 fusion
  29.6 0.5 convert_add_fusion.dest
  30.1 3.6 %shard_map.164 = bf16[6144,128]{1,0:T(8,128)(2,1)} custom-call(s32[256]{0:T(256)} %convert_add_fusion.dest, f32[256]{0:T(256)} %div.10.gate, bf16[128,2048]{1,0:T(8,128)(2,1)} %grad.3), custom_call_target="tpu_custom_call" | custom-call | tf_op jit(solution)/shard_map/pallas_call | solution.py:83
  33.7 12.0 %all-to-all-done = bf16[64,32,128]{2,1,0:T(8,128)(2,1)S(1)} async-done(((bf16[64,32,128]{2,1,0:T(8,128)(2,1)}), bf16[64,32,128]{2,1,0:T(8,128)(2,1)S(1)}, u32[]{:S(2)}, u32[]{:S(2)}) %all-to-all-start) | async-done | bytes 524320 | tf_op jit(solution)/shard_map/all_to_all | solution.py:456
  45.7 10.8 %all-to-all-start.2 = ((bf16[64,96,128]{2,1,0:T(8,128)(2,1)}), bf16[64,96,128]{2,1,0:T(8,128)(2,1)S(1)}, u32[]{:S(2)}, u32[]{:S(2)}) async-start(bf16[64,96,128]{2,1,0:T(8,128)(2,1)} %bitcast.46), calls=%async_computation.2 | async-start | bytes 3145728 | tf_op jit(solution)/shard_map/all_to_all | solution.py:456
  56.5 0.1 copy.26.seg_col
  56.7 2.7 shard_map.165.refs_0_
  59.4 3.3 %collective-permute-start = (bf16[128,1024]{1,0:T(8,128)(2,1)S(1)}, bf16[128,1024]{1,0:T(8,128)(2,1)S(1)}, u32[]{:S(2)}, u32[]{:S(2)}) collective-permute-start(bf16[128,1024]{1,0:T(8,128)(2,1)S(1)} %shard_map.165.refs_0_), channel_id=1, source_target_pairs={{0,16},{16,32},{32,48},{48,0},{1,17},{17,33},{33,49},{49,1},{2,18}... | collective-permute-start | bytes 786440 | tf_op jit(solution)/shard_map/ppermute | solution.py:484
  62.6 4.5 %collective-permute-start.1 = (bf16[128,1024]{1,0:T(8,128)(2,1)S(1)}, bf16[128,1024]{1,0:T(8,128)(2,1)S(1)}, u32[]{:S(2)}, u32[]{:S(2)}) collective-permute-start(bf16[128,1024]{1,0:T(8,128)(2,1)S(1)} %shard_map.165.refs_0_), channel_id=1, source_target_pairs={{0,32},{16,48},{32,0},{48,16},{1,33},{17,49},{33,1},{49,17},{2,34}... | collective-permute-start | bytes 786440 | tf_op jit(solution)/shard_map/ppermute | solution.py:484
  67.1 3.0 collective-permute-start.2
  70.1 5.2 %collective-permute-done.refs_1_ = bf16[128,1024]{1,0:T(8,128)(2,1)S(1)} collective-permute-done((bf16[128,1024]{1,0:T(8,128)(2,1)S(1)}, bf16[128,1024]{1,0:T(8,128)(2,1)S(1)}, u32[]{:S(2)}, u32[]{:S(2)}) %collective-permute-start) | collective-permute-done | bytes 262176 | tf_op jit(solution)/shard_map/ppermute | solution.py:484
  75.4 9.9 %collective-permute-done.1.refs_2_ = bf16[128,1024]{1,0:T(8,128)(2,1)S(1)} collective-permute-done((bf16[128,1024]{1,0:T(8,128)(2,1)S(1)}, bf16[128,1024]{1,0:T(8,128)(2,1)S(1)}, u32[]{:S(2)}, u32[]{:S(2)}) %collective-permute-start.1) | collective-permute-done | bytes 262176 | tf_op jit(solution)/shard_map/ppermute | solution.py:484
  85.3 1.0 collective-permute-done.2.refs_3_
  86.3 0.1 pad_maximum_fusion
  86.5 3.1 %collective-permute-start.3 = (bf16[4,128,1024]{2,1,0:T(8,128)(2,1)S(1)}, bf16[4,128,1024]{2,1,0:T(8,128)(2,1)S(1)}, u32[]{:S(2)}, u32[]{:S(2)}) collective-permute-start(bf16[4,128,1024]{2,1,0:T(8,128)(2,1)S(1)} %pad_maximum_fusion), channel_id=1, source_target_pairs={{0,1},{1,0},{2,3},{3,2},{4,5},{5,4},{6,7},{7,6},{8,9},{9,8},{10,11... | collective-permute-start | bytes 3145736 | tf_op jit(solution)/shard_map/ppermute | solution.py:479
  89.6 2.3 collective-permute-done.3.other
  91.8 1.5 shard_map.166
  93.3 0.0 copy-start.7
  93.3 5.6 %collective-permute-start.4 = (bf16[2,128,256]{2,1,0:T(8,128)(2,1)S(1)}, bf16[2,128,256]{2,1,0:T(8,128)(2,1)S(1)}, u32[]{:S(2)}, u32[]{:S(2)}) collective-permute-start(bf16[2,128,256]{2,1,0:T(8,128)(2,1)S(1)} %get-tuple-element.24), channel_id=1, source_target_pairs={{0,48},{16,0},{32,16},{48,32},{1,49},{17,1},{33,17},{49,33},{2,50}... | collective-permute-start | bytes 393224 | tf_op jit(solution)/shard_map/ppermute | solution.py:484
  99.0 3.2 %collective-permute-start.5 = (bf16[2,128,256]{2,1,0:T(8,128)(2,1)S(1)}, bf16[2,128,256]{2,1,0:T(8,128)(2,1)S(1)}, u32[]{:S(2)}, u32[]{:S(2)}) collective-permute-start(bf16[2,128,256]{2,1,0:T(8,128)(2,1)S(1)} %get-tuple-element.25), channel_id=1, source_target_pairs={{0,32},{16,48},{32,0},{48,16},{1,33},{17,49},{33,1},{49,17},{2,34}... | collective-permute-start | bytes 393224 | tf_op jit(solution)/shard_map/ppermute | solution.py:484
  102.2 1.9 collective-permute-start.6
  104.1 0.0 collective-permute-done.4.refs_1_
  104.1 0.0 copy-start.13
  104.2 2.6 collective-permute-done.5.refs_2_
  106.8 3.3 %collective-permute-done.6.refs_3_ = bf16[2,128,256]{2,1,0:T(8,128)(2,1)S(1)} collective-permute-done((bf16[2,128,256]{2,1,0:T(8,128)(2,1)S(1)}, bf16[2,128,256]{2,1,0:T(8,128)(2,1)S(1)}, u32[]{:S(2)}, u32[]{:S(2)}) %collective-permute-start.6) | collective-permute-done | bytes 131104 | tf_op jit(solution)/shard_map/ppermute | solution.py:484
  110.1 3.4 %collective-permute-start.7 = (bf16[4,128,256]{2,1,0:T(8,128)(2,1)S(1)}, bf16[4,128,256]{2,1,0:T(8,128)(2,1)}, u32[]{:S(2)}, u32[]{:S(2)}) collective-permute-start(bf16[4,128,256]{2,1,0:T(8,128)(2,1)S(1)} %pad_maximum_fusion.2), channel_id=1, source_target_pairs={{0,1},{1,0},{2,3},{3,2},{4,5},{5,4},{6,7},{7,6},{8,9},{9,8},{10,11... | collective-permute-start | bytes 786440 | tf_op jit(solution)/shard_map/ppermute | solution.py:479
  113.5 0.6 pad_add_fusion.place
  114.1 0.7 collective-permute-done.7.refs_4_
  114.8 4.6 %shard_map.167 = (bf16[128,2048]{1,0:T(8,128)(2,1)}, bf16[6144,128]{1,0:T(8,128)(2,1)}) custom-call(s32[256]{0:T(256)} %convert_add_fusion.dest, s32[2]{0:T(128)} %pad_add_fusion.place, bf16[2,128,256]{2,1,0:T(8,128)(2,1)} %copy-done.7, bf16[2,128,256]{2,1,0:T(8,128)(2,1)} %copy-done.13, bf16[2,128,256]{2,1,0:T(8,128)(2,1)} %copy-done.14, ...), custom_call_target="tpu_custom_call" | custom-call | tf_op jit(solution)/shard_map/pallas_call | solution.py:163
  119.4 1.2 copy-done.12
  120.6 11.1 %all-to-all-start.1 = ((bf16[64,96,128]{2,1,0:T(8,128)(2,1)}), bf16[64,96,128]{2,1,0:T(8,128)(2,1)S(1)}, u32[]{:S(2)}, u32[]{:S(2)}) async-start(bf16[64,96,128]{2,1,0:T(8,128)(2,1)} %bitcast.49), calls=%async_computation.1 | async-start | bytes 3145728 | tf_op jit(solution)/shard_map/all_to_all | solution.py:456
  131.7 0.0 all-gather.3.cloned.1.call-done
  131.7 5.0 %shard_map.168.act_grad = f32[384,512]{1,0:T(8,128)} custom-call(bf16[6144,128]{1,0:T(8,128)(2,1)} %bitcast.47, bf16[8,3,256,512]{3,2,1,0:T(8,128)(2,1)} %bitcast.43), custom_call_target="tpu_custom_call" | custom-call | tf_op jit(solution)/shard_map/pallas_call | solution.py:218
  136.7 34.7 %all-to-all-done.1 = bf16[64,96,128]{2,1,0:T(8,128)(2,1)S(1)} async-done(((bf16[64,96,128]{2,1,0:T(8,128)(2,1)}), bf16[64,96,128]{2,1,0:T(8,128)(2,1)S(1)}, u32[]{:S(2)}, u32[]{:S(2)}) %all-to-all-start.1) | async-done | bytes 1572896 | tf_op jit(solution)/shard_map/all_to_all | solution.py:456
  171.4 8.5 %shard_map.169 = (bf16[6144,128]{1,0:T(8,128)(2,1)}, bf16[384,512]{1,0:T(8,128)(2,1)}) custom-call(bf16[6144,128]{1,0:T(8,128)(2,1)S(1)} %bitcast.27, f32[384,512]{1,0:T(8,128)} %shard_map.168.act_grad, bf16[8,3,256,512]{3,2,1,0:T(8,128)(2,1)} %bitcast.44), custom_call_target="tpu_custom_call" | custom-call | tf_op jit(solution)/shard_map/pallas_call | solution.py:262
  180.0 6.1 %all-to-all-start.3 = ((bf16[64,96,128]{2,1,0:T(8,128)(2,1)}), bf16[64,96,128]{2,1,0:T(8,128)(2,1)S(1)}, u32[]{:S(2)}, u32[]{:S(2)}) async-start(bf16[64,96,128]{2,1,0:T(8,128)(2,1)} %bitcast.50), calls=%async_computation.3 | async-start | bytes 3145728 | tf_op jit(solution)/shard_map/all_to_all | solution.py:456
  186.1 5.3 %shard_map.170 = bf16[6144,128]{1,0:T(8,128)(2,1)} custom-call(bf16[384,512]{1,0:T(8,128)(2,1)} %get-tuple-element.30.act, bf16[8,3,256,512]{3,2,1,0:T(8,128)(2,1)} %bitcast.45), custom_call_target="tpu_custom_call" | custom-call | tf_op jit(solution)/shard_map/pallas_call | solution.py:291
  191.4 34.4 %all-to-all-done.3 = bf16[64,96,128]{2,1,0:T(8,128)(2,1)S(1)} async-done(((bf16[64,96,128]{2,1,0:T(8,128)(2,1)}), bf16[64,96,128]{2,1,0:T(8,128)(2,1)S(1)}, u32[]{:S(2)}, u32[]{:S(2)}) %all-to-all-start.3) | async-done | bytes 1572896 | tf_op jit(solution)/shard_map/all_to_all | solution.py:456
  225.9 6.4 %all-to-all-start.4 = ((bf16[64,96,128]{2,1,0:T(8,128)(2,1)}), bf16[64,96,128]{2,1,0:T(8,128)(2,1)}, u32[]{:S(2)}, u32[]{:S(2)}) async-start(bf16[64,96,128]{2,1,0:T(8,128)(2,1)} %bitcast.48), calls=%async_computation.4 | async-start | bytes 3145728 | tf_op jit(solution)/shard_map/all_to_all | solution.py:456
  232.3 3.3 %collective-permute-start.9 = (bf16[8,8,32,128]{3,2,1,0:T(8,128)(2,1)S(1)}, bf16[8,8,32,128]{3,2,1,0:T(8,128)(2,1)S(1)}, u32[]{:S(2)}, u32[]{:S(2)}) collective-permute-start(bf16[8,8,32,128]{3,2,1,0:T(8,128)(2,1)S(1)} %bitcast.29), channel_id=1, source_target_pairs={{0,16},{16,32},{32,48},{48,0},{1,17},{17,33},{33,49},{49,1},{2,18}... | collective-permute-start | bytes 1572872 | tf_op jit(solution)/shard_map/ppermute | solution.py:469
  235.5 4.5 %collective-permute-start.11 = (bf16[8,8,32,128]{3,2,1,0:T(8,128)(2,1)S(1)}, bf16[8,8,32,128]{3,2,1,0:T(8,128)(2,1)S(1)}, u32[]{:S(2)}, u32[]{:S(2)}) collective-permute-start(bf16[8,8,32,128]{3,2,1,0:T(8,128)(2,1)S(1)} %bitcast.30), channel_id=1, source_target_pairs={{0,32},{16,48},{32,0},{48,16},{1,33},{17,49},{33,1},{49,17},{2,34}... | collective-permute-start | bytes 1572872 | tf_op jit(solution)/shard_map/ppermute | solution.py:469
  240.1 3.0 collective-permute-start.13
  243.0 3.1 %collective-permute-start.8 = (bf16[8,8,32,128]{3,2,1,0:T(8,128)(2,1)S(1)}, bf16[8,8,32,128]{3,2,1,0:T(8,128)(2,1)S(1)}, u32[]{:S(2)}, u32[]{:S(2)}) collective-permute-start(bf16[8,8,32,128]{3,2,1,0:T(8,128)(2,1)S(1)} %bitcast.32), channel_id=1, source_target_pairs={{0,1},{1,0},{2,3},{3,2},{4,5},{5,4},{6,7},{7,6},{8,9},{9,8},{10,11... | collective-permute-start | bytes 1572872 | tf_op jit(solution)/shard_map/ppermute | solution.py:474
  246.2 11.7 %collective-permute-done.9.refs_2_ = bf16[8,8,32,128]{3,2,1,0:T(8,128)(2,1)S(1)} collective-permute-done((bf16[8,8,32,128]{3,2,1,0:T(8,128)(2,1)S(1)}, bf16[8,8,32,128]{3,2,1,0:T(8,128)(2,1)S(1)}, u32[]{:S(2)}, u32[]{:S(2)}) %collective-permute-start.9) | collective-permute-done | bytes 524320 | tf_op jit(solution)/shard_map/ppermute | solution.py:469
  257.9 3.6 %collective-permute-start.10 = (bf16[8,8,32,128]{3,2,1,0:T(8,128)(2,1)S(1)}, bf16[8,8,32,128]{3,2,1,0:T(8,128)(2,1)S(1)}, u32[]{:S(2)}, u32[]{:S(2)}) collective-permute-start(bf16[8,8,32,128]{3,2,1,0:T(8,128)(2,1)S(1)} %collective-permute-done.9.refs_2_), channel_id=1, source_target_pairs={{0,1},{1,0},{2,3},{3,2},{4,5},{5,4},{6,7},{7,6},{8,9},{9,8},{10,11... | collective-permute-start | bytes 1572872 | tf_op jit(solution)/shard_map/ppermute | solution.py:474
  261.5 14.5 %collective-permute-done.11.refs_4_ = bf16[8,8,32,128]{3,2,1,0:T(8,128)(2,1)S(1)} collective-permute-done((bf16[8,8,32,128]{3,2,1,0:T(8,128)(2,1)S(1)}, bf16[8,8,32,128]{3,2,1,0:T(8,128)(2,1)S(1)}, u32[]{:S(2)}, u32[]{:S(2)}) %collective-permute-start.11) | collective-permute-done | bytes 524320 | tf_op jit(solution)/shard_map/ppermute | solution.py:469
  276.0 2.9 collective-permute-start.12
  278.9 2.1 collective-permute-start.14
  281.1 1.6 collective-permute-done.14.refs_7_
  282.7 1.0 copy-done.1
  283.8 3.7 %shard_map.172 = (bf16[128,2048]{1,0:T(8,128)(2,1)}, bf16[128,1024]{1,0:T(8,128)(2,1)S(1)}) custom-call(s32[256]{0:T(256)S(1)} %copy-done.9, s32[2]{0:T(128)S(1)} %copy-done.11, bf16[6144,128]{1,0:T(8,128)(2,1)S(1)} %bitcast.26, bf16[128,2048]{1,0:T(8,128)(2,1)S(1)} %copy-done.1, f32[1,2048]{1,0:T(1,128)S(1)} %bitcast.39, bf16[128,2048]{1,0:T(8,128)(2,1)S(1)} %copy-done, ...), custom_call_target="tpu_custom_call" | custom-call | tf_op jit(solution)/shard_map/pallas_call | solution.py:350
  287.4 4.5 %shard_map.173 = (bf16[128,1024]{1,0:T(8,128)(2,1)}, bf16[128,1024]{1,0:T(8,128)(2,1)}, bf16[128,1024]{1,0:T(8,128)(2,1)}) custom-call(s32[1,128]{1,0:T(1,128)S(1)} %bitcast.42, s32[128,1]{1,0:T(8,128)S(1)} %copy.26.seg_col, bf16[128,1024]{1,0:T(8,128)(2,1)S(1)} %copy-done.2, bf16[128,1024]{1,0:T(8,128)(2,1)S(1)} %copy-done.4, ...), custom_call_target="tpu_custom_call" | custom-call | tf_op jit(solution)/shard_map/pallas_call | solution.py:450
  291.9 3.4 %shard_map.171 = bf16[128,2048]{1,0:T(8,128)(2,1)} custom-call(s32[256]{0:T(256)} %convert_add_fusion.dest, f32[256]{0:T(256)} %div.10.gate, bf16[6144,128]{1,0:T(8,128)(2,1)} %bitcast.22.source, bf16[128,2048]{1,0:T(8,128)(2,1)} %get-tuple-element.32.resid), custom_call_target="tpu_custom_call" | custom-call | tf_op jit(solution)/shard_map/pallas_call | solution.py:383
  (46 shorter events, 0.2 us)
Async XLA Ops:
  7.2 124.5 %all-gather.3.cloned.1.call-start = ((), (), s32[]{:S(2)}) async-start(), calls=%async_computation.5 | async-start | bytes 7077888 | tf_op jit(solution)/shard_map/all_gather | solution.py:503
  8.2 2.1 copy-start.16
  10.3 18.0 %copy-start.17 = (s32[128,2]{0,1:T(2,128)S(1)}, s32[128,2]{0,1:T(2,128)}, u32[]{:S(2)}) copy-start(s32[128,2]{0,1:T(2,128)} %param.23) | copy-start | bytes 3076
  10.3 18.3 %copy-start.18 = (s32[128,2]{0,1:T(2,128)S(1)}, s32[128,2]{0,1:T(2,128)}, u32[]{:S(2)}) copy-start(s32[128,2]{0,1:T(2,128)} %param.24) | copy-start | bytes 3076
  11.2 34.6 %all-to-all-start = ((bf16[64,32,128]{2,1,0:T(8,128)(2,1)}), bf16[64,32,128]{2,1,0:T(8,128)(2,1)S(1)}, u32[]{:S(2)}, u32[]{:S(2)}) async-start(bf16[64,32,128]{2,1,0:T(8,128)(2,1)} %broadcast_in_dim.8), calls=%async_computation | async-start | bytes 1048576 | tf_op jit(solution)/shard_map/all_to_all | solution.py:456
  45.7 10.8 %copy-start.10 = (s32[128]{0:T(128)S(1)}, s32[128]{0:T(128)}, u32[]{:S(2)}) copy-start(s32[128]{0:T(128)} %param.17) | copy-start | bytes 1540
  45.7 10.9 %copy-start.2 = (bf16[128,1024]{1,0:T(8,128)(2,1)S(1)}, bf16[128,1024]{1,0:T(8,128)(2,1)}, u32[]{:S(2)}) copy-start(bf16[128,1024]{1,0:T(8,128)(2,1)} %queries.3) | copy-start | bytes 786436
  45.7 10.9 %copy-start.3 = (bf16[128,1024]{1,0:T(8,128)(2,1)S(1)}, bf16[128,1024]{1,0:T(8,128)(2,1)}, u32[]{:S(2)}) copy-start(bf16[128,1024]{1,0:T(8,128)(2,1)} %keys.3) | copy-start | bytes 786436
  45.7 10.9 %copy-start.5 = (bf16[128,1024]{1,0:T(8,128)(2,1)S(1)}, bf16[128,1024]{1,0:T(8,128)(2,1)}, u32[]{:S(2)}) copy-start(bf16[128,1024]{1,0:T(8,128)(2,1)} %values.3) | copy-start | bytes 786436
  45.7 73.6 %all-to-all-start.2 = ((bf16[64,96,128]{2,1,0:T(8,128)(2,1)}), bf16[64,96,128]{2,1,0:T(8,128)(2,1)S(1)}, u32[]{:S(2)}, u32[]{:S(2)}) async-start(bf16[64,96,128]{2,1,0:T(8,128)(2,1)} %bitcast.46), calls=%async_computation.2 | async-start | bytes 3145728 | tf_op jit(solution)/shard_map/all_to_all | solution.py:456
  59.4 16.0 %collective-permute-start = (bf16[128,1024]{1,0:T(8,128)(2,1)S(1)}, bf16[128,1024]{1,0:T(8,128)(2,1)S(1)}, u32[]{:S(2)}, u32[]{:S(2)}) collective-permute-start(bf16[128,1024]{1,0:T(8,128)(2,1)S(1)} %shard_map.165.refs_0_), channel_id=1, source_target_pairs={{0,16},{16,32},{32,48},{48,0},{1,17},{17,33},{33,49},{49,1},{2,18}... | collective-permute-start | bytes 786440 | tf_op jit(solution)/shard_map/ppermute | solution.py:484
  62.6 22.7 %collective-permute-start.1 = (bf16[128,1024]{1,0:T(8,128)(2,1)S(1)}, bf16[128,1024]{1,0:T(8,128)(2,1)S(1)}, u32[]{:S(2)}, u32[]{:S(2)}) collective-permute-start(bf16[128,1024]{1,0:T(8,128)(2,1)S(1)} %shard_map.165.refs_0_), channel_id=1, source_target_pairs={{0,32},{16,48},{32,0},{48,16},{1,33},{17,49},{33,1},{49,17},{2,34}... | collective-permute-start | bytes 786440 | tf_op jit(solution)/shard_map/ppermute | solution.py:484
  67.1 19.2 %collective-permute-start.2 = (bf16[128,1024]{1,0:T(8,128)(2,1)S(1)}, bf16[128,1024]{1,0:T(8,128)(2,1)S(1)}, u32[]{:S(2)}, u32[]{:S(2)}) collective-permute-start(bf16[128,1024]{1,0:T(8,128)(2,1)S(1)} %shard_map.165.refs_0_), channel_id=1, source_target_pairs={{0,48},{16,0},{32,16},{48,32},{1,49},{17,1},{33,17},{49,33},{2,50}... | collective-permute-start | bytes 786440 | tf_op jit(solution)/shard_map/ppermute | solution.py:484
  86.5 5.4 %collective-permute-start.3 = (bf16[4,128,1024]{2,1,0:T(8,128)(2,1)S(1)}, bf16[4,128,1024]{2,1,0:T(8,128)(2,1)S(1)}, u32[]{:S(2)}, u32[]{:S(2)}) collective-permute-start(bf16[4,128,1024]{2,1,0:T(8,128)(2,1)S(1)} %pad_maximum_fusion), channel_id=1, source_target_pairs={{0,1},{1,0},{2,3},{3,2},{4,5},{5,4},{6,7},{7,6},{8,9},{9,8},{10,11... | collective-permute-start | bytes 3145736 | tf_op jit(solution)/shard_map/ppermute | solution.py:479
  93.3 21.4 %copy-start.7 = (bf16[2,128,256]{2,1,0:T(8,128)(2,1)}, bf16[2,128,256]{2,1,0:T(8,128)(2,1)S(1)}, u32[]{:S(2)}) copy-start(bf16[2,128,256]{2,1,0:T(8,128)(2,1)S(1)} %get-tuple-element.23.refs_0_) | copy-start | bytes 393220
  93.3 10.8 %collective-permute-start.4 = (bf16[2,128,256]{2,1,0:T(8,128)(2,1)S(1)}, bf16[2,128,256]{2,1,0:T(8,128)(2,1)S(1)}, u32[]{:S(2)}, u32[]{:S(2)}) collective-permute-start(bf16[2,128,256]{2,1,0:T(8,128)(2,1)S(1)} %get-tuple-element.24), channel_id=1, source_target_pairs={{0,48},{16,0},{32,16},{48,32},{1,49},{17,1},{33,17},{49,33},{2,50}... | collective-permute-start | bytes 393224 | tf_op jit(solution)/shard_map/ppermute | solution.py:484
  99.0 7.8 %collective-permute-start.5 = (bf16[2,128,256]{2,1,0:T(8,128)(2,1)S(1)}, bf16[2,128,256]{2,1,0:T(8,128)(2,1)S(1)}, u32[]{:S(2)}, u32[]{:S(2)}) collective-permute-start(bf16[2,128,256]{2,1,0:T(8,128)(2,1)S(1)} %get-tuple-element.25), channel_id=1, source_target_pairs={{0,32},{16,48},{32,0},{48,16},{1,33},{17,49},{33,1},{49,17},{2,34}... | collective-permute-start | bytes 393224 | tf_op jit(solution)/shard_map/ppermute | solution.py:484
  102.2 7.9 %collective-permute-start.6 = (bf16[2,128,256]{2,1,0:T(8,128)(2,1)S(1)}, bf16[2,128,256]{2,1,0:T(8,128)(2,1)S(1)}, u32[]{:S(2)}, u32[]{:S(2)}) collective-permute-start(bf16[2,128,256]{2,1,0:T(8,128)(2,1)S(1)} %get-tuple-element.26), channel_id=1, source_target_pairs={{0,16},{16,32},{32,48},{48,0},{1,17},{17,33},{33,49},{49,1},{2,18}... | collective-permute-start | bytes 393224 | tf_op jit(solution)/shard_map/ppermute | solution.py:484
  104.1 10.6 %copy-start.13 = (bf16[2,128,256]{2,1,0:T(8,128)(2,1)}, bf16[2,128,256]{2,1,0:T(8,128)(2,1)S(1)}, u32[]{:S(2)}) copy-start(bf16[2,128,256]{2,1,0:T(8,128)(2,1)S(1)} %collective-permute-done.4.refs_1_) | copy-start | bytes 393220
  106.8 8.0 %copy-start.14 = (bf16[2,128,256]{2,1,0:T(8,128)(2,1)}, bf16[2,128,256]{2,1,0:T(8,128)(2,1)S(1)}, u32[]{:S(2)}) copy-start(bf16[2,128,256]{2,1,0:T(8,128)(2,1)S(1)} %collective-permute-done.5.refs_2_) | copy-start | bytes 393220
  110.0 4.7 %copy-start.15 = (bf16[2,128,256]{2,1,0:T(8,128)(2,1)}, bf16[2,128,256]{2,1,0:T(8,128)(2,1)S(1)}, u32[]{:S(2)}) copy-start(bf16[2,128,256]{2,1,0:T(8,128)(2,1)S(1)} %collective-permute-done.6.refs_3_) | copy-start | bytes 393220
  110.1 4.7 %collective-permute-start.7 = (bf16[4,128,256]{2,1,0:T(8,128)(2,1)S(1)}, bf16[4,128,256]{2,1,0:T(8,128)(2,1)}, u32[]{:S(2)}, u32[]{:S(2)}) collective-permute-start(bf16[4,128,256]{2,1,0:T(8,128)(2,1)S(1)} %pad_maximum_fusion.2), channel_id=1, source_target_pairs={{0,1},{1,0},{2,3},{3,2},{4,5},{5,4},{6,7},{7,6},{8,9},{9,8},{10,11... | collective-permute-start | bytes 786440 | tf_op jit(solution)/shard_map/ppermute | solution.py:479
  119.3 1.2 copy-start.12
  120.6 50.9 %all-to-all-start.1 = ((bf16[64,96,128]{2,1,0:T(8,128)(2,1)}), bf16[64,96,128]{2,1,0:T(8,128)(2,1)S(1)}, u32[]{:S(2)}, u32[]{:S(2)}) async-start(bf16[64,96,128]{2,1,0:T(8,128)(2,1)} %bitcast.49), calls=%async_computation.1 | async-start | bytes 3145728 | tf_op jit(solution)/shard_map/all_to_all | solution.py:456
  180.0 45.9 %all-to-all-start.3 = ((bf16[64,96,128]{2,1,0:T(8,128)(2,1)}), bf16[64,96,128]{2,1,0:T(8,128)(2,1)S(1)}, u32[]{:S(2)}, u32[]{:S(2)}) async-start(bf16[64,96,128]{2,1,0:T(8,128)(2,1)} %bitcast.50), calls=%async_computation.3 | async-start | bytes 3145728 | tf_op jit(solution)/shard_map/all_to_all | solution.py:456
  225.8 56.9 %copy-start = (bf16[128,2048]{1,0:T(8,128)(2,1)S(1)}, bf16[128,2048]{1,0:T(8,128)(2,1)}, u32[]{:S(2)}) copy-start(bf16[128,2048]{1,0:T(8,128)(2,1)} %grad.3) | copy-start | bytes 1572868
  225.8 56.9 %copy-start.8 = (f32[2048]{0:T(1024)S(1)}, f32[2048]{0:T(1024)}, u32[]{:S(2)}) copy-start(f32[2048]{0:T(1024)} %param.19) | copy-start | bytes 24580
  225.8 56.9 %copy-start.9 = (s32[256]{0:T(256)S(1)}, s32[256]{0:T(256)}, u32[]{:S(2)}) copy-start(s32[256]{0:T(256)} %convert_add_fusion.dest) | copy-start | bytes 3076
  225.8 56.9 %copy-start.11 = (s32[2]{0:T(128)S(1)}, s32[2]{0:T(128)}, u32[]{:S(2)}) copy-start(s32[2]{0:T(128)} %pad_add_fusion.place) | copy-start | bytes 28
  225.9 66.1 %all-to-all-start.4 = ((bf16[64,96,128]{2,1,0:T(8,128)(2,1)}), bf16[64,96,128]{2,1,0:T(8,128)(2,1)}, u32[]{:S(2)}, u32[]{:S(2)}) async-start(bf16[64,96,128]{2,1,0:T(8,128)(2,1)} %bitcast.48), calls=%async_computation.4 | async-start | bytes 3145728 | tf_op jit(solution)/shard_map/all_to_all | solution.py:456
  232.3 25.6 %collective-permute-start.9 = (bf16[8,8,32,128]{3,2,1,0:T(8,128)(2,1)S(1)}, bf16[8,8,32,128]{3,2,1,0:T(8,128)(2,1)S(1)}, u32[]{:S(2)}, u32[]{:S(2)}) collective-permute-start(bf16[8,8,32,128]{3,2,1,0:T(8,128)(2,1)S(1)} %bitcast.29), channel_id=1, source_target_pairs={{0,16},{16,32},{32,48},{48,0},{1,17},{17,33},{33,49},{49,1},{2,18}... | collective-permute-start | bytes 1572872 | tf_op jit(solution)/shard_map/ppermute | solution.py:469
  235.5 40.5 %collective-permute-start.11 = (bf16[8,8,32,128]{3,2,1,0:T(8,128)(2,1)S(1)}, bf16[8,8,32,128]{3,2,1,0:T(8,128)(2,1)S(1)}, u32[]{:S(2)}, u32[]{:S(2)}) collective-permute-start(bf16[8,8,32,128]{3,2,1,0:T(8,128)(2,1)S(1)} %bitcast.30), channel_id=1, source_target_pairs={{0,32},{16,48},{32,0},{48,16},{1,33},{17,49},{33,1},{49,17},{2,34}... | collective-permute-start | bytes 1572872 | tf_op jit(solution)/shard_map/ppermute | solution.py:469
  240.1 38.8 %collective-permute-start.13 = (bf16[8,8,32,128]{3,2,1,0:T(8,128)(2,1)S(1)}, bf16[8,8,32,128]{3,2,1,0:T(8,128)(2,1)S(1)}, u32[]{:S(2)}, u32[]{:S(2)}) collective-permute-start(bf16[8,8,32,128]{3,2,1,0:T(8,128)(2,1)S(1)} %bitcast.31), channel_id=1, source_target_pairs={{0,48},{16,0},{32,16},{48,32},{1,49},{17,1},{33,17},{49,33},{2,50}... | collective-permute-start | bytes 1572872 | tf_op jit(solution)/shard_map/ppermute | solution.py:469
  243.0 38.0 %collective-permute-start.8 = (bf16[8,8,32,128]{3,2,1,0:T(8,128)(2,1)S(1)}, bf16[8,8,32,128]{3,2,1,0:T(8,128)(2,1)S(1)}, u32[]{:S(2)}, u32[]{:S(2)}) collective-permute-start(bf16[8,8,32,128]{3,2,1,0:T(8,128)(2,1)S(1)} %bitcast.32), channel_id=1, source_target_pairs={{0,1},{1,0},{2,3},{3,2},{4,5},{5,4},{6,7},{7,6},{8,9},{9,8},{10,11... | collective-permute-start | bytes 1572872 | tf_op jit(solution)/shard_map/ppermute | solution.py:474
  257.9 23.2 %collective-permute-start.10 = (bf16[8,8,32,128]{3,2,1,0:T(8,128)(2,1)S(1)}, bf16[8,8,32,128]{3,2,1,0:T(8,128)(2,1)S(1)}, u32[]{:S(2)}, u32[]{:S(2)}) collective-permute-start(bf16[8,8,32,128]{3,2,1,0:T(8,128)(2,1)S(1)} %collective-permute-done.9.refs_2_), channel_id=1, source_target_pairs={{0,1},{1,0},{2,3},{3,2},{4,5},{5,4},{6,7},{7,6},{8,9},{9,8},{10,11... | collective-permute-start | bytes 1572872 | tf_op jit(solution)/shard_map/ppermute | solution.py:474
  276.0 5.1 %collective-permute-start.12 = (bf16[8,8,32,128]{3,2,1,0:T(8,128)(2,1)S(1)}, bf16[8,8,32,128]{3,2,1,0:T(8,128)(2,1)S(1)}, u32[]{:S(2)}, u32[]{:S(2)}) collective-permute-start(bf16[8,8,32,128]{3,2,1,0:T(8,128)(2,1)S(1)} %collective-permute-done.11.refs_4_), channel_id=1, source_target_pairs={{0,1},{1,0},{2,3},{3,2},{4,5},{5,4},{6,7},{7,6},{8,9},{9,8},{10,11... | collective-permute-start | bytes 1572872 | tf_op jit(solution)/shard_map/ppermute | solution.py:474
  278.9 3.8 %collective-permute-start.14 = (bf16[8,8,32,128]{3,2,1,0:T(8,128)(2,1)S(1)}, bf16[8,8,32,128]{3,2,1,0:T(8,128)(2,1)S(1)}, u32[]{:S(2)}, u32[]{:S(2)}) collective-permute-start(bf16[8,8,32,128]{3,2,1,0:T(8,128)(2,1)S(1)} %collective-permute-done.13.refs_6_), channel_id=1, source_target_pairs={{0,1},{1,0},{2,3},{3,2},{4,5},{5,4},{6,7},{7,6},{8,9},{9,8},{10,11... | collective-permute-start | bytes 1572872 | tf_op jit(solution)/shard_map/ppermute | solution.py:474
  282.7 1.0 copy-start.1
  283.8 3.7 %copy-start.4 = (bf16[128,1024]{1,0:T(8,128)(2,1)S(1)}, bf16[128,1024]{1,0:T(8,128)(2,1)}, u32[]{:S(2)}) copy-start(bf16[128,1024]{1,0:T(8,128)(2,1)} %keys.3) | copy-start | bytes 786436
  283.8 3.7 %copy-start.6 = (bf16[128,1024]{1,0:T(8,128)(2,1)S(1)}, bf16[128,1024]{1,0:T(8,128)(2,1)}, u32[]{:S(2)}) copy-start(bf16[128,1024]{1,0:T(8,128)(2,1)} %values.3) | copy-start | bytes 786436
Sparse Core Ops, SparseCore 0:
  10.4 93.2 all-gather.2
